TPU v7x, 768 devices: a whole 4x8x12 slice. The times are simulated.
768 devices in a mesh: pole: 1, prow: 16 (over y, core), pcol: 48 (over z, x).
Axes of the slice: x: 4, y: 8, z: 12, core: 2. Of those that a mesh axis runs over, the one named last changes fastest.
Arguments:
- hamiltonian: bfloat16 [12288, 12288], P(('prow', 'pcol')), may hold values from -2 to 32, as said below
- margin: bfloat16 [12288, 12288], P(('prow', 'pcol')), may hold values from -1 to 1, as said below
- pole_shift: float32 [2], P('pole'), may hold values from 0.3 to 1.5
- row_map: int32 [12288], P('prow'), may hold values from 0 to 12287, as said below
- parent: int32 [96], replicated, may hold values from 1 to 96, as said below
Outputs:
- factored: float32 [2, 12288, 12288], P('pole', 'prow', 'pcol')
Inputs may be any that keep to these rules, and one draw needn't show every extreme that they name: For each aligned block of 768 rows, row_map maps the block's rows one to one onto the same block's indices. parent[s] is greater than s; the value 96 marks a root. Supernode 0's parent is 1 and the last supernode is a root. `hamiltonian`: as a matrix over orbitals it is symmetric. `margin`: as a matrix over orbitals it is symmetric, with ones on its diagonal.
All inputs are finite; a program needn't handle non-finite values.
Results may differ from a plain program's by a relative error of at most 0.0023.
Values may be sent and summed in bfloat16 or wider, within the bound.
No kernel may reach another device: no remote copies, remote signals or barrier semaphores. Data moves between devices by JAX's collectives and lax.ppermute only.
A program may use at most 32 MiB of HBM per device.

v0:
```python
import jax
import jax.numpy as jnp
from jax import lax
from jax.sharding import PartitionSpec as P

SN = 128
STEPS = 3
NSI = 4


def broadcast(array, axis, root):
    mine = lax.axis_index(axis) == root
    return lax.psum(jnp.where(mine, array, jnp.zeros_like(array)), axis)


def complex_product(left_pair, right_pair):
    highest = lax.Precision.HIGHEST
    real_part = jnp.dot(
        left_pair[0], right_pair[0], precision=highest, preferred_element_type=jnp.float32
    ) - jnp.dot(left_pair[1], right_pair[1], precision=highest, preferred_element_type=jnp.float32)
    imag_part = jnp.dot(
        left_pair[0], right_pair[1], precision=highest, preferred_element_type=jnp.float32
    ) + jnp.dot(left_pair[1], right_pair[0], precision=highest, preferred_element_type=jnp.float32)
    return jnp.stack([real_part, imag_part])


def structure(parent, node_count):
    node_index = jnp.arange(node_count, dtype=jnp.int32)
    reached = (parent[:, None] == node_index[None, :]).astype(jnp.int32)
    for level_index in range(node_count.bit_length()):
        reached = jnp.minimum(reached + jnp.dot(reached, reached), 1)
    diagonal_ones = (node_index[:, None] == node_index[None, :]).astype(jnp.int32)
    return jnp.minimum(diagonal_ones + reached + reached.T, 1)


def invert_pivot(pivot, sweeps):
    pivot_size = pivot.shape[-1]
    places = jnp.arange(pivot_size, dtype=jnp.int32)
    identity_real = (places[:, None] == places[None, :]).astype(jnp.float32)
    diag_real = jnp.diagonal(pivot[0])
    diag_imag = jnp.diagonal(pivot[1])
    modulus = diag_real * diag_real + diag_imag * diag_imag
    approx = jnp.stack(
        [
            identity_real * (diag_real / modulus)[None, :],
            identity_real * (-diag_imag / modulus)[None, :],
        ]
    )
    for sweep_index in range(sweeps):
        product = complex_product(pivot, approx)
        residue = jnp.stack([2.0 * identity_real - product[0], -product[1]])
        approx = complex_product(approx, residue)
    return approx


def body(hamiltonian, margin, pole_shift, row_map, parent):
    grid_rows = lax.axis_size("prow")
    grid_cols = lax.axis_size("pcol")
    my_row = lax.axis_index("prow")
    my_col = lax.axis_index("pcol")
    ham_block, over_block = (
        lax.all_to_all(hamiltonian, "pcol", split_axis=1, concat_axis=0, tiled=True),
        lax.all_to_all(margin, "pcol", split_axis=1, concat_axis=0, tiled=True),
    )
    block_height = ham_block.shape[0]
    block_width = ham_block.shape[1]
    local_rows = row_map - my_row * block_height
    ham_block = jnp.take(ham_block, local_rows, axis=0).astype(jnp.float32)
    over_block = jnp.take(over_block, local_rows, axis=0).astype(jnp.float32)
    matrix = jnp.stack([ham_block - pole_shift[0] * over_block, -pole_shift[1] * over_block])
    node_count = parent.shape[0]
    pattern = structure(parent, node_count)
    row_nodes = jnp.arange(block_height // SN, dtype=jnp.int32) * grid_rows + my_row
    col_nodes = jnp.arange(block_width // SN, dtype=jnp.int32) * grid_cols + my_col
    all_nodes = jnp.arange(node_count, dtype=jnp.int32)
    pick_rows = (row_nodes[:, None] == all_nodes[None, :]).astype(jnp.int32)
    pick_cols = (col_nodes[:, None] == all_nodes[None, :]).astype(jnp.int32)
    local_pattern = jnp.dot(jnp.dot(pick_rows, pattern), pick_cols.T)
    row_owner = jnp.repeat(row_nodes, SN)
    col_owner = jnp.repeat(col_nodes, SN)
    keep_mask = jnp.repeat(jnp.repeat(local_pattern, SN, axis=0), SN, axis=1).astype(jnp.float32)
    matrix = matrix * keep_mask[None]
    places = jnp.arange(SN, dtype=jnp.int32)
    identity_real = (places[:, None] == places[None, :]).astype(jnp.float32)
    identity_pair = jnp.stack([identity_real, jnp.zeros_like(identity_real)])
    for elimination in range(STEPS):
        owner_row = elimination % grid_rows
        owner_col = elimination % grid_cols
        row_slot = elimination // grid_rows * SN
        col_slot = elimination // grid_cols * SN
        is_owner = (my_row == owner_row) & (my_col == owner_col)
        pivot_here = jnp.where(
            is_owner, matrix[:, row_slot : row_slot + SN, col_slot : col_slot + SN], identity_pair
        )
        below_rows = row_owner > elimination
        below_mask = below_rows.astype(jnp.float32)[None, :, None]
        column_here = matrix[:, :, col_slot : col_slot + SN]
        inverse = broadcast(
            invert_pivot(pivot_here, NSI).astype(jnp.bfloat16), "prow", owner_row
        ).astype(jnp.float32)
        factor = broadcast(
            (complex_product(column_here, inverse) * below_mask).astype(jnp.bfloat16),
            "pcol",
            owner_col,
        ).astype(jnp.float32)
        beyond = (col_owner > elimination).astype(jnp.float32)[None, None, :]
        row_panel = broadcast(
            matrix[:, row_slot : row_slot + SN, :].astype(jnp.bfloat16), "prow", owner_row
        ).astype(jnp.float32)
        matrix = matrix - complex_product(factor, row_panel * beyond)
        current = matrix[:, :, col_slot : col_slot + SN]
        written = jnp.where(below_rows[None, :, None] & (my_col == owner_col), factor, current)
        matrix = matrix.at[:, :, col_slot : col_slot + SN].set(written)
    return matrix


def solution(mesh):
    return jax.shard_map(
        body,
        mesh=mesh,
        in_specs=(P(("prow", "pcol"), None), P(("prow", "pcol"), None), P("pole"), P("prow"), P()),
        out_specs=P("pole", "prow", "pcol"),
        check_vma=False,
    )
```

profile of v0, /device:TPU:8, one launch (start us, length us, event | category | flops | bytes accessed | tf_op | source)
XLA Modules:
  0.0 1132.7 jit_solution(9893067009445533964)
XLA Ops:
  6.5 1.8 copy.34
  8.3 18.4 %all-to-all-start = ((bf16[16,48,256]{2,0,1:T(8,128)(2,1)}), bf16[16,48,256]{2,0,1:T(8,128)(2,1)S(1)}, u32[]{:S(2)}, u32[]{:S(2)}) async-start(bf16[16,48,256]{2,0,1:T(8,128)(2,1)} %bitcast.418), calls=%async_computation | async-start | bytes 786432 | tf_op jit(solution)/shard_map/all_to_all | solution.py:62
  31.6 16.8 %all-to-all-done = bf16[16,48,256]{2,0,1:T(8,128)(2,1)S(1)} async-done(((bf16[16,48,256]{2,0,1:T(8,128)(2,1)}), bf16[16,48,256]{2,0,1:T(8,128)(2,1)S(1)}, u32[]{:S(2)}, u32[]{:S(2)}) %all-to-all-start) | async-done | bytes 393248 | tf_op jit(solution)/shard_map/all_to_all | solution.py:62
  48.5 5.3 all-to-all-start.1
  55.9 2.6 gather_fusion.6
  58.6 15.9 %all-to-all-done.1 = bf16[16,48,256]{2,0,1:T(8,128)(2,1)S(1)} async-done(((bf16[16,48,256]{2,0,1:T(8,128)(2,1)}), bf16[16,48,256]{2,0,1:T(8,128)(2,1)S(1)}, u32[]{:S(2)}, u32[]{:S(2)}) %all-to-all-start.1) | async-done | bytes 393248 | tf_op jit(solution)/shard_map/all_to_all | solution.py:63
  74.5 2.6 gather_fusion.7
  79.5 1.2 gather_fusion
  80.8 1.2 gather_fusion.1
  89.8 109.0 %all-reduce.21.cloned.1.call-done = (bf16[2,128,128]{2,1,0:T(8,128)(2,1)}, bf16[2,128,256]{2,1,0:T(8,128)(2,1)}) async-done(((bf16[2,128,128]{2,1,0:T(8,128)(2,1)}, bf16[2,128,256]{2,1,0:T(8,128)(2,1)}), (bf16[2,128,128]{2,1,0:T(8,128)(2,1)}, bf16[2,128,256]{2,1,0:T(8,128)(2,1)})) %all-reduce.21.cloned.1.call-update) | async-done | bytes 196624 | tf_op jit(solution)/shard_map/psum | solution.py:13
  202.8 217.8 %all-reduce.11.cloned.1.call-done = bf16[2,768,128]{2,1,0:T(8,128)(2,1)} async-done(((bf16[2,768,128]{2,1,0:T(8,128)(2,1)}), bf16[2,768,128]{2,1,0:T(8,128)(2,1)}) %all-reduce.11.cloned.1.call-update) | async-done | bytes 393232 | tf_op jit(solution)/shard_map/psum | solution.py:13
  420.6 1.5 fusion.71
  422.0 1.4 fusion.70
  435.9 111.9 %all-reduce.19.cloned.1.call-done = (bf16[2,128,128]{2,1,0:T(8,128)(2,1)}, bf16[2,128,256]{2,1,0:T(8,128)(2,1)}) async-done(((bf16[2,128,128]{2,1,0:T(8,128)(2,1)}, bf16[2,128,256]{2,1,0:T(8,128)(2,1)}), (bf16[2,128,128]{2,1,0:T(8,128)(2,1)}, bf16[2,128,256]{2,1,0:T(8,128)(2,1)})) %all-reduce.19.cloned.1.call-update) | async-done | bytes 196624 | tf_op jit(solution)/shard_map/psum | solution.py:13
  552.0 217.6 %all-reduce.13.cloned.1.call-done = bf16[2,768,128]{2,1,0:T(8,128)(2,1)} async-done(((bf16[2,768,128]{2,1,0:T(8,128)(2,1)}), bf16[2,768,128]{2,1,0:T(8,128)(2,1)}) %all-reduce.13.cloned.1.call-update) | async-done | bytes 393232 | tf_op jit(solution)/shard_map/psum | solution.py:13
  769.7 1.5 fusion.73
  771.1 1.4 fusion.72
  774.0 1.2 gather_fusion.4
  784.8 111.9 %all-reduce.17.cloned.1.call-done = (bf16[2,128,128]{2,1,0:T(8,128)(2,1)}, bf16[2,128,256]{2,1,0:T(8,128)(2,1)}) async-done(((bf16[2,128,128]{2,1,0:T(8,128)(2,1)}, bf16[2,128,256]{2,1,0:T(8,128)(2,1)}), (bf16[2,128,128]{2,1,0:T(8,128)(2,1)}, bf16[2,128,256]{2,1,0:T(8,128)(2,1)})) %all-reduce.17.cloned.1.call-update) | async-done | bytes 196624 | tf_op jit(solution)/shard_map/psum | solution.py:13
  900.6 217.8 %all-reduce.15.cloned.1.call-done = bf16[2,768,128]{2,1,0:T(8,128)(2,1)} async-done(((bf16[2,768,128]{2,1,0:T(8,128)(2,1)}), bf16[2,768,128]{2,1,0:T(8,128)(2,1)}) %all-reduce.15.cloned.1.call-update) | async-done | bytes 393232 | tf_op jit(solution)/shard_map/psum | solution.py:13
  1118.5 1.5 fusion.75
  1119.9 1.4 fusion.74
  1122.3 1.3 maximum_subtract_fusion.2
  1123.7 2.2 fusion.57
  (233 shorter events, 51.6 us)
Async XLA Ops:
  6.5 20.3 %copy-start.12 = (s32[96]{0:T(128)S(1)}, s32[96]{0:T(128)}, u32[]{:S(2)}) copy-start(s32[96]{0:T(128)} %param.17) | copy-start | bytes 1156
  8.3 21.4 %copy-start.5 = (bf16[16,12288]{1,0:T(8,128)(2,1)S(1)}, bf16[16,12288]{1,0:T(8,128)(2,1)}, u32[]{:S(2)}) copy-start(bf16[16,12288]{1,0:T(8,128)(2,1)} %param.14) | copy-start | bytes 1179652
  8.3 40.1 %all-to-all-start = ((bf16[16,48,256]{2,0,1:T(8,128)(2,1)}), bf16[16,48,256]{2,0,1:T(8,128)(2,1)S(1)}, u32[]{:S(2)}, u32[]{:S(2)}) async-start(bf16[16,48,256]{2,0,1:T(8,128)(2,1)} %bitcast.418), calls=%async_computation | async-start | bytes 786432 | tf_op jit(solution)/shard_map/all_to_all | solution.py:62
  26.7 3.8 copy-start.13
  26.8 3.8 copy-start.14
  48.5 26.0 %all-to-all-start.1 = ((bf16[16,48,256]{2,0,1:T(8,128)(2,1)}), bf16[16,48,256]{2,0,1:T(8,128)(2,1)S(1)}, u32[]{:S(2)}, u32[]{:S(2)}) async-start(bf16[16,48,256]{2,0,1:T(8,128)(2,1)} %bitcast.417), calls=%async_computation.1 | async-start | bytes 786432 | tf_op jit(solution)/shard_map/all_to_all | solution.py:63
  53.7 145.0 %all-reduce.21.cloned.1.call-start = ((), (), s32[]{:S(2)}) async-start(), calls=%async_computation.7 | async-start | bytes 393216 | tf_op jit(solution)/shard_map/psum | solution.py:13
  77.9 0.9 copy-start
  89.5 331.1 %all-reduce.11.cloned.1.call-start = ((), (), s32[]{:S(2)}) async-start(), calls=%async_computation.2 | async-start | bytes 786432 | tf_op jit(solution)/shard_map/psum | solution.py:13
  198.8 2.2 copy-start.8
  201.3 1.4 copy-start.10
  202.6 345.2 %all-reduce.19.cloned.1.call-start = ((), (), s32[]{:S(2)}) async-start(), calls=%async_computation.6 | async-start | bytes 393216 | tf_op jit(solution)/shard_map/psum | solution.py:13
  420.6 2.9 copy-start.2
  423.4 1.1 copy-start.1
  435.8 333.8 %all-reduce.13.cloned.1.call-start = ((), (), s32[]{:S(2)}) async-start(), calls=%async_computation.3 | async-start | bytes 786432 | tf_op jit(solution)/shard_map/psum | solution.py:13
  547.8 2.2 copy-start.6
  550.4 1.6 copy-start.9
  551.7 345.0 %all-reduce.17.cloned.1.call-start = ((), (), s32[]{:S(2)}) async-start(), calls=%async_computation.5 | async-start | bytes 393216 | tf_op jit(solution)/shard_map/psum | solution.py:13
  769.7 2.9 copy-start.3
  784.7 333.8 %all-reduce.15.cloned.1.call-start = ((), (), s32[]{:S(2)}) async-start(), calls=%async_computation.4 | async-start | bytes 786432 | tf_op jit(solution)/shard_map/psum | solution.py:13
  896.7 2.2 copy-start.7
  899.2 1.4 copy-start.11
  1118.5 2.9 copy-start.4
Sparse Core Ops, SparseCore 0:
  89.6 109.0 all-reduce.20
  202.7 217.7 all-reduce.10
  435.9 111.8 all-reduce.18
  551.8 217.8 all-reduce.12
  784.8 111.8 all-reduce.16
  900.6 217.7 all-reduce.14
where the time goes:
time: 1130 us
  waiting for transfers between devices  1020 us (90%)
  matrix products  42.1 us (4%)
  starting transfers between devices  24.3 us (2%)
  local copies, waits for them, and re-layouts  19.2 us (2%)
  between operations  15.6 us (1%)
  other arithmetic  12.5 us (1%)
    psum x6, waiting for transfers between devices, broadcast(): return lax.psum(jnp.where(mine, array, jnp.zeros_like(array)), axis)  986 us
  transfers between devices with their start and end apart: 8, of which 8 were waited for; matrix products, arithmetic and copies ran while one was open for 1% of the time, Pallas kernels for 0%

commit v1 on v0

v1 whole, which is shorter than its diff:
```python
import functools

import jax
import jax.numpy as jnp
from jax import lax
from jax.experimental import pallas as pl
from jax.experimental.pallas import tpu as pltpu
from jax.sharding import PartitionSpec as P

SN = 128
STEPS = 3
NSI = 4
N_Z = 12
N_X = 4
F32 = jnp.float32
BF16 = jnp.bfloat16


def split(x):
    high = x.astype(BF16)
    return high, (x - high.astype(F32)).astype(BF16)


def mm(left, right):
    left_high, left_low = split(left)
    right_high, right_low = split(right)
    dot = functools.partial(jnp.dot, preferred_element_type=F32)
    return dot(left_high, right_high) + (dot(left_high, right_low) + dot(left_low, right_high))


def embed(column):
    real, imag = column[:SN], column[SN:]
    return jnp.concatenate([column, jnp.concatenate([-imag, real], axis=0)], axis=1)


def times(scalar, column):
    real, imag = column[: column.shape[0] // 2], column[column.shape[0] // 2 :]
    return jnp.concatenate(
        [scalar[0] * real - scalar[1] * imag, scalar[0] * imag + scalar[1] * real], axis=0
    )


def invert_pivot(pivot):
    row = lax.broadcasted_iota(jnp.int32, (SN, SN), 0)
    col = lax.broadcasted_iota(jnp.int32, (SN, SN), 1)
    eye = (row == col).astype(F32)
    real, imag = pivot[:SN], pivot[SN:]
    diag_real = jnp.sum(real * eye, axis=0, keepdims=True)
    diag_imag = jnp.sum(imag * eye, axis=0, keepdims=True)
    modulus = diag_real * diag_real + diag_imag * diag_imag
    inv_real, inv_imag = diag_real / modulus, -diag_imag / modulus
    residue = jnp.concatenate(
        [eye - (real * inv_real - imag * inv_imag), -(real * inv_imag + imag * inv_real)], axis=0
    )
    scale_real = jnp.sum(eye * inv_real, axis=1, keepdims=True)
    scale_imag = jnp.sum(eye * inv_imag, axis=1, keepdims=True)
    plus_real, plus_imag = eye + residue[:SN], residue[SN:]
    approx = jnp.concatenate(
        [
            scale_real * plus_real - scale_imag * plus_imag,
            scale_real * plus_imag + scale_imag * plus_real,
        ],
        axis=0,
    )
    power = mm(embed(residue), residue)
    for sweep in range(NSI - 1):
        if sweep < NSI - 2:
            both = mm(jnp.concatenate([embed(approx), embed(power)], axis=0), power)
            approx = approx + both[: 2 * SN]
            power = both[2 * SN :]
        else:
            approx = approx + mm(embed(approx), power)
    return approx


def permute_kernel(place_ref, mask_ref, raw_ref, out_ref):
    height = raw_ref.shape[0]
    for slot in range(height // SN):
        rows = slice(slot * SN, (slot + 1) * SN)
        pick = (
            place_ref[rows, :] == lax.broadcasted_iota(jnp.int32, (SN, height), 1)
        ).astype(BF16)
        got = jnp.dot(pick, raw_ref[...], preferred_element_type=F32)
        for part in range(2 * STEPS):
            out_ref[rows, part * SN : (part + 1) * SN] = (
                got[:, part * SN : (part + 1) * SN] * mask_ref[slot, part % STEPS]
            ).astype(BF16)


def root_kernel(shift_ref, which_ref, a0_ref, a1_ref, a2_ref, r0_ref, r1_ref, w_ref, u_ref):
    z_real, z_imag = shift_ref[0], shift_ref[1]
    my_col = which_ref[0]

    def block(ref, step, transposed):
        ham = ref[:, step * SN : (step + 1) * SN].astype(F32)
        over = ref[:, (STEPS + step) * SN : (STEPS + step + 1) * SN].astype(F32)
        real, imag = ham - z_real * over, -z_imag * over
        if transposed:
            real, imag = real.T, imag.T
        return jnp.concatenate([real, imag], axis=0)

    a_refs = (a0_ref, a1_ref, a2_ref)
    rows = [
        jnp.concatenate(
            [block(a_refs[t], s, False) for s in range(STEPS)]
            + [block(r0_ref, t, True), block(r1_ref, t, True)],
            axis=1,
        )
        for t in range(STEPS)
    ]
    inverse, solved, lower = [], [], {}
    for t in range(STEPS):
        inverse.append(invert_pivot(rows[t][:, t * SN : (t + 1) * SN]))
        solved.append(mm(embed(inverse[t]), rows[t][:, (t + 1) * SN :]))
        for i in range(t + 1, STEPS):
            lower[i, t] = embed(rows[i][:, t * SN : (t + 1) * SN])
            changed = rows[i][:, (t + 1) * SN :] - mm(lower[i, t], solved[t])
            rows[i] = jnp.concatenate([rows[i][:, : (t + 1) * SN], changed], axis=1)

    def upper(t, s):
        return embed(solved[t][:, (s - t - 1) * SN : (s - t) * SN])

    def right(t):
        return solved[t][:, (STEPS - 1 - t) * SN :]

    def chosen(t, special):
        unit = jnp.where(my_col == t, inverse[t], jnp.zeros_like(inverse[t]))
        first = jnp.where(special, unit, right(t)[:, :SN])
        return jnp.concatenate([first, right(t)[:, SN:]], axis=1)

    y = [chosen(t, my_col < STEPS) for t in range(STEPS)]
    w2 = y[2]
    w1 = y[1] - mm(upper(1, 2), w2)
    w0 = y[0] - (mm(upper(0, 1), w1) + mm(upper(0, 2), w2))
    for t, w in enumerate((w0, w1, w2)):
        w_ref[0, t * SN : (t + 1) * SN, :] = w[:SN].astype(BF16)
        w_ref[1, t * SN : (t + 1) * SN, :] = w[SN:].astype(BF16)
    u1 = mm(lower[1, 0], chosen(0, my_col < 1))
    u2 = mm(lower[2, 0], chosen(0, my_col < 2)) + mm(lower[2, 1], chosen(1, my_col < 2))
    for i, u in enumerate((u1, u2)):
        u_ref[i, 0] = u[:SN].astype(BF16)
        u_ref[i, 1] = u[SN:].astype(BF16)


def final_kernel(
    shift_ref, which_ref, mask_ref, place_ref, main_ref, panel_ref, w_ref, u_ref, out_ref
):
    z_real, z_imag = shift_ref[0], shift_ref[1]
    my_row, my_col, grid_rows = which_ref[1], which_ref[0], which_ref[2]
    height, width = out_ref.shape[1], out_ref.shape[2]
    w_real, w_imag = w_ref[0].astype(F32), w_ref[1].astype(F32)
    depth = w_real.shape[0]
    w_all = jnp.concatenate(
        [
            jnp.concatenate([w_ref[0], w_ref[1]], axis=1),
            jnp.concatenate(
                [z_imag * w_imag - z_real * w_real, -z_real * w_imag - z_imag * w_real], axis=1
            ).astype(BF16),
        ],
        axis=0,
    )
    ham_raw = main_ref[:, :16, :].reshape(height, width)
    over_raw = main_ref[:, 16:, :].reshape(height, width)
    for slot in range(height // SN):
        rows = slice(slot * SN, (slot + 1) * SN)
        pick = (
            place_ref[rows, :] == lax.broadcasted_iota(jnp.int32, (SN, height), 1)
        ).astype(BF16)
        ham = jnp.dot(pick, ham_raw, preferred_element_type=F32)
        over = jnp.dot(pick, over_raw, preferred_element_type=F32)
        real, imag = ham - z_real * over, -z_imag * over
        change = jnp.dot(panel_ref[rows, :], w_all, preferred_element_type=F32)
        change_real, change_imag = change[:, :width], change[:, width:]
        if slot == 0:
            early = my_row < STEPS
            change_real = jnp.where(early, u_ref[0].astype(F32), change_real)
            change_imag = jnp.where(early, u_ref[1].astype(F32), change_imag)
        node = my_row + grid_rows * slot
        for half in range(width // SN):
            cols = slice(half * SN, (half + 1) * SN)
            keep, sign = mask_ref[slot, half], F32(-1.0)
            if half == 0:
                factor = (my_col < STEPS) & (node > my_col)
                keep = jnp.where(factor, 0.0, keep)
                sign = jnp.where(factor, 1.0, -1.0)
            out_ref[0, rows, cols] = real[:, cols] * keep + change_real[:, cols] * sign
            out_ref[1, rows, cols] = imag[:, cols] * keep + change_imag[:, cols] * sign


def structure(parent, node_count):
    node_index = jnp.arange(node_count, dtype=jnp.int32)
    reached = (parent[:, None] == node_index[None, :]).astype(BF16)
    for level_index in range(node_count.bit_length()):
        more = jnp.dot(reached, reached, preferred_element_type=F32)
        reached = ((reached.astype(F32) + more) > 0.5).astype(BF16)
    diagonal_ones = (node_index[:, None] == node_index[None, :]).astype(F32)
    return jnp.minimum(diagonal_ones + reached.astype(F32) + reached.T.astype(F32), 1.0)


def body(hamiltonian, margin, pole_shift, row_map, parent):
    grid_rows = lax.axis_size("prow")
    grid_cols = lax.axis_size("pcol")
    my_row = lax.axis_index("prow")
    my_col = lax.axis_index("pcol")
    node_count = parent.shape[0]
    band = hamiltonian.shape[0]
    height = band * grid_cols
    width = hamiltonian.shape[1] // grid_cols
    row_slots, col_slots = height // SN, width // SN

    own = jnp.concatenate(
        [array[:, t * width : t * width + SN] for array in (hamiltonian, margin) for t in range(STEPS)],
        axis=1,
    )
    along_z = [[z * N_X + x for z in range(N_Z)] for x in range(N_X)]
    along_x = [[z * N_X + x for x in range(N_X)] for z in range(N_Z)]
    panel_z = lax.all_to_all(
        jnp.broadcast_to(own[None], (N_Z,) + own.shape), "pcol", 0, 0, axis_index_groups=along_z
    ).reshape(N_Z * band, -1)
    panel_raw = lax.all_to_all(
        jnp.broadcast_to(panel_z[None], (N_X,) + panel_z.shape),
        "pcol",
        0,
        0,
        axis_index_groups=along_x,
    ).reshape(height, -1)
    main = lax.all_to_all(
        jnp.concatenate(
            [array.reshape(band, grid_cols, width) for array in (hamiltonian, margin)], axis=0
        ),
        "pcol",
        split_axis=1,
        concat_axis=0,
        tiled=True,
    )
    pattern = structure(parent, node_count)
    row_nodes = jnp.arange(row_slots, dtype=jnp.int32) * grid_rows + my_row
    col_nodes = jnp.arange(col_slots, dtype=jnp.int32) * grid_cols + my_col
    all_nodes = jnp.arange(node_count, dtype=jnp.int32)
    pick_rows = (row_nodes[:, None] == all_nodes[None, :]).astype(F32)
    pick_cols = (col_nodes[:, None] == all_nodes[None, :]).astype(F32)
    row_pattern = jnp.dot(pick_rows, pattern)
    local_pattern = jnp.dot(row_pattern, pick_cols.T)
    panel_pattern = row_pattern[:, :STEPS]

    place = row_map - my_row * height
    source, inner = place // band, place % band
    panel_place = ((source % N_X) * N_Z + source // N_X) * band + inner
    smem = pl.BlockSpec(memory_space=pltpu.SMEM)
    vmem = pl.BlockSpec(memory_space=pltpu.VMEM)
    params = pltpu.CompilerParams(vmem_limit_bytes=40 * 1024 * 1024)
    which = jnp.stack([my_col, my_row, jnp.int32(grid_rows)]).astype(jnp.int32)

    panel = pl.pallas_call(
        permute_kernel,
        out_shape=jax.ShapeDtypeStruct(panel_raw.shape, BF16),
        in_specs=[vmem, smem, vmem],
        out_specs=vmem,
        compiler_params=params,
        name="permute_panel",
    )(panel_place[:, None], panel_pattern, panel_raw)

    both = ("prow", "pcol")

    def device(row, col):
        return row * grid_cols + col

    roots = [c % grid_rows for c in range(grid_cols)]
    pivot_rows = [
        lax.ppermute(
            panel[:SN], both, [(device(t, c), device(roots[c], c)) for c in range(grid_cols)]
        )
        for t in range(STEPS)
    ]
    slot = my_col // grid_rows
    row_blocks = [
        lax.dynamic_slice_in_dim(panel, (slot + half * (grid_cols // grid_rows)) * SN, SN, 0)
        for half in range(col_slots)
    ]
    w, u = pl.pallas_call(
        root_kernel,
        out_shape=(
            jax.ShapeDtypeStruct((2, STEPS * SN, width), BF16),
            jax.ShapeDtypeStruct((STEPS - 1, 2, SN, width), BF16),
        ),
        in_specs=[smem, smem] + [vmem] * 5,
        out_specs=(vmem, vmem),
        compiler_params=params,
        name="pivot_chain",
    )(pole_shift, which, *pivot_rows, *row_blocks)

    my_root = my_col % grid_rows
    offset = (my_row // 2 - my_root // 2) % (grid_rows // 2)
    same_core = my_row % 2 == my_root % 2
    early = [
        lax.ppermute(
            u[i - 1], both, [(device(roots[c], c), device(i, c)) for c in range(grid_cols)]
        )
        for i in range(1, STEPS)
    ]
    u_here = jnp.where(my_row == 1, early[0], early[1])
    u_here = jnp.where(my_row == 0, jnp.zeros_like(u_here), u_here)
    held = [0]
    chips = grid_rows // 2
    stride = chips // 2
    while stride:
        pairs = [
            (
                device((roots[c] + 2 * h) % grid_rows, c),
                device((roots[c] + 2 * (h + stride)) % grid_rows, c),
            )
            for c in range(grid_cols)
            for h in held
        ]
        came = lax.ppermute(w, both, pairs)
        new = [h + stride for h in held]
        takes = functools.reduce(jnp.logical_or, [offset == n for n in new]) & same_core
        w = jnp.where(takes, came, w)
        held = held + new
        stride //= 2
    pairs = [
        (
            device((roots[c] + 2 * h) % grid_rows, c),
            device(((roots[c] + 2 * h) % grid_rows) ^ 1, c),
        )
        for c in range(grid_cols)
        for h in held
    ]
    came = lax.ppermute(w, both, pairs)
    w = jnp.where(same_core, w, came)

    out = pl.pallas_call(
        final_kernel,
        out_shape=jax.ShapeDtypeStruct((2, height, width), F32),
        in_specs=[smem, smem, smem] + [vmem] * 5,
        out_specs=vmem,
        compiler_params=params,
        name="update",
    )(
        pole_shift,
        which,
        local_pattern,
        place[:, None],
        main.reshape(grid_cols, 2 * band, width),
        panel,
        w,
        u_here,
    )
    return out


def solution(mesh):
    return jax.shard_map(
        body,
        mesh=mesh,
        in_specs=(P(("prow", "pcol"), None), P(("prow", "pcol"), None), P("pole"), P("prow"), P()),
        out_specs=P("pole", "prow", "pcol"),
        check_vma=False,
    )
```

time: 1130 us -> 126 us (0.11)
  the two profiles are of different devices: /device:TPU:8 before, /device:TPU:40 now
where the time goes in v1:
time: 126 us
  waiting for transfers between devices  53.3 us (42%)
  starting transfers between devices  46.3 us (37%)
  Pallas kernels  13.1 us (10%)
  local copies, waits for them, and re-layouts  7.05 us (6%)
  matrix products  3.14 us (2%)
  other arithmetic  2.07 us (2%)
    all_to_all x1, starting transfers between devices, body(): lax.all_to_all(jnp.concatenate([array.reshape(band, grid_cols, width) for...  19.3 us
    all_to_all x1, starting transfers between devices, body(): lax.all_to_all(jnp.broadcast_to(own[None], (N_Z,) + own.shape), 'pcol', 0...  15.2 us
    all_to_all x1, waiting for transfers between devices, body(): lax.all_to_all(jnp.concatenate([array.reshape(band, grid_cols, width) for...  14.5 us
    all_to_all x1, waiting for transfers between devices, body(): lax.all_to_all(jnp.broadcast_to(panel_z[None], (N_X,) + panel_z.shape), '...  13.6 us
    all_to_all x1, waiting for transfers between devices, body(): lax.all_to_all(jnp.broadcast_to(own[None], (N_Z,) + own.shape), 'pcol', 0...  13 us
    ppermute x4, waiting for transfers between devices, body(): came = lax.ppermute(w, both, pairs)  12.1 us
    pallas_call x1, Pallas kernels, body(): pl.pallas_call(root_kernel, out_shape=(jax.ShapeDtypeStruct((2, STEPS * S...  8.02 us
    all_to_all x1, starting transfers between devices, body(): lax.all_to_all(jnp.broadcast_to(panel_z[None], (N_X,) + panel_z.shape), '...  4.42 us
  transfers between devices with their start and end apart: 12, of which 5 were waited for; matrix products, arithmetic and copies ran while one was open for 5% of the time, Pallas kernels for 0%

profile of v1, /device:TPU:40, one launch (start us, length us, event | category | flops | bytes accessed | tf_op | source)
XLA Modules:
  0.0 125.5 jit_solution(2015946509360377282)
XLA Ops:
  0.7 0.7 constant_dynamic-update-slice_fusion.4
  1.4 0.7 constant_dynamic-update-slice_fusion.3
  2.1 0.7 constant_dynamic-update-slice_fusion.2
  2.8 0.7 constant_dynamic-update-slice_fusion.1
  3.5 0.7 constant_dynamic-update-slice_fusion
  4.2 0.7 broadcast_in_dim.14
  4.9 15.2 %all-to-all-start.1 = ((bf16[12,16,768]{2,1,0:T(8,128)(2,1)}), bf16[12,16,768]{2,1,0:T(8,128)(2,1)S(1)}, u32[]{:S(2)}, u32[]{:S(2)}) async-start(bf16[12,16,768]{2,1,0:T(8,128)(2,1)} %broadcast_in_dim.14), calls=%async_computation.1 | async-start | bytes 589824 | tf_op jit(solution)/shard_map/all_to_all | solution.py:217
  20.1 0.9 fusion.13
  21.1 0.9 fusion.35
  24.0 13.0 %all-to-all-done.1 = bf16[12,16,768]{2,1,0:T(8,128)(2,1)S(1)} async-done(((bf16[12,16,768]{2,1,0:T(8,128)(2,1)}), bf16[12,16,768]{2,1,0:T(8,128)(2,1)S(1)}, u32[]{:S(2)}, u32[]{:S(2)}) %all-to-all-start.1) | async-done | bytes 294944 | tf_op jit(solution)/shard_map/all_to_all | solution.py:217
  37.0 1.1 broadcast_in_dim.16
  38.1 4.4 %all-to-all-start.2 = ((bf16[4,192,768]{2,1,0:T(8,128)(2,1)}), bf16[4,192,768]{2,1,0:T(8,128)(2,1)S(1)}, u32[]{:S(2)}, u32[]{:S(2)}) async-start(bf16[4,192,768]{2,1,0:T(8,128)(2,1)} %broadcast_in_dim.16), calls=%async_computation.2 | async-start | bytes 2359296 | tf_op jit(solution)/shard_map/all_to_all | solution.py:220
  43.3 13.6 %all-to-all-done.2 = bf16[4,192,768]{2,1,0:T(8,128)(2,1)S(1)} async-done(((bf16[4,192,768]{2,1,0:T(8,128)(2,1)}), bf16[4,192,768]{2,1,0:T(8,128)(2,1)S(1)}, u32[]{:S(2)}, u32[]{:S(2)}) %all-to-all-start.2) | async-done | bytes 1179680 | tf_op jit(solution)/shard_map/all_to_all | solution.py:220
  57.0 1.7 %permute_panel.1.panel_ref = bf16[768,768]{1,0:T(8,128)(2,1)S(1)} custom-call(s32[768,1]{1,0:T(8,128)S(1)} %broadcast_in_dim.37.place_ref, f32[6,3]{1,0:T(8,128)S(1)} %bitcast.94, bf16[768,768]{1,0:T(8,128)(2,1)S(1)} %bitcast.92), custom_call_target="tpu_custom_call" | custom-call | tf_op jit(solution)/shard_map/permute_panel/pallas_call | solution.py:254
  58.8 0.8 collective-permute-start.2
  61.1 8.0 %pivot_chain.1 = (bf16[2,384,256]{2,1,0:T(8,128)(2,1)S(1)}, bf16[2,2,128,256]{3,2,1,0:T(8,128)(2,1)S(1)}) custom-call(f32[2]{0:T(128)S(1)} %copy-done, s32[3]{0:T(128)S(1)} %pad_add_fusion.which_ref, bf16[128,768]{1,0:T(8,128)(2,1)S(1)} %collective-permute-done.a0_ref, bf16[128,768]{1,0:T(8,128)(2,1)S(1)} %collective-permute-done.1.a1_ref, ...), custom_call_target="tpu_custom_call" | custom-call | tf_op jit(solution)/shard_map/pivot_chain/pallas_call | solution.py:280
  69.9 1.0 pad_maximum_fusion
  70.9 19.3 %all-to-all-start = ((bf16[32,48,256]{2,0,1:T(8,128)(2,1)}), bf16[32,48,256]{2,0,1:T(8,128)(2,1)S(1)}, u32[]{:S(2)}, u32[]{:S(2)}) async-start(bf16[32,48,256]{2,0,1:T(8,128)(2,1)} %pad_maximum_fusion), calls=%async_computation | async-start | bytes 1572864 | tf_op jit(solution)/shard_map/all_to_all | solution.py:227
  91.1 1.3 %collective-permute-start.5 = (bf16[2,384,256]{2,1,0:T(8,128)(2,1)S(1)}, bf16[2,384,256]{2,1,0:T(8,128)(2,1)S(1)}, u32[]{:S(2)}, u32[]{:S(2)}) collective-permute-start(bf16[2,384,256]{2,1,0:T(8,128)(2,1)S(1)} %broadcast_select_fusion.1), channel_id=1, source_target_pairs={{0,96},{384,480},{192,288},{576,672},{49,145},{433,529},{241,337},... | collective-permute-start | bytes 1179656 | tf_op jit(solution)/shard_map/ppermute | solution.py:315
  94.0 11.0 %collective-permute-done.5 = bf16[2,384,256]{2,1,0:T(8,128)(2,1)S(1)} collective-permute-done((bf16[2,384,256]{2,1,0:T(8,128)(2,1)S(1)}, bf16[2,384,256]{2,1,0:T(8,128)(2,1)S(1)}, u32[]{:S(2)}, u32[]{:S(2)}) %collective-permute-start.5) | collective-permute-done | bytes 393248 | tf_op jit(solution)/shard_map/ppermute | solution.py:315
  105.0 1.3 %collective-permute-start.6 = (bf16[2,384,256]{2,1,0:T(8,128)(2,1)S(1)}, bf16[2,384,256]{2,1,0:T(8,128)(2,1)S(1)}, u32[]{:S(2)}, u32[]{:S(2)}) collective-permute-start(bf16[2,384,256]{2,1,0:T(8,128)(2,1)S(1)} %broadcast_select_fusion.2), channel_id=1, source_target_pairs={{0,48},{384,432},{192,240},{576,624},{96,144},{480,528},{288,336},... | collective-permute-start | bytes 1179656 | tf_op jit(solution)/shard_map/ppermute | solution.py:329
  106.6 1.1 collective-permute-done.6
  107.7 14.5 %all-to-all-done = bf16[32,48,256]{2,0,1:T(8,128)(2,1)S(1)} async-done(((bf16[32,48,256]{2,0,1:T(8,128)(2,1)}), bf16[32,48,256]{2,0,1:T(8,128)(2,1)S(1)}, u32[]{:S(2)}, u32[]{:S(2)}) %all-to-all-start) | async-done | bytes 786464 | tf_op jit(solution)/shard_map/all_to_all | solution.py:227
  122.2 3.3 %update.1 = f32[2,768,256]{2,1,0:T(8,128)} custom-call(f32[2]{0:T(128)S(1)} %copy-done, s32[3]{0:T(128)S(1)} %pad_add_fusion.which_ref, f32[6,2]{1,0:T(8,128)S(1)} %fusion.62.mask_ref, s32[768,1]{1,0:T(8,128)S(1)} %broadcast_in_dim.36.place_ref, bf16[48,32,256]{2,1,0:T(8,128)(2,1)S(1)} %bitcast.93, bf16[768,768]{1,0:T(8,128)(2,1)S(1)} %permute_panel.1.panel_ref, ...), custom_call_target="tpu_custom_call" | custom-call | tf_op jit(solution)/shard_map/update/pallas_call | solution.py:332
  (58 shorter events, 8.2 us)
Async XLA Ops:
  4.9 32.1 %all-to-all-start.1 = ((bf16[12,16,768]{2,1,0:T(8,128)(2,1)}), bf16[12,16,768]{2,1,0:T(8,128)(2,1)S(1)}, u32[]{:S(2)}, u32[]{:S(2)}) async-start(bf16[12,16,768]{2,1,0:T(8,128)(2,1)} %broadcast_in_dim.14), calls=%async_computation.1 | async-start | bytes 589824 | tf_op jit(solution)/shard_map/all_to_all | solution.py:217
  38.1 4.8 %copy-start.4 = (s32[768]{0:T(1024)S(1)}, s32[768]{0:T(1024)}, u32[]{:S(2)}) copy-start(s32[768]{0:T(1024)} %param.8) | copy-start | bytes 9220
  38.1 5.0 %copy-start.3 = (s32[96]{0:T(128)S(1)}, s32[96]{0:T(128)}, u32[]{:S(2)}) copy-start(s32[96]{0:T(128)} %param.9) | copy-start | bytes 1156
  38.1 18.9 %all-to-all-start.2 = ((bf16[4,192,768]{2,1,0:T(8,128)(2,1)}), bf16[4,192,768]{2,1,0:T(8,128)(2,1)S(1)}, u32[]{:S(2)}, u32[]{:S(2)}) async-start(bf16[4,192,768]{2,1,0:T(8,128)(2,1)} %broadcast_in_dim.16), calls=%async_computation.2 | async-start | bytes 2359296 | tf_op jit(solution)/shard_map/all_to_all | solution.py:220
  57.0 4.1 %copy-start = (f32[2]{0:T(128)S(1)}, f32[2]{0:T(128)}, u32[]{:S(2)}) copy-start(f32[2]{0:T(128)} %shift_ref.3) | copy-start | bytes 28
  58.7 11.1 %copy-start.1 = (bf16[16,12288]{1,0:T(8,128)(2,1)S(1)}, bf16[16,12288]{1,0:T(8,128)(2,1)}, u32[]{:S(2)}) copy-start(bf16[16,12288]{1,0:T(8,128)(2,1)} %param.6) | copy-start | bytes 1179652
  58.7 11.1 %copy-start.2 = (bf16[16,12288]{1,0:T(8,128)(2,1)S(1)}, bf16[16,12288]{1,0:T(8,128)(2,1)}, u32[]{:S(2)}) copy-start(bf16[16,12288]{1,0:T(8,128)(2,1)} %param.5) | copy-start | bytes 1179652
  58.8 2.3 %collective-permute-start.2 = (bf16[128,768]{1,0:T(8,128)(2,1)S(1)}, bf16[128,768]{1,0:T(8,128)(2,1)S(1)}, u32[]{:S(2)}, u32[]{:S(2)}) collective-permute-start(bf16[128,768]{1,0:T(8,128)(2,1)S(1)} %get-tuple-element.13), channel_id=1, source_target_pairs={{96,0},{97,49},{98,98},{99,147},{100,196},{101,245},{102,294},{103... | collective-permute-start | bytes 589832 | tf_op jit(solution)/shard_map/ppermute | solution.py:270
  59.6 1.4 %collective-permute-start.1 = (bf16[128,768]{1,0:T(8,128)(2,1)S(1)}, bf16[128,768]{1,0:T(8,128)(2,1)S(1)}, u32[]{:S(2)}, u32[]{:S(2)}) collective-permute-start(bf16[128,768]{1,0:T(8,128)(2,1)S(1)} %get-tuple-element.13), channel_id=1, source_target_pairs={{48,0},{49,49},{50,98},{51,147},{52,196},{53,245},{54,294},{55,343... | collective-permute-start | bytes 589832 | tf_op jit(solution)/shard_map/ppermute | solution.py:270
  60.3 0.8 collective-permute-start
  69.1 21.2 %collective-permute-start.3 = (bf16[2,384,256]{2,1,0:T(8,128)(2,1)S(1)}, bf16[2,384,256]{2,1,0:T(8,128)(2,1)S(1)}, u32[]{:S(2)}, u32[]{:S(2)}) collective-permute-start(bf16[2,384,256]{2,1,0:T(8,128)(2,1)S(1)} %get-tuple-element.7), channel_id=1, source_target_pairs={{0,384},{49,433},{98,482},{147,531},{196,580},{245,629},{294,678},... | collective-permute-start | bytes 1179656 | tf_op jit(solution)/shard_map/ppermute | solution.py:315
  70.9 51.3 %all-to-all-start = ((bf16[32,48,256]{2,0,1:T(8,128)(2,1)}), bf16[32,48,256]{2,0,1:T(8,128)(2,1)S(1)}, u32[]{:S(2)}, u32[]{:S(2)}) async-start(bf16[32,48,256]{2,0,1:T(8,128)(2,1)} %pad_maximum_fusion), calls=%async_computation | async-start | bytes 1572864 | tf_op jit(solution)/shard_map/all_to_all | solution.py:227
  90.3 0.7 collective-permute-start.4
  91.1 13.9 %collective-permute-start.5 = (bf16[2,384,256]{2,1,0:T(8,128)(2,1)S(1)}, bf16[2,384,256]{2,1,0:T(8,128)(2,1)S(1)}, u32[]{:S(2)}, u32[]{:S(2)}) collective-permute-start(bf16[2,384,256]{2,1,0:T(8,128)(2,1)S(1)} %broadcast_select_fusion.1), channel_id=1, source_target_pairs={{0,96},{384,480},{192,288},{576,672},{49,145},{433,529},{241,337},... | collective-permute-start | bytes 1179656 | tf_op jit(solution)/shard_map/ppermute | solution.py:315
  92.6 14.0 %collective-permute-start.8 = (bf16[2,128,256]{2,1,0:T(8,128)(2,1)S(1)}, bf16[2,128,256]{2,1,0:T(8,128)(2,1)S(1)}, u32[]{:S(2)}, u32[]{:S(2)}) collective-permute-start(bf16[2,128,256]{2,1,0:T(8,128)(2,1)S(1)} %get-tuple-element.14), channel_id=1, source_target_pairs={{0,96},{49,97},{98,98},{147,99},{196,100},{245,101},{294,102},{343... | collective-permute-start | bytes 393224 | tf_op jit(solution)/shard_map/ppermute | solution.py:296
  93.3 13.3 %collective-permute-start.7 = (bf16[2,128,256]{2,1,0:T(8,128)(2,1)S(1)}, bf16[2,128,256]{2,1,0:T(8,128)(2,1)S(1)}, u32[]{:S(2)}, u32[]{:S(2)}) collective-permute-start(bf16[2,128,256]{2,1,0:T(8,128)(2,1)S(1)} %get-tuple-element.15), channel_id=1, source_target_pairs={{0,48},{49,49},{98,50},{147,51},{196,52},{245,53},{294,54},{343,55... | collective-permute-start | bytes 393224 | tf_op jit(solution)/shard_map/ppermute | solution.py:296
  105.0 2.6 %collective-permute-start.6 = (bf16[2,384,256]{2,1,0:T(8,128)(2,1)S(1)}, bf16[2,384,256]{2,1,0:T(8,128)(2,1)S(1)}, u32[]{:S(2)}, u32[]{:S(2)}) collective-permute-start(bf16[2,384,256]{2,1,0:T(8,128)(2,1)S(1)} %broadcast_select_fusion.2), channel_id=1, source_target_pairs={{0,48},{384,432},{192,240},{576,624},{96,144},{480,528},{288,336},... | collective-permute-start | bytes 1179656 | tf_op jit(solution)/shard_map/ppermute | solution.py:329

commit v2 on v0

v2 whole, which is shorter than its diff:
```python
import functools

import jax
import jax.numpy as jnp
from jax import lax
from jax.experimental import pallas as pl
from jax.experimental.pallas import tpu as pltpu
from jax.sharding import PartitionSpec as P

SN = 128
STEPS = 3
NSI = 4
NBW = 96
CB = 2
N_Z = 12
N_X = 4
F32 = jnp.float32
BF16 = jnp.bfloat16


def split(x):
    high = x.astype(BF16)
    return high, (x - high.astype(F32)).astype(BF16)


def embed(block):
    real, imag = block[:, :SN], block[:, SN:]
    return jnp.concatenate([block, jnp.concatenate([-imag, real], axis=1)], axis=0)


def times(left, right, passes=1):
    dot = functools.partial(jnp.dot, preferred_element_type=F32)
    if passes == 1:
        return dot(left.astype(BF16), embed(right.astype(BF16)))
    height = left.shape[0]
    left_high, left_low = split(left)
    right_high, right_low = split(right)
    both = dot(jnp.concatenate([left_high, left_low], axis=0), embed(right_high))
    return both[:height] + (both[height:] + dot(left_high, embed(right_low)))


def invert_pivot(pivot):
    row = lax.broadcasted_iota(jnp.int32, (SN, SN), 0)
    col = lax.broadcasted_iota(jnp.int32, (SN, SN), 1)
    eye = (row == col).astype(F32)
    real, imag = pivot[:, :SN], pivot[:, SN:]
    diag_real = jnp.sum(real * eye, axis=0, keepdims=True)
    diag_imag = jnp.sum(imag * eye, axis=0, keepdims=True)
    modulus = diag_real * diag_real + diag_imag * diag_imag
    inv_real, inv_imag = diag_real / modulus, -diag_imag / modulus
    res_real = eye - (real * inv_real - imag * inv_imag)
    res_imag = -(real * inv_imag + imag * inv_real)
    scale_real = jnp.sum(eye * inv_real, axis=1, keepdims=True)
    scale_imag = jnp.sum(eye * inv_imag, axis=1, keepdims=True)
    plus_real = eye + res_real
    approx = jnp.concatenate(
        [
            scale_real * plus_real - scale_imag * res_imag,
            scale_real * res_imag + scale_imag * plus_real,
        ],
        axis=1,
    )
    residue = jnp.concatenate([res_real, res_imag], axis=1)
    power = times(residue, residue, 3)
    for sweep in range(NSI - 2):
        both = times(jnp.concatenate([approx, power], axis=0), power, 3 if sweep == 0 else 1)
        approx, power = approx + both[:SN], both[SN:]
    return approx + times(approx, power)


def spread_kernel(ham_ref, over_ref, out_ref, own_ref, sems):
    stride = ham_ref.shape[1] // (NBW // CB)
    copies = []
    for k, ref in enumerate((ham_ref, over_ref)):
        for t in range(STEPS):
            piece = k * STEPS + t
            copies.append(
                pltpu.make_async_copy(
                    ref.at[:, t * stride : t * stride + SN],
                    own_ref.at[:, piece * SN : (piece + 1) * SN],
                    sems.at[piece],
                )
            )
    for copy in copies:
        copy.start()
    for copy in copies:
        copy.wait()
    for receiver in range(out_ref.shape[0]):
        out_ref[receiver] = own_ref[...]


def pick_rows(place, chunks):
    start, total = 0, None
    for chunk in chunks:
        length = chunk.shape[0]
        pick = (
            place - start == lax.broadcasted_iota(jnp.int32, (SN, length), 1)
        ).astype(BF16)
        part = jnp.dot(pick, chunk[...], preferred_element_type=F32)
        total = part if total is None else total + part
        start += length
    return total


def store_masked(out_ref, rows, got, mask_ref, slot):
    for part in range(2 * STEPS):
        cols = slice(part * SN, (part + 1) * SN)
        out_ref[rows, cols] = (got[:, cols] * mask_ref[slot, part % STEPS]).astype(BF16)


def early_kernel(slot_ref, mask_ref, place_ref, *refs):
    chunks, (own_ref, cross_ref) = refs[:-2], refs[-2:]
    place = place_ref[0:SN, :]
    store_masked(own_ref, slice(0, SN), pick_rows(place, chunks), mask_ref, 0)
    for half in range(cross_ref.shape[0] // SN):
        slot = slot_ref[half]
        place = place_ref[pl.ds(pl.multiple_of(slot * SN, SN), SN), :]
        rows = slice(half * SN, (half + 1) * SN)
        store_masked(cross_ref, rows, pick_rows(place, chunks), mask_ref, slot)


def panel_kernel(mask_ref, place_ref, *refs):
    chunks, out_ref = refs[:-1], refs[-1]
    for slot in range(out_ref.shape[0] // SN):
        rows = slice(slot * SN, (slot + 1) * SN)
        store_masked(out_ref, rows, pick_rows(place_ref[rows, :], chunks), mask_ref, slot)


def for_raw_rows(z_real, z_imag, blocks):
    real, imag = blocks
    return z_imag * imag - z_real * real, -z_real * imag - z_imag * real


def pivot_kernel(
    shift_ref,
    which_ref,
    a0_ref,
    a1_ref,
    a2_ref,
    solve_ref,
    early_ref,
    column_ref,
    factor_ref,
    rows_ref,
    sems,
):
    z_real, z_imag = shift_ref[0], shift_ref[1]
    my_col = which_ref[0]
    copies = [
        pltpu.make_async_copy(ref, rows_ref.at[t], sems.at[t])
        for t, ref in enumerate((a0_ref, a1_ref, a2_ref))
    ]
    for copy in copies:
        copy.start()
    for copy in copies:
        copy.wait()

    def block(t, step):
        ham = rows_ref[t, :, step * SN : (step + 1) * SN].astype(F32)
        over = rows_ref[t, :, (STEPS + step) * SN : (STEPS + step + 1) * SN].astype(F32)
        return jnp.concatenate([ham - z_real * over, -z_imag * over], axis=1)

    a = [[block(t, s) for s in range(STEPS)] for t in range(STEPS)]
    x, f, k = [], {}, {}
    for t in range(STEPS):
        x.append(invert_pivot(a[t][t]))
        if t == STEPS - 1:
            break
        below = times(jnp.concatenate([a[i][t] for i in range(t + 1, STEPS)], axis=0), x[t], 3)
        for s in range(t + 1, STEPS):
            f[s, t] = below[(s - t - 1) * SN : (s - t) * SN]
        for s in range(t + 1, STEPS):
            change = times(below, a[t][s], 3)
            for i in range(t + 1, STEPS):
                a[i][s] = a[i][s] - change[(i - t - 1) * SN : (i - t) * SN]
    k[0, 1] = -times(x[0], a[0][1])
    k[1, 2] = -times(x[1], a[1][2])
    k[0, 2] = times(k[0, 1], k[1, 2]) - times(x[0], a[0][2])
    g = {(t, t): x[t] for t in range(STEPS)}
    g[1, 0] = -times(x[1], f[1, 0])
    g[2, 1] = -times(x[2], f[2, 1])
    g[2, 0] = -times(g[2, 1], f[1, 0]) - times(x[2], f[2, 0])
    zero = jnp.zeros((SN, 2 * SN), F32)
    half = STEPS * SN

    def store(ref, t, parts, offset, stride):
        real = jnp.concatenate([p[:, :SN] for p in parts], axis=1)
        imag = jnp.concatenate([p[:, SN:] for p in parts], axis=1)
        rows = slice(t * SN, (t + 1) * SN)
        ref[rows, offset : offset + real.shape[1]] = real.astype(BF16)
        ref[rows, offset + stride : offset + stride + real.shape[1]] = imag.astype(BF16)
        rows = slice(half + t * SN, half + (t + 1) * SN)
        real, imag = for_raw_rows(z_real, z_imag, (real, imag))
        ref[rows, offset : offset + real.shape[1]] = real.astype(BF16)
        ref[rows, offset + stride : offset + stride + real.shape[1]] = imag.astype(BF16)

    for t in range(STEPS):
        parts = []
        for s in range(STEPS):
            total = g[t, s] if s <= t else None
            for i in range(max(t + 1, s), STEPS):
                term = times(k[t, i], g[i, s])
                total = term if total is None else total + term
            parts.append(total)
        store(solve_ref, t, parts, 0, half)
        for i in range(1, STEPS):
            store(early_ref, t, [-k[t, i] if i > t else zero], (i - 1) * 2 * SN, SN)
    for s in range(STEPS):
        total = zero
        for t in range(s, STEPS):
            total = jnp.where(my_col == t, g[t, s], total)
        column_ref[:, s * SN : (s + 1) * SN] = total[:, :SN].astype(BF16)
        column_ref[:, half + s * SN : half + (s + 1) * SN] = total[:, SN:].astype(BF16)
    factor_ref[0] = f[1, 0]
    factor_ref[1] = jnp.where(my_col == 0, f[2, 0], f[2, 1])


def solve_kernel(which_ref, cross_ref, solve_ref, column_ref, v_ref):
    v = jnp.dot(cross_ref[...], solve_ref[...], preferred_element_type=F32).astype(BF16)
    v_ref[SN:] = v[SN:]
    v_ref[:SN] = jnp.where(which_ref[0] < STEPS, column_ref[...], v[:SN])


def pivot_rows_kernel(which_ref, cross_ref, early_ref, factor_ref, u_ref):
    my_col = which_ref[0]
    change = jnp.dot(cross_ref[...], early_ref[...], preferred_element_type=F32)
    for i in range(STEPS - 1):
        for part in range(2):
            cols = slice((2 * i + part) * SN, (2 * i + part + 1) * SN)
            for half in range(cross_ref.shape[0] // SN):
                block = change[half * SN : (half + 1) * SN, cols].T
                if half == 0:
                    factor = factor_ref[i, :, part * SN : (part + 1) * SN]
                    block = jnp.where(my_col < i + 1, factor, block)
                u_ref[i, part, :, half * SN : (half + 1) * SN] = block.astype(BF16)


def is_factor(which_ref, slot, half):
    node = which_ref[1] + which_ref[2] * slot
    return (which_ref[0] < STEPS) & (node > which_ref[0]) if half == 0 else None


def assemble_kernel(shift_ref, which_ref, mask_ref, place_ref, main_ref, out_ref):
    z_real, z_imag = shift_ref[0], shift_ref[1]
    height, width = out_ref.shape[1], out_ref.shape[2]
    band = main_ref.shape[1] // 2
    ham_raw = main_ref[:, :band, :].reshape(height, width)
    over_raw = main_ref[:, band:, :].reshape(height, width)
    for slot in range(height // SN):
        rows = slice(slot * SN, (slot + 1) * SN)
        place = place_ref[rows, :]
        ham = pick_rows(place, [ham_raw])
        over = pick_rows(place, [over_raw])
        real, imag = ham - z_real * over, -z_imag * over
        for half in range(width // SN):
            cols = slice(half * SN, (half + 1) * SN)
            keep = mask_ref[slot, half]
            factor = is_factor(which_ref, slot, half)
            if factor is not None:
                keep = jnp.where(factor, 0.0, keep)
            out_ref[0, rows, cols] = real[:, cols] * keep
            out_ref[1, rows, cols] = imag[:, cols] * keep


def update_kernel(
    shift_ref, which_ref, base_ref, panel_ref, v_ref, v_other_ref, u1_ref, u2_ref, out_ref
):
    z_real, z_imag = shift_ref[0], shift_ref[1]
    my_row, own = which_ref[1], which_ref[3] > 0
    height, width = out_ref.shape[1], out_ref.shape[2]
    v = jnp.where(own, v_ref[...], v_other_ref[...])
    half_depth = v.shape[1] // 2
    v_real, v_imag = v[:, :half_depth], v[:, half_depth:]
    m_real, m_imag = for_raw_rows(z_real, z_imag, (v_real.astype(F32), v_imag.astype(F32)))
    v_all = jnp.concatenate(
        [
            jnp.concatenate([v_real, m_real.astype(BF16)], axis=1),
            jnp.concatenate([v_imag, m_imag.astype(BF16)], axis=1),
        ],
        axis=0,
    )
    for slot in range(height // SN):
        rows = slice(slot * SN, (slot + 1) * SN)
        change = lax.dot_general(
            panel_ref[rows, :], v_all, (((1,), (1,)), ((), ())), preferred_element_type=F32
        )
        for part in range(2):
            part_change = change[:, part * width : (part + 1) * width]
            if slot == 0:
                later = jnp.where(my_row == 1, u1_ref[part].astype(F32), part_change)
                later = jnp.where(my_row == 2, u2_ref[part].astype(F32), later)
                part_change = jnp.where(my_row == 0, 0.0, later)
            for half in range(width // SN):
                cols = slice(half * SN, (half + 1) * SN)
                factor = is_factor(which_ref, slot, half)
                sign = -1.0 if factor is None else jnp.where(factor, 1.0, -1.0)
                out_ref[part, rows, cols] = (
                    base_ref[part, rows, cols] + part_change[:, cols] * sign
                )


def structure(parent, node_count):
    node_index = jnp.arange(node_count, dtype=jnp.int32)
    reached = (parent[:, None] == node_index[None, :]).astype(BF16)
    for level_index in range(node_count.bit_length()):
        more = jnp.dot(reached, reached, preferred_element_type=F32)
        reached = ((reached.astype(F32) + more) > 0.5).astype(BF16)
    diagonal_ones = (node_index[:, None] == node_index[None, :]).astype(F32)
    return jnp.minimum(diagonal_ones + reached.astype(F32) + reached.T.astype(F32), 1.0)


def body(hamiltonian, margin, pole_shift, row_map, parent):
    grid_rows = lax.axis_size("prow")
    grid_cols = lax.axis_size("pcol")
    my_row = lax.axis_index("prow")
    my_col = lax.axis_index("pcol")
    node_count = parent.shape[0]
    band = hamiltonian.shape[0]
    height = band * grid_cols
    width = hamiltonian.shape[1] // grid_cols
    row_slots, col_slots = height // SN, width // SN

    smem = pl.BlockSpec(memory_space=pltpu.SMEM)
    vmem = pl.BlockSpec(memory_space=pltpu.VMEM)
    params = pltpu.CompilerParams(vmem_limit_bytes=20 * 1024 * 1024)
    both = ("prow", "pcol")

    def device(row, col):
        return row * grid_cols + col

    hbm = pl.BlockSpec(memory_space=pltpu.HBM)
    pieces = 2 * STEPS
    copies = pl.pallas_call(
        spread_kernel,
        out_shape=jax.ShapeDtypeStruct((N_Z, band, pieces * SN), BF16),
        in_specs=[hbm, hbm],
        out_specs=vmem,
        scratch_shapes=[
            pltpu.VMEM((band, pieces * SN), BF16),
            pltpu.SemaphoreType.DMA((pieces,)),
        ],
        compiler_params=params,
        name="spread",
    )(hamiltonian, margin)
    along_z = [[z * N_X + x for z in range(N_Z)] for x in range(N_X)]
    held_rows = N_Z * band
    mine = lax.all_to_all(copies, "pcol", 0, 0, axis_index_groups=along_z).reshape(held_rows, -1)

    hamiltonian, margin, mine = lax.optimization_barrier((hamiltonian, margin, mine))
    packed = jnp.concatenate(
        [array.reshape(band, grid_cols, width) for array in (hamiltonian, margin)], axis=0
    )

    def shift_x(array, by):
        return lax.ppermute(
            array, "pcol", [(c, c - c % N_X + (c % N_X + by) % N_X) for c in range(grid_cols)]
        )

    below, above = shift_x(mine, 1), shift_x(mine, -1)
    far_first = shift_x(below[: held_rows // 2], 1)
    far_last = shift_x(above[held_rows // 2 :], -1)
    chunks = [mine, above, far_first, far_last, below]
    main = lax.all_to_all(packed, "pcol", split_axis=1, concat_axis=0, tiled=True)
    pattern = structure(parent, node_count)
    row_nodes = jnp.arange(row_slots, dtype=jnp.int32) * grid_rows + my_row
    col_nodes = jnp.arange(col_slots, dtype=jnp.int32) * grid_cols + my_col
    all_nodes = jnp.arange(node_count, dtype=jnp.int32)
    pick_rows = (row_nodes[:, None] == all_nodes[None, :]).astype(F32)
    pick_cols = (col_nodes[:, None] == all_nodes[None, :]).astype(F32)
    row_pattern = jnp.dot(pick_rows, pattern)
    local_pattern = jnp.dot(row_pattern, pick_cols.T)
    panel_pattern = row_pattern[:, :STEPS]

    place = row_map - my_row * height
    source, inner = place // band, place % band
    distance = (source % N_X - my_col % N_X) % N_X
    panel_place = distance * held_rows + source // N_X * band + inner
    same_core = my_row % 2 == 0
    which = jnp.stack(
        [my_col, my_row, jnp.int32(grid_rows), same_core.astype(jnp.int32)]
    ).astype(jnp.int32)
    first_slot = my_col // grid_rows
    slots = jnp.stack([first_slot, first_slot + grid_cols // grid_rows]).astype(jnp.int32)

    depth = 2 * STEPS * SN
    own_rows, cross_rows = pl.pallas_call(
        early_kernel,
        out_shape=(
            jax.ShapeDtypeStruct((SN, depth), BF16),
            jax.ShapeDtypeStruct((width, depth), BF16),
        ),
        in_specs=[smem, smem, vmem] + [vmem] * len(chunks),
        out_specs=(vmem,) * 2,
        compiler_params=params,
        name="early_rows",
    )(slots, panel_pattern, panel_place[:, None], *chunks)
    panel = pl.pallas_call(
        panel_kernel,
        out_shape=jax.ShapeDtypeStruct((height, 2 * STEPS * SN), BF16),
        in_specs=[smem, vmem] + [vmem] * len(chunks),
        out_specs=vmem,
        compiler_params=params,
        name="panel_rows",
    )(panel_pattern, panel_place[:, None], *chunks)

    columns = range(grid_cols)
    pivot_rows = [own_rows] + [
        lax.ppermute(own_rows, both, [(device(t, c), device(0, c)) for c in columns])
        for t in range(1, STEPS)
    ]
    cross_rows = lax.ppermute(
        cross_rows, both, [(device(c % grid_rows, c), device(0, c)) for c in columns]
    )
    solve, early_solve, column, factor = pl.pallas_call(
        pivot_kernel,
        out_shape=(
            jax.ShapeDtypeStruct((depth, depth), BF16),
            jax.ShapeDtypeStruct((depth, 2 * (STEPS - 1) * SN), BF16),
            jax.ShapeDtypeStruct((SN, depth), BF16),
            jax.ShapeDtypeStruct((STEPS - 1, SN, 2 * SN), F32),
        ),
        in_specs=[smem, smem] + [pl.BlockSpec(memory_space=pl.ANY)] * STEPS,
        out_specs=(vmem,) * 4,
        scratch_shapes=[
            pltpu.VMEM((STEPS, SN, depth), BF16),
            pltpu.SemaphoreType.DMA((STEPS,)),
        ],
        compiler_params=params,
        name="pivots",
    )(pole_shift, which, *pivot_rows)
    w = pl.pallas_call(
        solve_kernel,
        out_shape=jax.ShapeDtypeStruct((width, depth), BF16),
        in_specs=[smem] + [vmem] * 3,
        out_specs=vmem,
        compiler_params=params,
        name="solve",
    )(which, cross_rows, solve, column)
    u = pl.pallas_call(
        pivot_rows_kernel,
        out_shape=jax.ShapeDtypeStruct((STEPS - 1, 2, SN, width), BF16),
        in_specs=[smem] + [vmem] * 3,
        out_specs=vmem,
        compiler_params=params,
        name="pivot_rows",
    )(which, cross_rows, early_solve, factor)

    offset = my_row // 2

    def along_y(array, hops):
        return lax.ppermute(
            array,
            both,
            [(device(2 * start, c), device(2 * end, c)) for c in columns for start, end in hops],
        )

    up, down = along_y(w, [(0, 3)]), along_y(w, [(0, 6)])
    w = jnp.where((offset == 3) & same_core, up, jnp.where((offset == 6) & same_core, down, w))
    up, down = along_y(w, [(0, 1), (3, 4)]), along_y(w, [(0, 7), (3, 2), (6, 5)])
    near = (offset == 1) | (offset == 4)
    kept = (offset == 0) | (offset == 3) | (offset == 6)
    w = jnp.where(kept, w, jnp.where(near, up, down))
    early = [
        lax.ppermute(u[i - 1], both, [(device(0, c), device(i, c)) for c in columns])
        for i in range(1, STEPS)
    ]
    base = pl.pallas_call(
        assemble_kernel,
        out_shape=jax.ShapeDtypeStruct((2, height, width), F32),
        in_specs=[smem, smem, smem] + [vmem] * 2,
        out_specs=vmem,
        compiler_params=params,
        name="assemble",
    )(pole_shift, which, local_pattern, place[:, None], main.reshape(grid_cols, 2 * band, width))
    w, base, panel, early = lax.optimization_barrier((w, base, panel, early))
    other = lax.ppermute(
        w,
        both,
        [(device(row, c), device(row + 1, c)) for c in columns for row in range(0, grid_rows, 2)],
    )
    return pl.pallas_call(
        update_kernel,
        out_shape=jax.ShapeDtypeStruct((2, height, width), F32),
        in_specs=[smem, smem] + [vmem] * 6,
        out_specs=vmem,
        compiler_params=params,
        name="update",
    )(pole_shift, which, base, panel, w, other, *early)


def solution(mesh):
    return jax.shard_map(
        body,
        mesh=mesh,
        in_specs=(P(("prow", "pcol"), None), P(("prow", "pcol"), None), P("pole"), P("prow"), P()),
        out_specs=P("pole", "prow", "pcol"),
        check_vma=False,
    )
```

time: 1130 us -> 114 us (0.10)
  the two profiles are of different devices: /device:TPU:8 before, /device:TPU:76 now
where the time goes in v2:
time: 114 us; the launch traced here: 112 us
  starting transfers between devices  45.4 us (40%)
  waiting for transfers between devices  34.7 us (30%)
  Pallas kernels  18.4 us (16%)
  local copies, waits for them, and re-layouts  10.2 us (9%)
  matrix products  1.67 us (1%)
  other arithmetic  1.43 us (1%)
    all_to_all x1, starting transfers between devices, body(): lax.all_to_all(copies, 'pcol', 0, 0, axis_index_groups=along_z)  14.8 us
    all_to_all x1, waiting for transfers between devices, body(): lax.all_to_all(copies, 'pcol', 0, 0, axis_index_groups=along_z)  13.9 us
    ppermute x4, starting transfers between devices, shift_x(): lax.ppermute(array, 'pcol', [(c, c - c % N_X + (c % N_X + by) % N_X) for...  11.7 us
    ppermute x4, waiting for transfers between devices, along_y(): lax.ppermute(array, both, [(device(2 * start, c), device(2 * end, c)) for...  8.05 us
    unnamed x50, local copies, waits for them, and re-layouts  7.75 us
    all_to_all x1, starting transfers between devices, body(): lax.all_to_all(packed, 'pcol', split_axis=1, concat_axis=0, tiled=True)  6.38 us
    pallas_call x1, Pallas kernels, body(): pl.pallas_call(pivot_kernel, out_shape=(jax.ShapeDtypeStruct((depth, dept...  5.95 us
    ppermute x2, waiting for transfers between devices, body(): lax.ppermute(own_rows, both, [(device(t, c), device(0, c)) for c in colum...  5.35 us
  transfers between devices with their start and end apart: 16, of which 7 were waited for; matrix products, arithmetic and copies ran while one was open for 5% of the time, Pallas kernels for 13%

profile of v2, /device:TPU:76, one launch (start us, length us, event | category | flops | bytes accessed | tf_op | source)
XLA Modules:
  0.0 112.3 jit_solution(1975793141802886554)
XLA Ops:
  2.8 14.8 %all-to-all-start = ((bf16[12,16,768]{2,1,0:T(8,128)(2,1)}), bf16[12,16,768]{2,1,0:T(8,128)(2,1)S(1)}, u32[]{:S(2)}, u32[]{:S(2)}) async-start(bf16[12,16,768]{2,1,0:T(8,128)(2,1)} %spread.1), calls=%async_computation | async-start | bytes 589824 | tf_op jit(solution)/shard_map/all_to_all | solution.py:347
  20.4 13.9 %all-to-all-done = bf16[12,16,768]{2,1,0:T(8,128)(2,1)S(1)} async-done(((bf16[12,16,768]{2,1,0:T(8,128)(2,1)}), bf16[12,16,768]{2,1,0:T(8,128)(2,1)S(1)}, u32[]{:S(2)}, u32[]{:S(2)}) %all-to-all-start) | async-done | bytes 294944 | tf_op jit(solution)/shard_map/all_to_all | solution.py:347
  34.3 3.1 %collective-permute-start.1 = (bf16[192,768]{1,0:T(8,128)(2,1)S(1)}, bf16[192,768]{1,0:T(8,128)(2,1)S(1)}, u32[]{:S(2)}, u32[]{:S(2)}) collective-permute-start(bf16[192,768]{1,0:T(8,128)(2,1)S(1)} %bitcast.93), channel_id=1, source_target_pairs={{0,1},{1,2},{2,3},{3,0},{4,5},{5,6},{6,7},{7,4},{8,9},{9,10},{10,1... | collective-permute-start | bytes 884744 | tf_op jit(solution)/shard_map/ppermute | solution.py:355
  37.4 2.7 %collective-permute-start = (bf16[192,768]{1,0:T(8,128)(2,1)S(1)}, bf16[192,768]{1,0:T(8,128)(2,1)S(1)}, u32[]{:S(2)}, u32[]{:S(2)}) collective-permute-start(bf16[192,768]{1,0:T(8,128)(2,1)S(1)} %bitcast.94), channel_id=1, source_target_pairs={{0,3},{1,0},{2,1},{3,2},{4,7},{5,4},{6,5},{7,6},{8,11},{9,8},{10,9... | collective-permute-start | bytes 884744 | tf_op jit(solution)/shard_map/ppermute | solution.py:355
  41.3 6.4 %all-to-all-start.1 = ((bf16[32,48,256]{2,0,1:T(8,128)(2,1)}), bf16[32,48,256]{2,0,1:T(8,128)(2,1)S(1)}, u32[]{:S(2)}, u32[]{:S(2)}) async-start(bf16[32,48,256]{2,0,1:T(8,128)(2,1)} %pad_maximum_fusion), calls=%async_computation.1 | async-start | bytes 1572864 | tf_op jit(solution)/shard_map/all_to_all | solution.py:363
  47.9 3.1 %collective-permute-start.2 = (bf16[96,768]{1,0:T(8,128)(2,1)S(1)}, bf16[96,768]{1,0:T(8,128)(2,1)S(1)}, u32[]{:S(2)}, u32[]{:S(2)}) collective-permute-start(bf16[96,768]{1,0:T(8,128)(2,1)S(1)} %slice.20), channel_id=1, source_target_pairs={{0,1},{1,2},{2,3},{3,0},{4,5},{5,6},{6,7},{7,4},{8,9},{9,10},{10,1... | collective-permute-start | bytes 442376 | tf_op jit(solution)/shard_map/ppermute | solution.py:355
  51.1 2.8 %collective-permute-start.3 = (bf16[96,768]{1,0:T(8,128)(2,1)S(1)}, bf16[96,768]{1,0:T(8,128)(2,1)S(1)}, u32[]{:S(2)}, u32[]{:S(2)}) collective-permute-start(bf16[96,768]{1,0:T(8,128)(2,1)S(1)} %slice.21), channel_id=1, source_target_pairs={{0,3},{1,0},{2,1},{3,2},{4,7},{5,4},{6,5},{7,6},{8,11},{9,8},{10,9... | collective-permute-start | bytes 442376 | tf_op jit(solution)/shard_map/ppermute | solution.py:355
  54.1 1.6 %collective-permute-done.2.refs_2_ = bf16[96,768]{1,0:T(8,128)(2,1)S(1)} collective-permute-done((bf16[96,768]{1,0:T(8,128)(2,1)S(1)}, bf16[96,768]{1,0:T(8,128)(2,1)S(1)}, u32[]{:S(2)}, u32[]{:S(2)}) %collective-permute-start.2) | collective-permute-done | bytes 147488 | tf_op jit(solution)/shard_map/ppermute | solution.py:355
  55.7 2.6 %collective-permute-done.3.refs_3_ = bf16[96,768]{1,0:T(8,128)(2,1)S(1)} collective-permute-done((bf16[96,768]{1,0:T(8,128)(2,1)S(1)}, bf16[96,768]{1,0:T(8,128)(2,1)S(1)}, u32[]{:S(2)}, u32[]{:S(2)}) %collective-permute-start.3) | collective-permute-done | bytes 147488 | tf_op jit(solution)/shard_map/ppermute | solution.py:355
  58.4 2.3 %early_rows.1 = (bf16[128,768]{1,0:T(8,128)(2,1)S(1)}, bf16[256,768]{1,0:T(8,128)(2,1)}) custom-call(s32[2]{0:T(128)S(1)} %pad_add_fusion.1.slot_ref, f32[6,3]{1,0:T(8,128)S(1)} %bitcast.99, s32[768,1]{1,0:T(8,128)S(1)} %broadcast_in_dim.7.place_ref, bf16[192,768]{1,0:T(8,128)(2,1)S(1)} %bitcast.95, bf16[192,768]{1,0:T(8,128)(2,1)S(1)} %collective-permute-done.refs_1_, ...), custom_call_target="tpu_custom_call" | custom-call | tf_op jit(solution)/shard_map/early_rows/pallas_call | solution.py:386
  62.0 3.6 %collective-permute-start.6 = (bf16[128,768]{1,0:T(8,128)(2,1)S(1)}, bf16[128,768]{1,0:T(8,128)(2,1)S(1)}, u32[]{:S(2)}, u32[]{:S(2)}) collective-permute-start(bf16[128,768]{1,0:T(8,128)(2,1)S(1)} %get-tuple-element.21.a0_ref), channel_id=1, source_target_pairs={{96,0},{97,1},{98,2},{99,3},{100,4},{101,5},{102,6},{103,7},{104,8... | collective-permute-start | bytes 589832 | tf_op jit(solution)/shard_map/ppermute | solution.py:408
  67.1 5.3 %collective-permute-done.6.a2_ref = bf16[128,768]{1,0:T(8,128)(2,1)S(1)} collective-permute-done((bf16[128,768]{1,0:T(8,128)(2,1)S(1)}, bf16[128,768]{1,0:T(8,128)(2,1)S(1)}, u32[]{:S(2)}, u32[]{:S(2)}) %collective-permute-start.6) | collective-permute-done | bytes 196640 | tf_op jit(solution)/shard_map/ppermute | solution.py:408
  75.9 5.9 %pivots.1 = (bf16[768,768]{1,0:T(8,128)(2,1)S(1)}, bf16[768,512]{1,0:T(8,128)(2,1)S(1)}, bf16[128,768]{1,0:T(8,128)(2,1)S(1)}, f32[2,128,256]{2,1,0:T(8,128)S(1)}) custom-call(f32[2]{0:T(128)S(1)} %copy-done.17, s32[4]{0:T(128)S(1)} %pad_add_fusion.which_ref, bf16[128,768]{1,0:T(8,128)(2,1)S(1)} %copy-done.12, bf16[128,768]{1,0:T(8,128)(2,1)S(1)} %copy-done.14, ...), custom_call_target="tpu_custom_call" | custom-call | tf_op jit(solution)/shard_map/pivots/pallas_call | solution.py:414
  82.7 1.0 solve.1
  84.5 1.4 %collective-permute-start.8 = (bf16[256,768]{1,0:T(8,128)(2,1)S(1)}, bf16[256,768]{1,0:T(8,128)(2,1)}, u32[]{:S(2)}, u32[]{:S(2)}) collective-permute-start(bf16[256,768]{1,0:T(8,128)(2,1)S(1)} %solve.1), channel_id=1, source_target_pairs={{0,576},{1,577},{2,578},{3,579},{4,580},{5,581},{6,582},{7,583},{8... | collective-permute-start | bytes 1179656 | tf_op jit(solution)/shard_map/ppermute | solution.py:451
  87.8 1.4 %collective-permute-start.9 = (bf16[256,768]{1,0:T(8,128)(2,1)S(1)}, bf16[256,768]{1,0:T(8,128)(2,1)S(1)}, u32[]{:S(2)}, u32[]{:S(2)}) collective-permute-start(bf16[256,768]{1,0:T(8,128)(2,1)S(1)} %select_select_fusion.1), channel_id=1, source_target_pairs={{0,96},{288,384},{1,97},{289,385},{2,98},{290,386},{3,99},{291,387... | collective-permute-start | bytes 1179656 | tf_op jit(solution)/shard_map/ppermute | solution.py:451
  89.4 2.4 %panel_rows.1.panel_ref = bf16[768,768]{1,0:T(8,128)(2,1)S(1)} custom-call(f32[6,3]{1,0:T(8,128)S(1)} %bitcast.100, s32[768,1]{1,0:T(8,128)S(1)} %broadcast_in_dim.7.place_ref, bf16[192,768]{1,0:T(8,128)(2,1)S(1)} %bitcast.96, bf16[192,768]{1,0:T(8,128)(2,1)S(1)} %collective-permute-done.refs_1_, bf16[96,768]{1,0:T(8,128)(2,1)S(1)} %collective-permute-done.2.refs_2_, ...), custom_call_target="tpu_custom_call" | custom-call | tf_op jit(solution)/shard_map/panel_rows/pallas_call | solution.py:397
  93.5 1.3 %collective-permute-start.12 = (bf16[2,128,256]{2,1,0:T(8,128)(2,1)S(1)}, bf16[2,128,256]{2,1,0:T(8,128)(2,1)S(1)}, u32[]{:S(2)}, u32[]{:S(2)}) collective-permute-start(bf16[2,128,256]{2,1,0:T(8,128)(2,1)S(1)} %get-tuple-element.35), channel_id=1, source_target_pairs={{0,96},{1,97},{2,98},{3,99},{4,100},{5,101},{6,102},{7,103},{8,104... | collective-permute-start | bytes 393224 | tf_op jit(solution)/shard_map/ppermute | solution.py:464
  94.9 8.0 %collective-permute-done.9 = bf16[256,768]{1,0:T(8,128)(2,1)S(1)} collective-permute-done((bf16[256,768]{1,0:T(8,128)(2,1)S(1)}, bf16[256,768]{1,0:T(8,128)(2,1)S(1)}, u32[]{:S(2)}, u32[]{:S(2)}) %collective-permute-start.9) | collective-permute-done | bytes 393248 | tf_op jit(solution)/shard_map/ppermute | solution.py:451
  103.0 1.5 %assemble.1.base_ref = f32[2,768,256]{2,1,0:T(8,128)S(1)} custom-call(f32[2]{0:T(128)S(1)} %copy-done.17, s32[4]{0:T(128)S(1)} %pad_add_fusion.which_ref, f32[6,2]{1,0:T(8,128)S(1)} %fusion.61.mask_ref, s32[768,1]{1,0:T(8,128)S(1)} %copy-done.2, bf16[48,32,256]{2,1,0:T(8,128)(2,1)S(1)} %bitcast.92), custom_call_target="tpu_custom_call" | custom-call | tf_op jit(solution)/shard_map/assemble/pallas_call | solution.py:467
  104.5 1.8 %collective-permute-done.12.u2_ref = bf16[2,128,256]{2,1,0:T(8,128)(2,1)S(1)} collective-permute-done((bf16[2,128,256]{2,1,0:T(8,128)(2,1)S(1)}, bf16[2,128,256]{2,1,0:T(8,128)(2,1)S(1)}, u32[]{:S(2)}, u32[]{:S(2)}) %collective-permute-start.12) | collective-permute-done | bytes 131104 | tf_op jit(solution)/shard_map/ppermute | solution.py:464
  106.3 1.3 %collective-permute-start.13 = (bf16[256,768]{1,0:T(8,128)(2,1)S(1)}, bf16[256,768]{1,0:T(8,128)(2,1)S(1)}, u32[]{:S(2)}, u32[]{:S(2)}) collective-permute-start(bf16[256,768]{1,0:T(8,128)(2,1)S(1)} %select_select_fusion.v_ref), channel_id=1, source_target_pairs={{0,48},{96,144},{192,240},{288,336},{384,432},{480,528},{576,624},... | collective-permute-start | bytes 1179656 | tf_op jit(solution)/shard_map/ppermute | solution.py:476
  107.7 1.3 %collective-permute-done.13.v_other_ref = bf16[256,768]{1,0:T(8,128)(2,1)S(1)} collective-permute-done((bf16[256,768]{1,0:T(8,128)(2,1)S(1)}, bf16[256,768]{1,0:T(8,128)(2,1)S(1)}, u32[]{:S(2)}, u32[]{:S(2)}) %collective-permute-start.13) | collective-permute-done | bytes 393248 | tf_op jit(solution)/shard_map/ppermute | solution.py:476
  109.0 3.4 %update.1 = f32[2,768,256]{2,1,0:T(8,128)} custom-call(f32[2]{0:T(128)S(1)} %copy-done.17, s32[4]{0:T(128)S(1)} %pad_add_fusion.which_ref, f32[2,768,256]{2,1,0:T(8,128)S(1)} %assemble.1.base_ref, bf16[768,768]{1,0:T(8,128)(2,1)S(1)} %panel_rows.1.panel_ref, bf16[256,768]{1,0:T(8,128)(2,1)S(1)} %select_select_fusion.v_ref, ...), custom_call_target="tpu_custom_call" | custom-call | tf_op jit(solution)/shard_map/update/pallas_call | solution.py:481
  (101 shorter events, 18.7 us)
Async XLA Ops:
  2.0 15.6 %copy-start.23 = (s32[96]{0:T(128)S(1)}, s32[96]{0:T(128)}, u32[]{:S(2)}) copy-start(s32[96]{0:T(128)} %param.9) | copy-start | bytes 1156
  2.0 38.1 %copy-start.4 = (bf16[16,12288]{1,0:T(8,128)(2,1)S(1)}, bf16[16,12288]{1,0:T(8,128)(2,1)}, u32[]{:S(2)}) copy-start(bf16[16,12288]{1,0:T(8,128)(2,1)} %over_ref.1) | copy-start | bytes 1179652
  2.0 38.2 %copy-start.6 = (bf16[16,12288]{1,0:T(8,128)(2,1)S(1)}, bf16[16,12288]{1,0:T(8,128)(2,1)}, u32[]{:S(2)}) copy-start(bf16[16,12288]{1,0:T(8,128)(2,1)} %ham_ref.1) | copy-start | bytes 1179652
  2.8 31.5 %all-to-all-start = ((bf16[12,16,768]{2,1,0:T(8,128)(2,1)}), bf16[12,16,768]{2,1,0:T(8,128)(2,1)S(1)}, u32[]{:S(2)}, u32[]{:S(2)}) async-start(bf16[12,16,768]{2,1,0:T(8,128)(2,1)} %spread.1), calls=%async_computation | async-start | bytes 589824 | tf_op jit(solution)/shard_map/all_to_all | solution.py:347
  19.5 14.8 %copy-start.21 = (pred[96,96]{0,1:T(32,128)(4,1)}, pred[96,96]{0,1:T(32,128)(4,1)S(1)}, u32[]{:S(2)}) copy-start(pred[96,96]{0,1:T(32,128)(4,1)S(1)} %add_compare_fusion.1) | copy-start | bytes 27652
  19.6 14.6 %copy-start.18 = (f32[96,96]{1,0:T(8,128)}, f32[96,96]{1,0:T(8,128)S(1)}, u32[]{:S(2)}) copy-start(f32[96,96]{1,0:T(8,128)S(1)} %fusion.25) | copy-start | bytes 110596
  34.3 13.6 %collective-permute-start.1 = (bf16[192,768]{1,0:T(8,128)(2,1)S(1)}, bf16[192,768]{1,0:T(8,128)(2,1)S(1)}, u32[]{:S(2)}, u32[]{:S(2)}) collective-permute-start(bf16[192,768]{1,0:T(8,128)(2,1)S(1)} %bitcast.93), channel_id=1, source_target_pairs={{0,1},{1,2},{2,3},{3,0},{4,5},{5,6},{6,7},{7,4},{8,9},{9,10},{10,1... | collective-permute-start | bytes 884744 | tf_op jit(solution)/shard_map/ppermute | solution.py:355
  37.4 13.6 %collective-permute-start = (bf16[192,768]{1,0:T(8,128)(2,1)S(1)}, bf16[192,768]{1,0:T(8,128)(2,1)S(1)}, u32[]{:S(2)}, u32[]{:S(2)}) collective-permute-start(bf16[192,768]{1,0:T(8,128)(2,1)S(1)} %bitcast.94), channel_id=1, source_target_pairs={{0,3},{1,0},{2,1},{3,2},{4,7},{5,4},{6,5},{7,6},{8,11},{9,8},{10,9... | collective-permute-start | bytes 884744 | tf_op jit(solution)/shard_map/ppermute | solution.py:355
  41.2 12.6 %copy-start.24 = (s32[768]{0:T(1024)S(1)}, s32[768]{0:T(1024)}, u32[]{:S(2)}) copy-start(s32[768]{0:T(1024)} %param.8) | copy-start | bytes 9220
  41.3 61.7 %all-to-all-start.1 = ((bf16[32,48,256]{2,0,1:T(8,128)(2,1)}), bf16[32,48,256]{2,0,1:T(8,128)(2,1)S(1)}, u32[]{:S(2)}, u32[]{:S(2)}) async-start(bf16[32,48,256]{2,0,1:T(8,128)(2,1)} %pad_maximum_fusion), calls=%async_computation.1 | async-start | bytes 1572864 | tf_op jit(solution)/shard_map/all_to_all | solution.py:363
  47.7 25.4 %copy-start.17 = (f32[2]{0:T(128)S(1)}, f32[2]{0:T(128)}, u32[]{:S(2)}) copy-start(f32[2]{0:T(128)} %shift_ref.5) | copy-start | bytes 28
  47.9 7.8 %collective-permute-start.2 = (bf16[96,768]{1,0:T(8,128)(2,1)S(1)}, bf16[96,768]{1,0:T(8,128)(2,1)S(1)}, u32[]{:S(2)}, u32[]{:S(2)}) collective-permute-start(bf16[96,768]{1,0:T(8,128)(2,1)S(1)} %slice.20), channel_id=1, source_target_pairs={{0,1},{1,2},{2,3},{3,0},{4,5},{5,6},{6,7},{7,4},{8,9},{9,10},{10,1... | collective-permute-start | bytes 442376 | tf_op jit(solution)/shard_map/ppermute | solution.py:355
  51.1 7.3 %collective-permute-start.3 = (bf16[96,768]{1,0:T(8,128)(2,1)S(1)}, bf16[96,768]{1,0:T(8,128)(2,1)S(1)}, u32[]{:S(2)}, u32[]{:S(2)}) collective-permute-start(bf16[96,768]{1,0:T(8,128)(2,1)S(1)} %slice.21), channel_id=1, source_target_pairs={{0,3},{1,0},{2,1},{3,2},{4,7},{5,4},{6,5},{7,6},{8,11},{9,8},{10,9... | collective-permute-start | bytes 442376 | tf_op jit(solution)/shard_map/ppermute | solution.py:355
  60.7 22.1 %collective-permute-start.4 = (bf16[256,768]{1,0:T(8,128)(2,1)}, bf16[256,768]{1,0:T(8,128)(2,1)S(1)}, u32[]{:S(2)}, u32[]{:S(2)}) collective-permute-start(bf16[256,768]{1,0:T(8,128)(2,1)} %get-tuple-element.20), channel_id=1, source_target_pairs={{0,0},{49,1},{98,2},{147,3},{196,4},{245,5},{294,6},{343,7},{392,8... | collective-permute-start | bytes 1179656 | tf_op jit(solution)/shard_map/ppermute | solution.py:411
  61.4 5.0 %collective-permute-start.5 = (bf16[128,768]{1,0:T(8,128)(2,1)S(1)}, bf16[128,768]{1,0:T(8,128)(2,1)S(1)}, u32[]{:S(2)}, u32[]{:S(2)}) collective-permute-start(bf16[128,768]{1,0:T(8,128)(2,1)S(1)} %get-tuple-element.21.a0_ref), channel_id=1, source_target_pairs={{48,0},{49,1},{50,2},{51,3},{52,4},{53,5},{54,6},{55,7},{56,8},{57... | collective-permute-start | bytes 589832 | tf_op jit(solution)/shard_map/ppermute | solution.py:408
  62.0 10.4 %collective-permute-start.6 = (bf16[128,768]{1,0:T(8,128)(2,1)S(1)}, bf16[128,768]{1,0:T(8,128)(2,1)S(1)}, u32[]{:S(2)}, u32[]{:S(2)}) collective-permute-start(bf16[128,768]{1,0:T(8,128)(2,1)S(1)} %get-tuple-element.21.a0_ref), channel_id=1, source_target_pairs={{96,0},{97,1},{98,2},{99,3},{100,4},{101,5},{102,6},{103,7},{104,8... | collective-permute-start | bytes 589832 | tf_op jit(solution)/shard_map/ppermute | solution.py:408
  83.8 3.1 %collective-permute-start.7 = (bf16[256,768]{1,0:T(8,128)(2,1)S(1)}, bf16[256,768]{1,0:T(8,128)(2,1)S(1)}, u32[]{:S(2)}, u32[]{:S(2)}) collective-permute-start(bf16[256,768]{1,0:T(8,128)(2,1)S(1)} %solve.1), channel_id=1, source_target_pairs={{0,288},{1,289},{2,290},{3,291},{4,292},{5,293},{6,294},{7,295},{8... | collective-permute-start | bytes 1179656 | tf_op jit(solution)/shard_map/ppermute | solution.py:451
  84.5 2.4 %collective-permute-start.8 = (bf16[256,768]{1,0:T(8,128)(2,1)S(1)}, bf16[256,768]{1,0:T(8,128)(2,1)}, u32[]{:S(2)}, u32[]{:S(2)}) collective-permute-start(bf16[256,768]{1,0:T(8,128)(2,1)S(1)} %solve.1), channel_id=1, source_target_pairs={{0,576},{1,577},{2,578},{3,579},{4,580},{5,581},{6,582},{7,583},{8... | collective-permute-start | bytes 1179656 | tf_op jit(solution)/shard_map/ppermute | solution.py:451
  87.0 7.9 %collective-permute-start.10 = (bf16[256,768]{1,0:T(8,128)(2,1)S(1)}, bf16[256,768]{1,0:T(8,128)(2,1)S(1)}, u32[]{:S(2)}, u32[]{:S(2)}) collective-permute-start(bf16[256,768]{1,0:T(8,128)(2,1)S(1)} %select_select_fusion.1), channel_id=1, source_target_pairs={{0,672},{288,192},{576,480},{1,673},{289,193},{577,481},{2,674},{2... | collective-permute-start | bytes 1179656 | tf_op jit(solution)/shard_map/ppermute | solution.py:451
  87.8 15.1 %collective-permute-start.9 = (bf16[256,768]{1,0:T(8,128)(2,1)S(1)}, bf16[256,768]{1,0:T(8,128)(2,1)S(1)}, u32[]{:S(2)}, u32[]{:S(2)}) collective-permute-start(bf16[256,768]{1,0:T(8,128)(2,1)S(1)} %select_select_fusion.1), channel_id=1, source_target_pairs={{0,96},{288,384},{1,97},{289,385},{2,98},{290,386},{3,99},{291,387... | collective-permute-start | bytes 1179656 | tf_op jit(solution)/shard_map/ppermute | solution.py:451
  91.8 11.2 %copy-start.2 = (s32[768,1]{1,0:T(8,128)S(1)}, s32[768,1]{1,0:T(8,128)}, u32[]{:S(2)}) copy-start(s32[768,1]{1,0:T(8,128)} %broadcast_in_dim.6.place_ref) | copy-start | bytes 9220
  92.9 11.7 %collective-permute-start.11 = (bf16[2,128,256]{2,1,0:T(8,128)(2,1)S(1)}, bf16[2,128,256]{2,1,0:T(8,128)(2,1)S(1)}, u32[]{:S(2)}, u32[]{:S(2)}) collective-permute-start(bf16[2,128,256]{2,1,0:T(8,128)(2,1)S(1)} %get-tuple-element.36), channel_id=1, source_target_pairs={{0,48},{1,49},{2,50},{3,51},{4,52},{5,53},{6,54},{7,55},{8,56},{9,... | collective-permute-start | bytes 393224 | tf_op jit(solution)/shard_map/ppermute | solution.py:464
  93.5 12.8 %collective-permute-start.12 = (bf16[2,128,256]{2,1,0:T(8,128)(2,1)S(1)}, bf16[2,128,256]{2,1,0:T(8,128)(2,1)S(1)}, u32[]{:S(2)}, u32[]{:S(2)}) collective-permute-start(bf16[2,128,256]{2,1,0:T(8,128)(2,1)S(1)} %get-tuple-element.35), channel_id=1, source_target_pairs={{0,96},{1,97},{2,98},{3,99},{4,100},{5,101},{6,102},{7,103},{8,104... | collective-permute-start | bytes 393224 | tf_op jit(solution)/shard_map/ppermute | solution.py:464
  106.3 2.6 %collective-permute-start.13 = (bf16[256,768]{1,0:T(8,128)(2,1)S(1)}, bf16[256,768]{1,0:T(8,128)(2,1)S(1)}, u32[]{:S(2)}, u32[]{:S(2)}) collective-permute-start(bf16[256,768]{1,0:T(8,128)(2,1)S(1)} %select_select_fusion.v_ref), channel_id=1, source_target_pairs={{0,48},{96,144},{192,240},{288,336},{384,432},{480,528},{576,624},... | collective-permute-start | bytes 1179656 | tf_op jit(solution)/shard_map/ppermute | solution.py:476
  (17 other events, 48.9 us)

commit v3 on v2

--- a/solution.py
+++ b/solution.py
@@ -89,6 +89,14 @@
         out_ref[receiver] = own_ref[...]
 
 
+def pack_kernel(ham_ref, over_ref, out_ref):
+    band, width = out_ref.shape[1] // 2, out_ref.shape[2]
+    for col in range(out_ref.shape[0]):
+        cols = slice(col * width, (col + 1) * width)
+        out_ref[col, :band] = ham_ref[:, cols]
+        out_ref[col, band:] = over_ref[:, cols]
+
+
 def pick_rows(place, chunks):
     start, total = 0, None
     for chunk in chunks:
@@ -109,14 +117,15 @@
 
 
 def early_kernel(slot_ref, mask_ref, place_ref, *refs):
-    chunks, (own_ref, cross_ref) = refs[:-2], refs[-2:]
-    place = place_ref[0:SN, :]
-    store_masked(own_ref, slice(0, SN), pick_rows(place, chunks), mask_ref, 0)
-    for half in range(cross_ref.shape[0] // SN):
-        slot = slot_ref[half]
-        place = place_ref[pl.ds(pl.multiple_of(slot * SN, SN), SN), :]
-        rows = slice(half * SN, (half + 1) * SN)
-        store_masked(cross_ref, rows, pick_rows(place, chunks), mask_ref, slot)
+    chunks, out_ref = refs[:-1], refs[-1]
+
+    @pl.when(slot_ref[0] >= 0)
+    def _():
+        for block in range(out_ref.shape[0] // SN):
+            slot = slot_ref[block]
+            place = place_ref[pl.ds(pl.multiple_of(slot * SN, SN), SN), :]
+            rows = slice(block * SN, (block + 1) * SN)
+            store_masked(out_ref, rows, pick_rows(place, chunks), mask_ref, slot)
 
 
 def panel_kernel(mask_ref, place_ref, *refs):
@@ -132,17 +141,7 @@
 
 
 def pivot_kernel(
-    shift_ref,
-    which_ref,
-    a0_ref,
-    a1_ref,
-    a2_ref,
-    solve_ref,
-    early_ref,
-    column_ref,
-    factor_ref,
-    rows_ref,
-    sems,
+    shift_ref, which_ref, a0_ref, a1_ref, a2_ref, solve_ref, special_ref, rows_ref, sems
 ):
     z_real, z_imag = shift_ref[0], shift_ref[1]
     my_col = which_ref[0]
@@ -160,79 +159,77 @@
         over = rows_ref[t, :, (STEPS + step) * SN : (STEPS + step + 1) * SN].astype(F32)
         return jnp.concatenate([ham - z_real * over, -z_imag * over], axis=1)
 
+    def stacked(lefts, right, passes=1):
+        product = times(jnp.concatenate(lefts, axis=0), right, passes)
+        return [product[i * SN : (i + 1) * SN] for i in range(len(lefts))]
+
     a = [[block(t, s) for s in range(STEPS)] for t in range(STEPS)]
-    x, f, k = [], {}, {}
-    for t in range(STEPS):
-        x.append(invert_pivot(a[t][t]))
-        if t == STEPS - 1:
-            break
-        below = times(jnp.concatenate([a[i][t] for i in range(t + 1, STEPS)], axis=0), x[t], 3)
-        for s in range(t + 1, STEPS):
-            f[s, t] = below[(s - t - 1) * SN : (s - t) * SN]
-        for s in range(t + 1, STEPS):
-            change = times(below, a[t][s], 3)
-            for i in range(t + 1, STEPS):
-                a[i][s] = a[i][s] - change[(i - t - 1) * SN : (i - t) * SN]
-    k[0, 1] = -times(x[0], a[0][1])
-    k[1, 2] = -times(x[1], a[1][2])
-    k[0, 2] = times(k[0, 1], k[1, 2]) - times(x[0], a[0][2])
-    g = {(t, t): x[t] for t in range(STEPS)}
-    g[1, 0] = -times(x[1], f[1, 0])
-    g[2, 1] = -times(x[2], f[2, 1])
-    g[2, 0] = -times(g[2, 1], f[1, 0]) - times(x[2], f[2, 0])
+    x0 = invert_pivot(a[0][0])
+    f10, f20 = stacked([a[1][0], a[2][0]], x0, 3)
+    change = stacked([f10, f20], a[0][1], 3)
+    a11, a21 = a[1][1] - change[0], a[2][1] - change[1]
+    change = stacked([f10, f20], a[0][2], 3)
+    a12, a22 = a[1][2] - change[0], a[2][2] - change[1]
+    x1 = invert_pivot(a11)
+    f21 = times(a21, x1, 3)
+    x2 = invert_pivot(a22 - times(f21, a12, 3))
+    k01 = -times(x0, a[0][1])
+    k12 = -times(x1, a12)
+    k02 = times(k01, k12) - times(x0, a[0][2])
+    h01 = times(k01, x1)
+    h12, h02 = stacked([k12, k02], x2)
+    by_f10 = stacked([f21, h01, x1], f10)
+    back = by_f10[0] - f20
+    by_back = stacked([h02, x2], back)
+    by_f21 = stacked([h12, h02, x2], f21)
+    m20 = by_back[1]
+    solve = [
+        [x0 - by_f10[1] + by_back[0], h01 - by_f21[1], h02],
+        [times(k12, m20) - by_f10[2], x1 - by_f21[0], h12],
+        [m20, -by_f21[2], x2],
+    ]
     zero = jnp.zeros((SN, 2 * SN), F32)
     half = STEPS * SN
 
-    def store(ref, t, parts, offset, stride):
+    def store(row, stride, parts):
         real = jnp.concatenate([p[:, :SN] for p in parts], axis=1)
         imag = jnp.concatenate([p[:, SN:] for p in parts], axis=1)
-        rows = slice(t * SN, (t + 1) * SN)
-        ref[rows, offset : offset + real.shape[1]] = real.astype(BF16)
-        ref[rows, offset + stride : offset + stride + real.shape[1]] = imag.astype(BF16)
-        rows = slice(half + t * SN, half + (t + 1) * SN)
-        real, imag = for_raw_rows(z_real, z_imag, (real, imag))
-        ref[rows, offset : offset + real.shape[1]] = real.astype(BF16)
-        ref[rows, offset + stride : offset + stride + real.shape[1]] = imag.astype(BF16)
+        over_real, over_imag = for_raw_rows(z_real, z_imag, (real, imag))
+        for offset, ham, over in ((0, real, over_real), (stride, imag, over_imag)):
+            rows = slice(row + offset, row + offset + SN)
+            solve_ref[rows, :half] = ham.astype(BF16)
+            solve_ref[rows, half:] = over.astype(BF16)
 
     for t in range(STEPS):
-        parts = []
-        for s in range(STEPS):
-            total = g[t, s] if s <= t else None
-            for i in range(max(t + 1, s), STEPS):
-                term = times(k[t, i], g[i, s])
-                total = term if total is None else total + term
-            parts.append(total)
-        store(solve_ref, t, parts, 0, half)
-        for i in range(1, STEPS):
-            store(early_ref, t, [-k[t, i] if i > t else zero], (i - 1) * 2 * SN, SN)
+        store(t * SN, half, solve[t])
+    store(2 * half, SN, [f10, zero, zero])
+    store(2 * half + 2 * SN, SN, [-back, f21, zero])
+    upper = [[x0, h01, h02], [zero, x1, h12], [zero, zero, x2]]
     for s in range(STEPS):
-        total = zero
-        for t in range(s, STEPS):
-            total = jnp.where(my_col == t, g[t, s], total)
-        column_ref[:, s * SN : (s + 1) * SN] = total[:, :SN].astype(BF16)
-        column_ref[:, half + s * SN : half + (s + 1) * SN] = total[:, SN:].astype(BF16)
-    factor_ref[0] = f[1, 0]
-    factor_ref[1] = jnp.where(my_col == 0, f[2, 0], f[2, 1])
-
-
-def solve_kernel(which_ref, cross_ref, solve_ref, column_ref, v_ref):
-    v = jnp.dot(cross_ref[...], solve_ref[...], preferred_element_type=F32).astype(BF16)
-    v_ref[SN:] = v[SN:]
-    v_ref[:SN] = jnp.where(which_ref[0] < STEPS, column_ref[...], v[:SN])
-
-
-def pivot_rows_kernel(which_ref, cross_ref, early_ref, factor_ref, u_ref):
+        total = jnp.where(my_col == 0, upper[s][0], upper[s][1])
+        total = jnp.where(my_col == 2, upper[s][2], total)
+        special_ref[s * SN : (s + 1) * SN, :] = total[:, :SN].astype(BF16)
+        special_ref[half + s * SN : half + (s + 1) * SN, :] = total[:, SN:].astype(BF16)
+    for i, total in enumerate((f10, jnp.where(my_col == 0, f20, f21))):
+        row = 2 * half + 2 * i * SN
+        special_ref[row : row + SN, :] = total[:, :SN].astype(BF16)
+        special_ref[row + SN : row + 2 * SN, :] = total[:, SN:].astype(BF16)
+
+
+def solve_kernel(which_ref, cross_ref, solve_ref, special_ref, w_ref, u1_ref, u2_ref):
     my_col = which_ref[0]
-    change = jnp.dot(cross_ref[...], early_ref[...], preferred_element_type=F32)
-    for i in range(STEPS - 1):
-        for part in range(2):
-            cols = slice((2 * i + part) * SN, (2 * i + part + 1) * SN)
-            for half in range(cross_ref.shape[0] // SN):
-                block = change[half * SN : (half + 1) * SN, cols].T
-                if half == 0:
-                    factor = factor_ref[i, :, part * SN : (part + 1) * SN]
-                    block = jnp.where(my_col < i + 1, factor, block)
-                u_ref[i, part, :, half * SN : (half + 1) * SN] = block.astype(BF16)
+    start = 0
+    for out_ref, limit in ((w_ref, STEPS), (u1_ref, 1), (u2_ref, 2)):
+        rows = slice(start, start + out_ref.shape[0])
+        got = lax.dot_general(
+            solve_ref[rows, :],
+            cross_ref[...],
+            (((1,), (1,)), ((), ())),
+            preferred_element_type=F32,
+        ).astype(BF16)
+        out_ref[:, SN:] = got[:, SN:]
+        out_ref[:, :SN] = jnp.where(my_col < limit, special_ref[rows, :], got[:, :SN])
+        start += out_ref.shape[0]
 
 
 def is_factor(which_ref, slot, half):
@@ -263,40 +260,58 @@
 
 
 def update_kernel(
-    shift_ref, which_ref, base_ref, panel_ref, v_ref, v_other_ref, u1_ref, u2_ref, out_ref
+    shift_ref,
+    which_ref,
+    base_ref,
+    panel_ref,
+    w_ref,
+    w_other_ref,
+    u1_ref,
+    u2_ref,
+    out_ref,
+    done_ref,
+    sems,
 ):
     z_real, z_imag = shift_ref[0], shift_ref[1]
     my_row, own = which_ref[1], which_ref[3] > 0
     height, width = out_ref.shape[1], out_ref.shape[2]
-    v = jnp.where(own, v_ref[...], v_other_ref[...])
-    half_depth = v.shape[1] // 2
-    v_real, v_imag = v[:, :half_depth], v[:, half_depth:]
-    m_real, m_imag = for_raw_rows(z_real, z_imag, (v_real.astype(F32), v_imag.astype(F32)))
-    v_all = jnp.concatenate(
+    w = jnp.where(own, w_ref[...], w_other_ref[...])
+    half = w.shape[0] // 2
+    over_real, over_imag = for_raw_rows(
+        z_real, z_imag, (w[:half].astype(F32), w[half:].astype(F32))
+    )
+    w_all = jnp.concatenate(
         [
-            jnp.concatenate([v_real, m_real.astype(BF16)], axis=1),
-            jnp.concatenate([v_imag, m_imag.astype(BF16)], axis=1),
+            jnp.concatenate([w[:half], w[half:]], axis=1),
+            jnp.concatenate([over_real, over_imag], axis=1).astype(BF16),
         ],
         axis=0,
     )
+    copies = []
     for slot in range(height // SN):
         rows = slice(slot * SN, (slot + 1) * SN)
-        change = lax.dot_general(
-            panel_ref[rows, :], v_all, (((1,), (1,)), ((), ())), preferred_element_type=F32
-        )
+        change = jnp.dot(panel_ref[rows, :], w_all, preferred_element_type=F32)
         for part in range(2):
             part_change = change[:, part * width : (part + 1) * width]
             if slot == 0:
-                later = jnp.where(my_row == 1, u1_ref[part].astype(F32), part_change)
-                later = jnp.where(my_row == 2, u2_ref[part].astype(F32), later)
+                block = slice(part * SN, (part + 1) * SN)
+                later = jnp.where(my_row == 1, u1_ref[block, :].astype(F32), part_change)
+                later = jnp.where(my_row == 2, u2_ref[block, :].astype(F32), later)
                 part_change = jnp.where(my_row == 0, 0.0, later)
-            for half in range(width // SN):
-                cols = slice(half * SN, (half + 1) * SN)
-                factor = is_factor(which_ref, slot, half)
+            for piece in range(width // SN):
+                cols = slice(piece * SN, (piece + 1) * SN)
+                factor = is_factor(which_ref, slot, piece)
                 sign = -1.0 if factor is None else jnp.where(factor, 1.0, -1.0)
-                out_ref[part, rows, cols] = (
+                done_ref[part, rows, cols] = (
                     base_ref[part, rows, cols] + part_change[:, cols] * sign
                 )
+            copy = pltpu.make_async_copy(
+                done_ref.at[part, rows], out_ref.at[part, rows], sems.at[slot, part]
+            )
+            copy.start()
+            copies.append(copy)
+    for copy in copies:
+        copy.wait()
 
 
 def structure(parent, node_count):
@@ -323,6 +338,7 @@
     smem = pl.BlockSpec(memory_space=pltpu.SMEM)
     vmem = pl.BlockSpec(memory_space=pltpu.VMEM)
     params = pltpu.CompilerParams(vmem_limit_bytes=20 * 1024 * 1024)
+    full = pltpu.CompilerParams(vmem_limit_bytes=56 * 1024 * 1024)
     both = ("prow", "pcol")
 
     def device(row, col):
@@ -339,17 +355,22 @@
             pltpu.VMEM((band, pieces * SN), BF16),
             pltpu.SemaphoreType.DMA((pieces,)),
         ],
-        compiler_params=params,
+        compiler_params=full,
         name="spread",
     )(hamiltonian, margin)
     along_z = [[z * N_X + x for z in range(N_Z)] for x in range(N_X)]
     held_rows = N_Z * band
     mine = lax.all_to_all(copies, "pcol", 0, 0, axis_index_groups=along_z).reshape(held_rows, -1)
 
-    hamiltonian, margin, mine = lax.optimization_barrier((hamiltonian, margin, mine))
-    packed = jnp.concatenate(
-        [array.reshape(band, grid_cols, width) for array in (hamiltonian, margin)], axis=0
-    )
+    packed = pl.pallas_call(
+        pack_kernel,
+        out_shape=jax.ShapeDtypeStruct((grid_cols, 2 * band, width), BF16),
+        in_specs=[vmem, vmem],
+        out_specs=vmem,
+        compiler_params=full,
+        name="pack",
+    )(hamiltonian, margin)
+    packed, mine = lax.optimization_barrier((packed, mine))
 
     def shift_x(array, by):
         return lax.ppermute(
@@ -360,7 +381,7 @@
     far_first = shift_x(below[: held_rows // 2], 1)
     far_last = shift_x(above[held_rows // 2 :], -1)
     chunks = [mine, above, far_first, far_last, below]
-    main = lax.all_to_all(packed, "pcol", split_axis=1, concat_axis=0, tiled=True)
+    main = lax.all_to_all(packed, "pcol", 0, 0)
     pattern = structure(parent, node_count)
     row_nodes = jnp.arange(row_slots, dtype=jnp.int32) * grid_rows + my_row
     col_nodes = jnp.arange(col_slots, dtype=jnp.int32) * grid_cols + my_col
@@ -383,17 +404,29 @@
     slots = jnp.stack([first_slot, first_slot + grid_cols // grid_rows]).astype(jnp.int32)
 
     depth = 2 * STEPS * SN
-    own_rows, cross_rows = pl.pallas_call(
-        early_kernel,
-        out_shape=(
-            jax.ShapeDtypeStruct((SN, depth), BF16),
-            jax.ShapeDtypeStruct((width, depth), BF16),
-        ),
-        in_specs=[smem, smem, vmem] + [vmem] * len(chunks),
-        out_specs=(vmem,) * 2,
-        compiler_params=params,
-        name="early_rows",
-    )(slots, panel_pattern, panel_place[:, None], *chunks)
+
+    def early_rows(slots, place, cost, name):
+        return pl.pallas_call(
+            early_kernel,
+            out_shape=jax.ShapeDtypeStruct((slots.shape[0] * SN, depth), BF16),
+            in_specs=[smem, smem, vmem] + [vmem] * len(chunks),
+            out_specs=vmem,
+            compiler_params=params,
+            cost_estimate=pl.CostEstimate(
+                flops=cost, bytes_accessed=4 * height * depth, transcendentals=0
+            ),
+            name=name,
+        )(slots, panel_pattern, place, *chunks)
+
+    panel_place = panel_place[:, None]
+    columns = range(grid_cols)
+    own_rows = early_rows(
+        jnp.where(my_row < STEPS, 0, -1)[None].astype(jnp.int32), panel_place, 0, "own_rows"
+    )
+    pivot_rows = [
+        lax.ppermute(own_rows, both, [(device(t, c), device(0, c)) for c in columns])
+        for t in range(1, STEPS)
+    ]
     panel = pl.pallas_call(
         panel_kernel,
         out_shape=jax.ShapeDtypeStruct((height, 2 * STEPS * SN), BF16),
@@ -401,26 +434,25 @@
         out_specs=vmem,
         compiler_params=params,
         name="panel_rows",
-    )(panel_pattern, panel_place[:, None], *chunks)
-
-    columns = range(grid_cols)
-    pivot_rows = [own_rows] + [
-        lax.ppermute(own_rows, both, [(device(t, c), device(0, c)) for c in columns])
-        for t in range(1, STEPS)
-    ]
+    )(panel_pattern, panel_place, *chunks)
+
+    *pivot_rows, panel, later_place = lax.optimization_barrier((*pivot_rows, panel, panel_place))
+    cross_rows = early_rows(
+        jnp.where(my_row == my_col % grid_rows, slots, -1), later_place, 0, "cross_rows"
+    )
     cross_rows = lax.ppermute(
         cross_rows, both, [(device(c % grid_rows, c), device(0, c)) for c in columns]
     )
-    solve, early_solve, column, factor = pl.pallas_call(
+    pivot_rows = [own_rows] + pivot_rows
+    solve_height = depth + 2 * (STEPS - 1) * SN
+    solve, special = pl.pallas_call(
         pivot_kernel,
         out_shape=(
-            jax.ShapeDtypeStruct((depth, depth), BF16),
-            jax.ShapeDtypeStruct((depth, 2 * (STEPS - 1) * SN), BF16),
-            jax.ShapeDtypeStruct((SN, depth), BF16),
-            jax.ShapeDtypeStruct((STEPS - 1, SN, 2 * SN), F32),
+            jax.ShapeDtypeStruct((solve_height, depth), BF16),
+            jax.ShapeDtypeStruct((solve_height, SN), BF16),
         ),
         in_specs=[smem, smem] + [pl.BlockSpec(memory_space=pl.ANY)] * STEPS,
-        out_specs=(vmem,) * 4,
+        out_specs=(vmem,) * 2,
         scratch_shapes=[
             pltpu.VMEM((STEPS, SN, depth), BF16),
             pltpu.SemaphoreType.DMA((STEPS,)),
@@ -428,22 +460,18 @@
         compiler_params=params,
         name="pivots",
     )(pole_shift, which, *pivot_rows)
-    w = pl.pallas_call(
+    w, *u = pl.pallas_call(
         solve_kernel,
-        out_shape=jax.ShapeDtypeStruct((width, depth), BF16),
+        out_shape=(
+            jax.ShapeDtypeStruct((depth, width), BF16),
+            jax.ShapeDtypeStruct((2 * SN, width), BF16),
+            jax.ShapeDtypeStruct((2 * SN, width), BF16),
+        ),
         in_specs=[smem] + [vmem] * 3,
-        out_specs=vmem,
+        out_specs=(vmem,) * 3,
         compiler_params=params,
         name="solve",
-    )(which, cross_rows, solve, column)
-    u = pl.pallas_call(
-        pivot_rows_kernel,
-        out_shape=jax.ShapeDtypeStruct((STEPS - 1, 2, SN, width), BF16),
-        in_specs=[smem] + [vmem] * 3,
-        out_specs=vmem,
-        compiler_params=params,
-        name="pivot_rows",
-    )(which, cross_rows, early_solve, factor)
+    )(which, cross_rows, solve, special)
 
     offset = my_row // 2
 
@@ -457,13 +485,6 @@
     up, down = along_y(w, [(0, 3)]), along_y(w, [(0, 6)])
     w = jnp.where((offset == 3) & same_core, up, jnp.where((offset == 6) & same_core, down, w))
     up, down = along_y(w, [(0, 1), (3, 4)]), along_y(w, [(0, 7), (3, 2), (6, 5)])
-    near = (offset == 1) | (offset == 4)
-    kept = (offset == 0) | (offset == 3) | (offset == 6)
-    w = jnp.where(kept, w, jnp.where(near, up, down))
-    early = [
-        lax.ppermute(u[i - 1], both, [(device(0, c), device(i, c)) for c in columns])
-        for i in range(1, STEPS)
-    ]
     base = pl.pallas_call(
         assemble_kernel,
         out_shape=jax.ShapeDtypeStruct((2, height, width), F32),
@@ -471,8 +492,15 @@
         out_specs=vmem,
         compiler_params=params,
         name="assemble",
-    )(pole_shift, which, local_pattern, place[:, None], main.reshape(grid_cols, 2 * band, width))
-    w, base, panel, early = lax.optimization_barrier((w, base, panel, early))
+    )(pole_shift, which, local_pattern, place[:, None], main)
+    early = [
+        lax.ppermute(u[i - 1], both, [(device(0, c), device(i, c)) for c in columns])
+        for i in range(1, STEPS)
+    ]
+    up, down, early = lax.optimization_barrier((up, down, early))
+    near = (offset == 1) | (offset == 4)
+    kept = (offset == 0) | (offset == 3) | (offset == 6)
+    w = jnp.where(kept, w, jnp.where(near, up, down))
     other = lax.ppermute(
         w,
         both,
@@ -482,7 +510,11 @@
         update_kernel,
         out_shape=jax.ShapeDtypeStruct((2, height, width), F32),
         in_specs=[smem, smem] + [vmem] * 6,
-        out_specs=vmem,
+        out_specs=pl.BlockSpec(memory_space=pl.ANY),
+        scratch_shapes=[
+            pltpu.VMEM((2, height, width), F32),
+            pltpu.SemaphoreType.DMA((row_slots, 2)),
+        ],
         compiler_params=params,
         name="update",
     )(pole_shift, which, base, panel, w, other, *early)

time: 114 us -> 110 us (0.965)
  the two profiles are of different devices: /device:TPU:76 before, /device:TPU:160 now
where the time goes in v3:
time: 110 us; the launch traced here: 109 us
  starting transfers between devices  53.4 us (49%)
  waiting for transfers between devices  29.1 us (26%)
  Pallas kernels  21.3 us (19%)
  other arithmetic  2 us (2%)
  matrix products  1.67 us (2%)
  local copies, waits for them, and re-layouts  1.19 us (1%)
    ppermute x4, waiting for transfers between devices, along_y(): lax.ppermute(array, both, [(device(2 * start, c), device(2 * end, c)) for...  18.4 us
    ppermute x4, starting transfers between devices, shift_x(): lax.ppermute(array, 'pcol', [(c, c - c % N_X + (c % N_X + by) % N_X) for...  14.1 us
    all_to_all x1, starting transfers between devices, body(): lax.all_to_all(copies, 'pcol', 0, 0, axis_index_groups=along_z)  13.9 us
    all_to_all x1, starting transfers between devices, body(): main = lax.all_to_all(packed, 'pcol', 0, 0)  10.1 us
    all_to_all x1, waiting for transfers between devices, body(): lax.all_to_all(copies, 'pcol', 0, 0, axis_index_groups=along_z)  7.55 us
    pallas_call x1, Pallas kernels, body(): pl.pallas_call(pivot_kernel, out_shape=(jax.ShapeDtypeStruct((solve_heigh...  6.33 us
    ppermute x4, starting transfers between devices, along_y(): lax.ppermute(array, both, [(device(2 * start, c), device(2 * end, c)) for...  5.49 us
    ppermute x1, starting transfers between devices, body(): lax.ppermute(cross_rows, both, [(device(c % grid_rows, c), device(0, c))...  4.49 us
  transfers between devices with their start and end apart: 16, of which 4 were waited for; matrix products, arithmetic and copies ran while one was open for 4% of the time, Pallas kernels for 16%

profile of v3, /device:TPU:160, one launch (start us, length us, event | category | flops | bytes accessed | tf_op | source)
XLA Modules:
  0.0 109.0 jit_solution(18599421908698292)
XLA Ops:
  0.0 1.6 %spread.1 = bf16[12,16,768]{2,1,0:T(8,128)(2,1)} custom-call(bf16[16,12288]{1,0:T(8,128)(2,1)} %ham_ref.3, bf16[16,12288]{1,0:T(8,128)(2,1)} %over_ref.3), custom_call_target="tpu_custom_call" | custom-call | tf_op jit(solution)/shard_map/spread/pallas_call | solution.py:349
  1.6 13.9 %all-to-all-start = ((bf16[12,16,768]{2,1,0:T(8,128)(2,1)}), bf16[12,16,768]{2,1,0:T(8,128)(2,1)S(1)}, u32[]{:S(2)}, u32[]{:S(2)}) async-start(bf16[12,16,768]{2,1,0:T(8,128)(2,1)} %spread.1), calls=%async_computation | async-start | bytes 589824 | tf_op jit(solution)/shard_map/all_to_all | solution.py:363
  15.5 2.0 %pack.1 = bf16[48,32,256]{2,1,0:T(8,128)(2,1)} custom-call(bf16[16,12288]{1,0:T(8,128)(2,1)} %ham_ref.3, bf16[16,12288]{1,0:T(8,128)(2,1)} %over_ref.3), custom_call_target="tpu_custom_call" | custom-call | tf_op jit(solution)/shard_map/pack/pallas_call | solution.py:365
  19.6 7.5 %all-to-all-done = bf16[12,16,768]{2,1,0:T(8,128)(2,1)S(1)} async-done(((bf16[12,16,768]{2,1,0:T(8,128)(2,1)}), bf16[12,16,768]{2,1,0:T(8,128)(2,1)S(1)}, u32[]{:S(2)}, u32[]{:S(2)}) %all-to-all-start) | async-done | bytes 294944 | tf_op jit(solution)/shard_map/all_to_all | solution.py:363
  27.2 3.4 %collective-permute-start.1 = (bf16[192,768]{1,0:T(8,128)(2,1)S(1)}, bf16[192,768]{1,0:T(8,128)(2,1)S(1)}, u32[]{:S(2)}, u32[]{:S(2)}) collective-permute-start(bf16[192,768]{1,0:T(8,128)(2,1)S(1)} %bitcast.78), channel_id=1, source_target_pairs={{0,1},{1,2},{2,3},{3,0},{4,5},{5,6},{6,7},{7,4},{8,9},{9,10},{10,1... | collective-permute-start | bytes 884744 | tf_op jit(solution)/shard_map/ppermute | solution.py:376
  30.6 3.7 %collective-permute-start = (bf16[192,768]{1,0:T(8,128)(2,1)S(1)}, bf16[192,768]{1,0:T(8,128)(2,1)S(1)}, u32[]{:S(2)}, u32[]{:S(2)}) collective-permute-start(bf16[192,768]{1,0:T(8,128)(2,1)S(1)} %bitcast.79), channel_id=1, source_target_pairs={{0,3},{1,0},{2,1},{3,2},{4,7},{5,4},{6,5},{7,6},{8,11},{9,8},{10,9... | collective-permute-start | bytes 884744 | tf_op jit(solution)/shard_map/ppermute | solution.py:376
  34.5 10.1 %all-to-all-start.1 = ((bf16[48,32,256]{2,1,0:T(8,128)(2,1)}), bf16[48,32,256]{2,1,0:T(8,128)(2,1)S(1)}, u32[]{:S(2)}, u32[]{:S(2)}) async-start(bf16[48,32,256]{2,1,0:T(8,128)(2,1)} %pack.1), calls=%async_computation.1 | async-start | bytes 1572864 | tf_op jit(solution)/shard_map/all_to_all | solution.py:384
  44.6 3.4 %collective-permute-start.2 = (bf16[96,768]{1,0:T(8,128)(2,1)S(1)}, bf16[96,768]{1,0:T(8,128)(2,1)S(1)}, u32[]{:S(2)}, u32[]{:S(2)}) collective-permute-start(bf16[96,768]{1,0:T(8,128)(2,1)S(1)} %slice.12), channel_id=1, source_target_pairs={{0,1},{1,2},{2,3},{3,0},{4,5},{5,6},{6,7},{7,4},{8,9},{9,10},{10,1... | collective-permute-start | bytes 442376 | tf_op jit(solution)/shard_map/ppermute | solution.py:376
  48.0 3.7 %collective-permute-start.3 = (bf16[96,768]{1,0:T(8,128)(2,1)S(1)}, bf16[96,768]{1,0:T(8,128)(2,1)S(1)}, u32[]{:S(2)}, u32[]{:S(2)}) collective-permute-start(bf16[96,768]{1,0:T(8,128)(2,1)S(1)} %slice.13), channel_id=1, source_target_pairs={{0,3},{1,0},{2,1},{3,2},{4,7},{5,4},{6,5},{7,6},{8,11},{9,8},{10,9... | collective-permute-start | bytes 442376 | tf_op jit(solution)/shard_map/ppermute | solution.py:376
  53.6 2.1 %collective-permute-done.3.refs_3_ = bf16[96,768]{1,0:T(8,128)(2,1)S(1)} collective-permute-done((bf16[96,768]{1,0:T(8,128)(2,1)S(1)}, bf16[96,768]{1,0:T(8,128)(2,1)S(1)}, u32[]{:S(2)}, u32[]{:S(2)}) %collective-permute-start.3) | collective-permute-done | bytes 147488 | tf_op jit(solution)/shard_map/ppermute | solution.py:376
  57.0 1.3 %collective-permute-start.5 = (bf16[128,768]{1,0:T(8,128)(2,1)}, bf16[128,768]{1,0:T(8,128)(2,1)}, u32[]{:S(2)}, u32[]{:S(2)}) collective-permute-start(bf16[128,768]{1,0:T(8,128)(2,1)} %own_rows.1.a0_ref), channel_id=1, source_target_pairs={{96,0},{97,1},{98,2},{99,3},{100,4},{101,5},{102,6},{103,7},{104,8... | collective-permute-start | bytes 589832 | tf_op jit(solution)/shard_map/ppermute | solution.py:427
  58.3 1.3 %collective-permute-start.4 = (bf16[128,768]{1,0:T(8,128)(2,1)}, bf16[128,768]{1,0:T(8,128)(2,1)}, u32[]{:S(2)}, u32[]{:S(2)}) collective-permute-start(bf16[128,768]{1,0:T(8,128)(2,1)} %own_rows.1.a0_ref), channel_id=1, source_target_pairs={{48,0},{49,1},{50,2},{51,3},{52,4},{53,5},{54,6},{55,7},{56,8},{57... | collective-permute-start | bytes 589832 | tf_op jit(solution)/shard_map/ppermute | solution.py:427
  59.7 2.4 %panel_rows.1.panel_ref = bf16[768,768]{1,0:T(8,128)(2,1)S(1)} custom-call(f32[6,3]{1,0:T(8,128)S(1)} %bitcast.84, s32[768,1]{1,0:T(8,128)S(1)} %copy.23.place_ref, bf16[192,768]{1,0:T(8,128)(2,1)S(1)} %bitcast.81, bf16[192,768]{1,0:T(8,128)(2,1)S(1)} %collective-permute-done.refs_1_, bf16[96,768]{1,0:T(8,128)(2,1)S(1)} %collective-permute-done.2.refs_2_, ...), custom_call_target="tpu_custom_call" | custom-call | tf_op jit(solution)/shard_map/panel_rows/pallas_call | solution.py:430
  62.3 2.1 %cross_rows.1 = bf16[256,768]{1,0:T(8,128)(2,1)} custom-call(s32[2]{0:T(128)S(1)} %broadcast_select_fusion.slot_ref, f32[6,3]{1,0:T(8,128)S(1)} %bitcast.85, s32[768,1]{1,0:T(8,128)S(1)} %copy.25.place_ref, bf16[192,768]{1,0:T(8,128)(2,1)S(1)} %bitcast.82, bf16[192,768]{1,0:T(8,128)(2,1)S(1)} %collective-permute-done.refs_1_, ...), custom_call_target="tpu_custom_call" | custom-call | bytes 2359296 | tf_op jit(solution)/shard_map/cross_rows/pallas_call | solution.py:409
  64.4 4.5 %collective-permute-start.6 = (bf16[256,768]{1,0:T(8,128)(2,1)}, bf16[256,768]{1,0:T(8,128)(2,1)S(1)}, u32[]{:S(2)}, u32[]{:S(2)}) collective-permute-start(bf16[256,768]{1,0:T(8,128)(2,1)} %cross_rows.1), channel_id=1, source_target_pairs={{0,0},{49,1},{98,2},{147,3},{196,4},{245,5},{294,6},{343,7},{392,8... | collective-permute-start | bytes 1179656 | tf_op jit(solution)/shard_map/ppermute | solution.py:443
  69.0 6.3 %pivots.1 = (bf16[1280,768]{1,0:T(8,128)(2,1)S(1)}, bf16[1280,128]{1,0:T(8,128)(2,1)S(1)}) custom-call(f32[2]{0:T(128)S(1)} %copy-done, s32[4]{0:T(128)S(1)} %pad_add_fusion.which_ref, bf16[128,768]{1,0:T(8,128)(2,1)} %own_rows.1.a0_ref, bf16[128,768]{1,0:T(8,128)(2,1)} %collective-permute-done.4.a1_ref, bf16[128,768]{1,0:T(8,128)(2,1)} %collective-permute-done.5.a2_ref), custom_call_target="tpu_custom_call" | custom-call | tf_op jit(solution)/shard_map/pivots/pallas_call | solution.py:448
  75.3 1.7 %solve.1 = (bf16[768,256]{1,0:T(8,128)(2,1)S(1)}, bf16[256,256]{1,0:T(8,128)(2,1)}, bf16[256,256]{1,0:T(8,128)(2,1)S(1)}) custom-call(s32[4]{0:T(128)S(1)} %pad_add_fusion.which_ref, bf16[256,768]{1,0:T(8,128)(2,1)S(1)} %collective-permute-done.6.cross_ref, bf16[1280,768]{1,0:T(8,128)(2,1)S(1)} %get-tuple-element.26.solve_ref, ...), custom_call_target="tpu_custom_call" | custom-call | tf_op jit(solution)/shard_map/solve/pallas_call | solution.py:463
  77.1 1.4 %collective-permute-start.8 = (bf16[768,256]{1,0:T(8,128)(2,1)S(1)}, bf16[768,256]{1,0:T(8,128)(2,1)}, u32[]{:S(2)}, u32[]{:S(2)}) collective-permute-start(bf16[768,256]{1,0:T(8,128)(2,1)S(1)} %get-tuple-element.28), channel_id=1, source_target_pairs={{0,576},{1,577},{2,578},{3,579},{4,580},{5,581},{6,582},{7,583},{8... | collective-permute-start | bytes 1179656 | tf_op jit(solution)/shard_map/ppermute | solution.py:479
  78.5 1.4 %collective-permute-start.7 = (bf16[768,256]{1,0:T(8,128)(2,1)S(1)}, bf16[768,256]{1,0:T(8,128)(2,1)}, u32[]{:S(2)}, u32[]{:S(2)}) collective-permute-start(bf16[768,256]{1,0:T(8,128)(2,1)S(1)} %get-tuple-element.28), channel_id=1, source_target_pairs={{0,288},{1,289},{2,290},{3,291},{4,292},{5,293},{6,294},{7,295},{8... | collective-permute-start | bytes 1179656 | tf_op jit(solution)/shard_map/ppermute | solution.py:479
  80.0 1.4 %collective-permute-start.10 = (bf16[768,256]{1,0:T(8,128)(2,1)S(1)}, bf16[768,256]{1,0:T(8,128)(2,1)}, u32[]{:S(2)}, u32[]{:S(2)}) collective-permute-start(bf16[768,256]{1,0:T(8,128)(2,1)S(1)} %select_select_fusion.1), channel_id=1, source_target_pairs={{0,672},{288,192},{576,480},{1,673},{289,193},{577,481},{2,674},{2... | collective-permute-start | bytes 1179656 | tf_op jit(solution)/shard_map/ppermute | solution.py:479
  84.1 18.4 %collective-permute-done.9 = bf16[768,256]{1,0:T(8,128)(2,1)} collective-permute-done((bf16[768,256]{1,0:T(8,128)(2,1)S(1)}, bf16[768,256]{1,0:T(8,128)(2,1)}, u32[]{:S(2)}, u32[]{:S(2)}) %collective-permute-start.9) | collective-permute-done | bytes 393248 | tf_op jit(solution)/shard_map/ppermute | solution.py:479
  103.5 1.3 %collective-permute-start.13 = (bf16[768,256]{1,0:T(8,128)(2,1)S(1)}, bf16[768,256]{1,0:T(8,128)(2,1)S(1)}, u32[]{:S(2)}, u32[]{:S(2)}) collective-permute-start(bf16[768,256]{1,0:T(8,128)(2,1)S(1)} %select_select_fusion.w_ref), channel_id=1, source_target_pairs={{0,48},{96,144},{192,240},{288,336},{384,432},{480,528},{576,624},... | collective-permute-start | bytes 1179656 | tf_op jit(solution)/shard_map/ppermute | solution.py:504
  105.2 1.6 %assemble.1.base_ref = f32[2,768,256]{2,1,0:T(8,128)S(1)} custom-call(f32[2]{0:T(128)S(1)} %copy-done, s32[4]{0:T(128)S(1)} %pad_add_fusion.which_ref, f32[6,2]{1,0:T(8,128)S(1)} %fusion.61.mask_ref, s32[768,1]{1,0:T(8,128)S(1)} %broadcast_in_dim.25.place_ref, bf16[48,32,256]{2,1,0:T(8,128)(2,1)S(1)} %all-to-all-done.1.main_ref), custom_call_target="tpu_custom_call" | custom-call | tf_op jit(solution)/shard_map/assemble/pallas_call | solution.py:488
  106.7 2.3 %update.1 = f32[2,768,256]{2,1,0:T(8,128)} custom-call(f32[2]{0:T(128)S(1)} %copy-done, s32[4]{0:T(128)S(1)} %pad_add_fusion.which_ref, f32[2,768,256]{2,1,0:T(8,128)S(1)} %assemble.1.base_ref, bf16[768,768]{1,0:T(8,128)(2,1)S(1)} %panel_rows.1.panel_ref, bf16[768,256]{1,0:T(8,128)(2,1)S(1)} %select_select_fusion.w_ref, ...), custom_call_target="tpu_custom_call" | custom-call | tf_op jit(solution)/shard_map/update/pallas_call | solution.py:509
  (59 shorter events, 9.9 us)
Async XLA Ops:
  0.0 17.5 %copy-start.1 = (s32[96]{0:T(128)S(1)}, s32[96]{0:T(128)}, u32[]{:S(2)}) copy-start(s32[96]{0:T(128)} %param.9) | copy-start | bytes 1156
  1.6 25.6 %all-to-all-start = ((bf16[12,16,768]{2,1,0:T(8,128)(2,1)}), bf16[12,16,768]{2,1,0:T(8,128)(2,1)S(1)}, u32[]{:S(2)}, u32[]{:S(2)}) async-start(bf16[12,16,768]{2,1,0:T(8,128)(2,1)} %spread.1), calls=%async_computation | async-start | bytes 589824 | tf_op jit(solution)/shard_map/all_to_all | solution.py:363
  18.9 32.8 %copy-start.3 = (s32[768]{0:T(1024)S(1)}, s32[768]{0:T(1024)}, u32[]{:S(2)}) copy-start(s32[768]{0:T(1024)} %param.8) | copy-start | bytes 9220
  27.2 17.4 %collective-permute-start.1 = (bf16[192,768]{1,0:T(8,128)(2,1)S(1)}, bf16[192,768]{1,0:T(8,128)(2,1)S(1)}, u32[]{:S(2)}, u32[]{:S(2)}) collective-permute-start(bf16[192,768]{1,0:T(8,128)(2,1)S(1)} %bitcast.78), channel_id=1, source_target_pairs={{0,1},{1,2},{2,3},{3,0},{4,5},{5,6},{6,7},{7,4},{8,9},{9,10},{10,1... | collective-permute-start | bytes 884744 | tf_op jit(solution)/shard_map/ppermute | solution.py:376
  30.6 17.4 %collective-permute-start = (bf16[192,768]{1,0:T(8,128)(2,1)S(1)}, bf16[192,768]{1,0:T(8,128)(2,1)S(1)}, u32[]{:S(2)}, u32[]{:S(2)}) collective-permute-start(bf16[192,768]{1,0:T(8,128)(2,1)S(1)} %bitcast.79), channel_id=1, source_target_pairs={{0,3},{1,0},{2,1},{3,2},{4,7},{5,4},{6,5},{7,6},{8,11},{9,8},{10,9... | collective-permute-start | bytes 884744 | tf_op jit(solution)/shard_map/ppermute | solution.py:376
  34.5 70.7 %all-to-all-start.1 = ((bf16[48,32,256]{2,1,0:T(8,128)(2,1)}), bf16[48,32,256]{2,1,0:T(8,128)(2,1)S(1)}, u32[]{:S(2)}, u32[]{:S(2)}) async-start(bf16[48,32,256]{2,1,0:T(8,128)(2,1)} %pack.1), calls=%async_computation.1 | async-start | bytes 1572864 | tf_op jit(solution)/shard_map/all_to_all | solution.py:384
  44.6 9.0 %collective-permute-start.2 = (bf16[96,768]{1,0:T(8,128)(2,1)S(1)}, bf16[96,768]{1,0:T(8,128)(2,1)S(1)}, u32[]{:S(2)}, u32[]{:S(2)}) collective-permute-start(bf16[96,768]{1,0:T(8,128)(2,1)S(1)} %slice.12), channel_id=1, source_target_pairs={{0,1},{1,2},{2,3},{3,0},{4,5},{5,6},{6,7},{7,4},{8,9},{9,10},{10,1... | collective-permute-start | bytes 442376 | tf_op jit(solution)/shard_map/ppermute | solution.py:376
  48.0 7.7 %collective-permute-start.3 = (bf16[96,768]{1,0:T(8,128)(2,1)S(1)}, bf16[96,768]{1,0:T(8,128)(2,1)S(1)}, u32[]{:S(2)}, u32[]{:S(2)}) collective-permute-start(bf16[96,768]{1,0:T(8,128)(2,1)S(1)} %slice.13), channel_id=1, source_target_pairs={{0,3},{1,0},{2,1},{3,2},{4,7},{5,4},{6,5},{7,6},{8,11},{9,8},{10,9... | collective-permute-start | bytes 442376 | tf_op jit(solution)/shard_map/ppermute | solution.py:376
  57.0 5.1 %collective-permute-start.5 = (bf16[128,768]{1,0:T(8,128)(2,1)}, bf16[128,768]{1,0:T(8,128)(2,1)}, u32[]{:S(2)}, u32[]{:S(2)}) collective-permute-start(bf16[128,768]{1,0:T(8,128)(2,1)} %own_rows.1.a0_ref), channel_id=1, source_target_pairs={{96,0},{97,1},{98,2},{99,3},{100,4},{101,5},{102,6},{103,7},{104,8... | collective-permute-start | bytes 589832 | tf_op jit(solution)/shard_map/ppermute | solution.py:427
  58.3 3.8 %collective-permute-start.4 = (bf16[128,768]{1,0:T(8,128)(2,1)}, bf16[128,768]{1,0:T(8,128)(2,1)}, u32[]{:S(2)}, u32[]{:S(2)}) collective-permute-start(bf16[128,768]{1,0:T(8,128)(2,1)} %own_rows.1.a0_ref), channel_id=1, source_target_pairs={{48,0},{49,1},{50,2},{51,3},{52,4},{53,5},{54,6},{55,7},{56,8},{57... | collective-permute-start | bytes 589832 | tf_op jit(solution)/shard_map/ppermute | solution.py:427
  62.1 6.9 %copy-start = (f32[2]{0:T(128)S(1)}, f32[2]{0:T(128)}, u32[]{:S(2)}) copy-start(f32[2]{0:T(128)} %shift_ref.5) | copy-start | bytes 28
  64.4 10.9 %collective-permute-start.6 = (bf16[256,768]{1,0:T(8,128)(2,1)}, bf16[256,768]{1,0:T(8,128)(2,1)S(1)}, u32[]{:S(2)}, u32[]{:S(2)}) collective-permute-start(bf16[256,768]{1,0:T(8,128)(2,1)} %cross_rows.1), channel_id=1, source_target_pairs={{0,0},{49,1},{98,2},{147,3},{196,4},{245,5},{294,6},{343,7},{392,8... | collective-permute-start | bytes 1179656 | tf_op jit(solution)/shard_map/ppermute | solution.py:443
  77.1 2.8 %collective-permute-start.8 = (bf16[768,256]{1,0:T(8,128)(2,1)S(1)}, bf16[768,256]{1,0:T(8,128)(2,1)}, u32[]{:S(2)}, u32[]{:S(2)}) collective-permute-start(bf16[768,256]{1,0:T(8,128)(2,1)S(1)} %get-tuple-element.28), channel_id=1, source_target_pairs={{0,576},{1,577},{2,578},{3,579},{4,580},{5,581},{6,582},{7,583},{8... | collective-permute-start | bytes 1179656 | tf_op jit(solution)/shard_map/ppermute | solution.py:479
  78.5 1.4 %collective-permute-start.7 = (bf16[768,256]{1,0:T(8,128)(2,1)S(1)}, bf16[768,256]{1,0:T(8,128)(2,1)}, u32[]{:S(2)}, u32[]{:S(2)}) collective-permute-start(bf16[768,256]{1,0:T(8,128)(2,1)S(1)} %get-tuple-element.28), channel_id=1, source_target_pairs={{0,288},{1,289},{2,290},{3,291},{4,292},{5,293},{6,294},{7,295},{8... | collective-permute-start | bytes 1179656 | tf_op jit(solution)/shard_map/ppermute | solution.py:479
  79.9 24.9 %copy-start.2 = (s32[768]{0:T(1024)S(1)}, s32[768]{0:T(1024)}, u32[]{:S(2)}) copy-start(s32[768]{0:T(1024)} %get-tuple-element.36) | copy-start | bytes 9220
  80.0 4.1 %collective-permute-start.10 = (bf16[768,256]{1,0:T(8,128)(2,1)S(1)}, bf16[768,256]{1,0:T(8,128)(2,1)}, u32[]{:S(2)}, u32[]{:S(2)}) collective-permute-start(bf16[768,256]{1,0:T(8,128)(2,1)S(1)} %select_select_fusion.1), channel_id=1, source_target_pairs={{0,672},{288,192},{576,480},{1,673},{289,193},{577,481},{2,674},{2... | collective-permute-start | bytes 1179656 | tf_op jit(solution)/shard_map/ppermute | solution.py:479
  81.4 21.0 %collective-permute-start.9 = (bf16[768,256]{1,0:T(8,128)(2,1)S(1)}, bf16[768,256]{1,0:T(8,128)(2,1)}, u32[]{:S(2)}, u32[]{:S(2)}) collective-permute-start(bf16[768,256]{1,0:T(8,128)(2,1)S(1)} %select_select_fusion.1), channel_id=1, source_target_pairs={{0,96},{288,384},{1,97},{289,385},{2,98},{290,386},{3,99},{291,387... | collective-permute-start | bytes 1179656 | tf_op jit(solution)/shard_map/ppermute | solution.py:479
  82.7 1.4 %collective-permute-start.11 = (bf16[256,256]{1,0:T(8,128)(2,1)}, bf16[256,256]{1,0:T(8,128)(2,1)S(1)}, u32[]{:S(2)}, u32[]{:S(2)}) collective-permute-start(bf16[256,256]{1,0:T(8,128)(2,1)} %get-tuple-element.29), channel_id=1, source_target_pairs={{0,48},{1,49},{2,50},{3,51},{4,52},{5,53},{6,54},{7,55},{8,56},{9,... | collective-permute-start | bytes 393224 | tf_op jit(solution)/shard_map/ppermute | solution.py:497
  83.3 0.7 collective-permute-start.12
  103.5 3.3 %collective-permute-start.13 = (bf16[768,256]{1,0:T(8,128)(2,1)S(1)}, bf16[768,256]{1,0:T(8,128)(2,1)S(1)}, u32[]{:S(2)}, u32[]{:S(2)}) collective-permute-start(bf16[768,256]{1,0:T(8,128)(2,1)S(1)} %select_select_fusion.w_ref), channel_id=1, source_target_pairs={{0,48},{96,144},{192,240},{288,336},{384,432},{480,528},{576,624},... | collective-permute-start | bytes 1179656 | tf_op jit(solution)/shard_map/ppermute | solution.py:504

commit v4 on v3

--- a/solution.py
+++ b/solution.py
@@ -117,15 +117,27 @@
 
 
 def early_kernel(slot_ref, mask_ref, place_ref, *refs):
-    chunks, out_ref = refs[:-1], refs[-1]
+    chunks, (own_ref, tail1_ref, tail2_ref, cross_ref) = refs[:-4], refs[-4:]
 
     @pl.when(slot_ref[0] >= 0)
     def _():
-        for block in range(out_ref.shape[0] // SN):
-            slot = slot_ref[block]
+        got = pick_rows(place_ref[:SN, :], chunks)
+        store_masked(own_ref, slice(0, SN), got, mask_ref, 0)
+        for first, out_ref in ((1, tail1_ref), (2, tail2_ref)):
+            length = (STEPS - first) * SN
+            for part in range(2):
+                start = (part * STEPS + first) * SN
+                out_ref[:, part * length : (part + 1) * length] = own_ref[
+                    :, start : start + length
+                ]
+
+    @pl.when(slot_ref[1] >= 0)
+    def _():
+        for block in range(cross_ref.shape[0] // SN):
+            slot = slot_ref[1 + block]
             place = place_ref[pl.ds(pl.multiple_of(slot * SN, SN), SN), :]
             rows = slice(block * SN, (block + 1) * SN)
-            store_masked(out_ref, rows, pick_rows(place, chunks), mask_ref, slot)
+            store_masked(cross_ref, rows, pick_rows(place, chunks), mask_ref, slot)
 
 
 def panel_kernel(mask_ref, place_ref, *refs):
@@ -140,42 +152,42 @@
     return z_imag * imag - z_real * real, -z_real * imag - z_imag * real
 
 
-def pivot_kernel(
-    shift_ref, which_ref, a0_ref, a1_ref, a2_ref, solve_ref, special_ref, rows_ref, sems
-):
+def shifted(shift_ref, ref, step, count):
+    ham = ref[:, step * SN : (step + 1) * SN].astype(F32)
+    over = ref[:, (count + step) * SN : (count + step + 1) * SN].astype(F32)
+    return jnp.concatenate([ham - shift_ref[0] * over, -shift_ref[1] * over], axis=1)
+
+
+def flip(block):
+    return jnp.concatenate([block[:, :SN].T, block[:, SN:].T], axis=1)
+
+
+def stacked(lefts, right, passes=1):
+    product = times(jnp.concatenate(lefts, axis=0), right, passes)
+    return [product[i * SN : (i + 1) * SN] for i in range(len(lefts))]
+
+
+def first_pivot_kernel(shift_ref, own_ref, out_ref):
+    a00, a01, a02 = [shifted(shift_ref, own_ref, s, STEPS) for s in range(STEPS)]
+    x0 = invert_pivot(a00)
+    f10, f20 = stacked([flip(a01), flip(a02)], x0, 3)
+    out_ref[0], out_ref[1], out_ref[2] = x0, f10, f20
+    out_ref[3] = times(f10, a01, 3)
+    out_ref[4], out_ref[5] = stacked([f10, f20], a02, 3)
+
+
+def pivot_kernel(shift_ref, which_ref, first_ref, a1_ref, a2_ref, solve_ref, special_ref):
     z_real, z_imag = shift_ref[0], shift_ref[1]
     my_col = which_ref[0]
-    copies = [
-        pltpu.make_async_copy(ref, rows_ref.at[t], sems.at[t])
-        for t, ref in enumerate((a0_ref, a1_ref, a2_ref))
-    ]
-    for copy in copies:
-        copy.start()
-    for copy in copies:
-        copy.wait()
-
-    def block(t, step):
-        ham = rows_ref[t, :, step * SN : (step + 1) * SN].astype(F32)
-        over = rows_ref[t, :, (STEPS + step) * SN : (STEPS + step + 1) * SN].astype(F32)
-        return jnp.concatenate([ham - z_real * over, -z_imag * over], axis=1)
-
-    def stacked(lefts, right, passes=1):
-        product = times(jnp.concatenate(lefts, axis=0), right, passes)
-        return [product[i * SN : (i + 1) * SN] for i in range(len(lefts))]
-
-    a = [[block(t, s) for s in range(STEPS)] for t in range(STEPS)]
-    x0 = invert_pivot(a[0][0])
-    f10, f20 = stacked([a[1][0], a[2][0]], x0, 3)
-    change = stacked([f10, f20], a[0][1], 3)
-    a11, a21 = a[1][1] - change[0], a[2][1] - change[1]
-    change = stacked([f10, f20], a[0][2], 3)
-    a12, a22 = a[1][2] - change[0], a[2][2] - change[1]
+    x0, f10, f20 = first_ref[0], first_ref[1], first_ref[2]
+    a11 = shifted(shift_ref, a1_ref, 0, 2) - first_ref[3]
+    a12 = shifted(shift_ref, a1_ref, 1, 2) - first_ref[4]
+    a22 = shifted(shift_ref, a2_ref, 0, 1) - first_ref[5]
     x1 = invert_pivot(a11)
-    f21 = times(a21, x1, 3)
+    f21 = times(flip(a12), x1, 3)
     x2 = invert_pivot(a22 - times(f21, a12, 3))
-    k01 = -times(x0, a[0][1])
-    k12 = -times(x1, a12)
-    k02 = times(k01, k12) - times(x0, a[0][2])
+    k01, k12 = -flip(f10), -flip(f21)
+    k02 = times(k01, k12) - flip(f20)
     h01 = times(k01, x1)
     h12, h02 = stacked([k12, k02], x2)
     by_f10 = stacked([f21, h01, x1], f10)
@@ -404,29 +416,40 @@
     slots = jnp.stack([first_slot, first_slot + grid_cols // grid_rows]).astype(jnp.int32)
 
     depth = 2 * STEPS * SN
-
-    def early_rows(slots, place, cost, name):
-        return pl.pallas_call(
-            early_kernel,
-            out_shape=jax.ShapeDtypeStruct((slots.shape[0] * SN, depth), BF16),
-            in_specs=[smem, smem, vmem] + [vmem] * len(chunks),
-            out_specs=vmem,
-            compiler_params=params,
-            cost_estimate=pl.CostEstimate(
-                flops=cost, bytes_accessed=4 * height * depth, transcendentals=0
-            ),
-            name=name,
-        )(slots, panel_pattern, place, *chunks)
-
     panel_place = panel_place[:, None]
     columns = range(grid_cols)
-    own_rows = early_rows(
-        jnp.where(my_row < STEPS, 0, -1)[None].astype(jnp.int32), panel_place, 0, "own_rows"
-    )
-    pivot_rows = [
-        lax.ppermute(own_rows, both, [(device(t, c), device(0, c)) for c in columns])
-        for t in range(1, STEPS)
+    wanted = jnp.concatenate(
+        [
+            jnp.where(my_row < STEPS, 0, -1)[None].astype(jnp.int32),
+            jnp.where(my_row == my_col % grid_rows, slots, -1),
+        ]
+    )
+    own_rows, tail1, tail2, cross_rows = pl.pallas_call(
+        early_kernel,
+        out_shape=tuple(
+            jax.ShapeDtypeStruct(shape, BF16)
+            for shape in ((SN, depth), (SN, 4 * SN), (SN, 2 * SN), (width, depth))
+        ),
+        in_specs=[smem, smem, vmem] + [vmem] * len(chunks),
+        out_specs=(vmem,) * 4,
+        compiler_params=params,
+        name="early_rows",
+    )(wanted, panel_pattern, panel_place, *chunks)
+    tails = [
+        lax.ppermute(tail, both, [(device(t, c), device(0, c)) for c in columns])
+        for t, tail in ((1, tail1), (2, tail2))
     ]
+    cross_rows = lax.ppermute(
+        cross_rows, both, [(device(c % grid_rows, c), device(0, c)) for c in columns]
+    )
+    first = pl.pallas_call(
+        first_pivot_kernel,
+        out_shape=jax.ShapeDtypeStruct((6, SN, 2 * SN), F32),
+        in_specs=[smem, vmem],
+        out_specs=vmem,
+        compiler_params=params,
+        name="first_pivot",
+    )(pole_shift, own_rows)
     panel = pl.pallas_call(
         panel_kernel,
         out_shape=jax.ShapeDtypeStruct((height, 2 * STEPS * SN), BF16),
@@ -436,14 +459,7 @@
         name="panel_rows",
     )(panel_pattern, panel_place, *chunks)
 
-    *pivot_rows, panel, later_place = lax.optimization_barrier((*pivot_rows, panel, panel_place))
-    cross_rows = early_rows(
-        jnp.where(my_row == my_col % grid_rows, slots, -1), later_place, 0, "cross_rows"
-    )
-    cross_rows = lax.ppermute(
-        cross_rows, both, [(device(c % grid_rows, c), device(0, c)) for c in columns]
-    )
-    pivot_rows = [own_rows] + pivot_rows
+    *tails, panel, first = lax.optimization_barrier((*tails, panel, first))
     solve_height = depth + 2 * (STEPS - 1) * SN
     solve, special = pl.pallas_call(
         pivot_kernel,
@@ -451,15 +467,11 @@
             jax.ShapeDtypeStruct((solve_height, depth), BF16),
             jax.ShapeDtypeStruct((solve_height, SN), BF16),
         ),
-        in_specs=[smem, smem] + [pl.BlockSpec(memory_space=pl.ANY)] * STEPS,
+        in_specs=[smem, smem] + [vmem] * 3,
         out_specs=(vmem,) * 2,
-        scratch_shapes=[
-            pltpu.VMEM((STEPS, SN, depth), BF16),
-            pltpu.SemaphoreType.DMA((STEPS,)),
-        ],
         compiler_params=params,
         name="pivots",
-    )(pole_shift, which, *pivot_rows)
+    )(pole_shift, which, first, *tails)
     w, *u = pl.pallas_call(
         solve_kernel,
         out_shape=(

time: 110 us -> 104 us (0.945)
  the two profiles are of different devices: /device:TPU:160 before, /device:TPU:8 now
where the time goes in v4:
time: 104 us; the launch traced here: 103 us
  starting transfers between devices  51.4 us (49%)
  waiting for transfers between devices  27.8 us (27%)
  Pallas kernels  19.6 us (19%)
  matrix products  1.67 us (2%)
  other arithmetic  1.5 us (1%)
    all_to_all x1, starting transfers between devices, body(): lax.all_to_all(copies, 'pcol', 0, 0, axis_index_groups=along_z)  15.2 us
    ppermute x4, starting transfers between devices, shift_x(): lax.ppermute(array, 'pcol', [(c, c - c % N_X + (c % N_X + by) % N_X) for...  14.1 us
    all_to_all x1, waiting for transfers between devices, body(): lax.all_to_all(copies, 'pcol', 0, 0, axis_index_groups=along_z)  12.7 us
    ppermute x2, waiting for transfers between devices, body(): lax.ppermute(u[i - 1], both, [(device(0, c), device(i, c)) for c in colum...  11.3 us
    ppermute x2, starting transfers between devices, body(): lax.ppermute(tail, both, [(device(t, c), device(0, c)) for c in columns])  7.48 us
    all_to_all x1, starting transfers between devices, body(): main = lax.all_to_all(packed, 'pcol', 0, 0)  5.15 us
    ppermute x4, starting transfers between devices, along_y(): lax.ppermute(array, both, [(device(2 * start, c), device(2 * end, c)) for...  4.79 us
    pallas_call x1, Pallas kernels, body(): pl.pallas_call(pivot_kernel, out_shape=(jax.ShapeDtypeStruct((solve_heigh...  3.93 us
  transfers between devices with their start and end apart: 16, of which 4 were waited for; matrix products, arithmetic and copies ran while one was open for 4% of the time, Pallas kernels for 15%

profile of v4, /device:TPU:8, one launch (start us, length us, event | category | flops | bytes accessed | tf_op | source)
XLA Modules:
  0.0 103.4 jit_solution(393447137994554210)
XLA Ops:
  0.0 1.6 %spread.1 = bf16[12,16,768]{2,1,0:T(8,128)(2,1)} custom-call(bf16[16,12288]{1,0:T(8,128)(2,1)} %ham_ref.3, bf16[16,12288]{1,0:T(8,128)(2,1)} %over_ref.3), custom_call_target="tpu_custom_call" | custom-call | tf_op jit(solution)/shard_map/spread/pallas_call | solution.py:361
  1.6 15.2 %all-to-all-start = ((bf16[12,16,768]{2,1,0:T(8,128)(2,1)}), bf16[12,16,768]{2,1,0:T(8,128)(2,1)S(1)}, u32[]{:S(2)}, u32[]{:S(2)}) async-start(bf16[12,16,768]{2,1,0:T(8,128)(2,1)} %spread.1), calls=%async_computation | async-start | bytes 589824 | tf_op jit(solution)/shard_map/all_to_all | solution.py:375
  16.8 2.0 %pack.1 = bf16[48,32,256]{2,1,0:T(8,128)(2,1)} custom-call(bf16[16,12288]{1,0:T(8,128)(2,1)} %ham_ref.3, bf16[16,12288]{1,0:T(8,128)(2,1)} %over_ref.3), custom_call_target="tpu_custom_call" | custom-call | tf_op jit(solution)/shard_map/pack/pallas_call | solution.py:377
  21.0 12.7 %all-to-all-done = bf16[12,16,768]{2,1,0:T(8,128)(2,1)S(1)} async-done(((bf16[12,16,768]{2,1,0:T(8,128)(2,1)}), bf16[12,16,768]{2,1,0:T(8,128)(2,1)S(1)}, u32[]{:S(2)}, u32[]{:S(2)}) %all-to-all-start) | async-done | bytes 294944 | tf_op jit(solution)/shard_map/all_to_all | solution.py:375
  33.7 3.4 %collective-permute-start.1 = (bf16[192,768]{1,0:T(8,128)(2,1)S(1)}, bf16[192,768]{1,0:T(8,128)(2,1)S(1)}, u32[]{:S(2)}, u32[]{:S(2)}) collective-permute-start(bf16[192,768]{1,0:T(8,128)(2,1)S(1)} %bitcast.78), channel_id=1, source_target_pairs={{0,1},{1,2},{2,3},{3,0},{4,5},{5,6},{6,7},{7,4},{8,9},{9,10},{10,1... | collective-permute-start | bytes 884744 | tf_op jit(solution)/shard_map/ppermute | solution.py:388
  37.1 3.7 %collective-permute-start = (bf16[192,768]{1,0:T(8,128)(2,1)S(1)}, bf16[192,768]{1,0:T(8,128)(2,1)S(1)}, u32[]{:S(2)}, u32[]{:S(2)}) collective-permute-start(bf16[192,768]{1,0:T(8,128)(2,1)S(1)} %bitcast.79), channel_id=1, source_target_pairs={{0,3},{1,0},{2,1},{3,2},{4,7},{5,4},{6,5},{7,6},{8,11},{9,8},{10,9... | collective-permute-start | bytes 884744 | tf_op jit(solution)/shard_map/ppermute | solution.py:388
  41.0 5.2 %all-to-all-start.1 = ((bf16[48,32,256]{2,1,0:T(8,128)(2,1)}), bf16[48,32,256]{2,1,0:T(8,128)(2,1)S(1)}, u32[]{:S(2)}, u32[]{:S(2)}) async-start(bf16[48,32,256]{2,1,0:T(8,128)(2,1)} %pack.1), calls=%async_computation.1 | async-start | bytes 1572864 | tf_op jit(solution)/shard_map/all_to_all | solution.py:396
  46.2 3.6 %collective-permute-start.2 = (bf16[96,768]{1,0:T(8,128)(2,1)S(1)}, bf16[96,768]{1,0:T(8,128)(2,1)S(1)}, u32[]{:S(2)}, u32[]{:S(2)}) collective-permute-start(bf16[96,768]{1,0:T(8,128)(2,1)S(1)} %slice.12), channel_id=1, source_target_pairs={{0,1},{1,2},{2,3},{3,0},{4,5},{5,6},{6,7},{7,4},{8,9},{9,10},{10,1... | collective-permute-start | bytes 442376 | tf_op jit(solution)/shard_map/ppermute | solution.py:388
  49.8 3.5 %collective-permute-start.3 = (bf16[96,768]{1,0:T(8,128)(2,1)S(1)}, bf16[96,768]{1,0:T(8,128)(2,1)S(1)}, u32[]{:S(2)}, u32[]{:S(2)}) collective-permute-start(bf16[96,768]{1,0:T(8,128)(2,1)S(1)} %slice.13), channel_id=1, source_target_pairs={{0,3},{1,0},{2,1},{3,2},{4,7},{5,4},{6,5},{7,6},{8,11},{9,8},{10,9... | collective-permute-start | bytes 442376 | tf_op jit(solution)/shard_map/ppermute | solution.py:388
  53.6 1.4 %collective-permute-done.2.refs_2_ = bf16[96,768]{1,0:T(8,128)(2,1)S(1)} collective-permute-done((bf16[96,768]{1,0:T(8,128)(2,1)S(1)}, bf16[96,768]{1,0:T(8,128)(2,1)S(1)}, u32[]{:S(2)}, u32[]{:S(2)}) %collective-permute-start.2) | collective-permute-done | bytes 147488 | tf_op jit(solution)/shard_map/ppermute | solution.py:388
  55.1 2.3 %collective-permute-done.3.refs_3_ = bf16[96,768]{1,0:T(8,128)(2,1)S(1)} collective-permute-done((bf16[96,768]{1,0:T(8,128)(2,1)S(1)}, bf16[96,768]{1,0:T(8,128)(2,1)S(1)}, u32[]{:S(2)}, u32[]{:S(2)}) %collective-permute-start.3) | collective-permute-done | bytes 147488 | tf_op jit(solution)/shard_map/ppermute | solution.py:388
  57.4 1.9 %early_rows.1 = (bf16[128,768]{1,0:T(8,128)(2,1)S(1)}, bf16[128,512]{1,0:T(8,128)(2,1)}, bf16[128,256]{1,0:T(8,128)(2,1)}, bf16[256,768]{1,0:T(8,128)(2,1)}) custom-call(s32[3]{0:T(128)S(1)} %pad_add_fusion.1.slot_ref, f32[6,3]{1,0:T(8,128)S(1)} %bitcast.82, s32[768,1]{1,0:T(8,128)S(1)} %broadcast_in_dim.26.place_ref, bf16[192,768]{1,0:T(8,128)(2,1)S(1)} %bitcast.80, ...), custom_call_target="tpu_custom_call" | custom-call | tf_op jit(solution)/shard_map/early_rows/pallas_call | solution.py:427
  59.3 1.4 %collective-permute-start.6 = (bf16[256,768]{1,0:T(8,128)(2,1)}, bf16[256,768]{1,0:T(8,128)(2,1)}, u32[]{:S(2)}, u32[]{:S(2)}) collective-permute-start(bf16[256,768]{1,0:T(8,128)(2,1)} %get-tuple-element.30), channel_id=1, source_target_pairs={{0,0},{49,1},{98,2},{147,3},{196,4},{245,5},{294,6},{343,7},{392,8... | collective-permute-start | bytes 1179656 | tf_op jit(solution)/shard_map/ppermute | solution.py:442
  62.0 6.2 %collective-permute-start.5 = (bf16[128,256]{1,0:T(8,128)(2,1)}, bf16[128,256]{1,0:T(8,128)(2,1)S(1)}, u32[]{:S(2)}, u32[]{:S(2)}) collective-permute-start(bf16[128,256]{1,0:T(8,128)(2,1)} %get-tuple-element.27), channel_id=1, source_target_pairs={{96,0},{97,1},{98,2},{99,3},{100,4},{101,5},{102,6},{103,7},{104,8... | collective-permute-start | bytes 196616 | tf_op jit(solution)/shard_map/ppermute | solution.py:439
  68.3 2.2 %first_pivot.1.first_ref = f32[6,128,256]{2,1,0:T(8,128)S(1)} custom-call(f32[2]{0:T(128)S(1)} %copy-done, bf16[128,768]{1,0:T(8,128)(2,1)S(1)} %get-tuple-element.28.own_ref), custom_call_target="tpu_custom_call" | custom-call | tf_op jit(solution)/shard_map/first_pivot/pallas_call | solution.py:445
  70.5 2.4 %panel_rows.1.panel_ref = bf16[768,768]{1,0:T(8,128)(2,1)S(1)} custom-call(f32[6,3]{1,0:T(8,128)S(1)} %bitcast.83, s32[768,1]{1,0:T(8,128)S(1)} %broadcast_in_dim.26.place_ref, bf16[192,768]{1,0:T(8,128)(2,1)S(1)} %bitcast.81, bf16[192,768]{1,0:T(8,128)(2,1)S(1)} %collective-permute-done.refs_1_, bf16[96,768]{1,0:T(8,128)(2,1)S(1)} %collective-permute-done.2.refs_2_, ...), custom_call_target="tpu_custom_call" | custom-call | tf_op jit(solution)/shard_map/panel_rows/pallas_call | solution.py:453
  72.9 3.9 %pivots.1 = (bf16[1280,768]{1,0:T(8,128)(2,1)S(1)}, bf16[1280,128]{1,0:T(8,128)(2,1)S(1)}) custom-call(f32[2]{0:T(128)S(1)} %copy-done, s32[4]{0:T(128)S(1)} %pad_add_fusion.which_ref, f32[6,128,256]{2,1,0:T(8,128)S(1)} %first_pivot.1.first_ref, bf16[128,512]{1,0:T(8,128)(2,1)} %collective-permute-done.4.a1_ref, ...), custom_call_target="tpu_custom_call" | custom-call | tf_op jit(solution)/shard_map/pivots/pallas_call | solution.py:464
  76.8 1.7 %solve.1 = (bf16[768,256]{1,0:T(8,128)(2,1)S(1)}, bf16[256,256]{1,0:T(8,128)(2,1)S(1)}, bf16[256,256]{1,0:T(8,128)(2,1)S(1)}) custom-call(s32[4]{0:T(128)S(1)} %pad_add_fusion.which_ref, bf16[256,768]{1,0:T(8,128)(2,1)} %collective-permute-done.6.cross_ref, bf16[1280,768]{1,0:T(8,128)(2,1)S(1)} %get-tuple-element.34.solve_ref, ...), custom_call_target="tpu_custom_call" | custom-call | tf_op jit(solution)/shard_map/solve/pallas_call | solution.py:475
  79.2 1.4 %collective-permute-start.8 = (bf16[768,256]{1,0:T(8,128)(2,1)S(1)}, bf16[768,256]{1,0:T(8,128)(2,1)}, u32[]{:S(2)}, u32[]{:S(2)}) collective-permute-start(bf16[768,256]{1,0:T(8,128)(2,1)S(1)} %get-tuple-element.36), channel_id=1, source_target_pairs={{0,576},{1,577},{2,578},{3,579},{4,580},{5,581},{6,582},{7,583},{8... | collective-permute-start | bytes 1179656 | tf_op jit(solution)/shard_map/ppermute | solution.py:491
  80.7 1.4 %collective-permute-start.10 = (bf16[768,256]{1,0:T(8,128)(2,1)S(1)}, bf16[768,256]{1,0:T(8,128)(2,1)}, u32[]{:S(2)}, u32[]{:S(2)}) collective-permute-start(bf16[768,256]{1,0:T(8,128)(2,1)S(1)} %select_select_fusion.1), channel_id=1, source_target_pairs={{0,672},{288,192},{576,480},{1,673},{289,193},{577,481},{2,674},{2... | collective-permute-start | bytes 1179656 | tf_op jit(solution)/shard_map/ppermute | solution.py:491
  85.4 11.3 %collective-permute-done.12.u2_ref = bf16[256,256]{1,0:T(8,128)(2,1)S(1)} collective-permute-done((bf16[256,256]{1,0:T(8,128)(2,1)S(1)}, bf16[256,256]{1,0:T(8,128)(2,1)S(1)}, u32[]{:S(2)}, u32[]{:S(2)}) %collective-permute-start.12) | collective-permute-done | bytes 131104 | tf_op jit(solution)/shard_map/ppermute | solution.py:509
  97.8 1.3 %collective-permute-start.13 = (bf16[768,256]{1,0:T(8,128)(2,1)S(1)}, bf16[768,256]{1,0:T(8,128)(2,1)S(1)}, u32[]{:S(2)}, u32[]{:S(2)}) collective-permute-start(bf16[768,256]{1,0:T(8,128)(2,1)S(1)} %select_select_fusion.w_ref), channel_id=1, source_target_pairs={{0,48},{96,144},{192,240},{288,336},{384,432},{480,528},{576,624},... | collective-permute-start | bytes 1179656 | tf_op jit(solution)/shard_map/ppermute | solution.py:516
  99.5 1.6 %assemble.1.base_ref = f32[2,768,256]{2,1,0:T(8,128)S(1)} custom-call(f32[2]{0:T(128)S(1)} %copy-done, s32[4]{0:T(128)S(1)} %pad_add_fusion.which_ref, f32[6,2]{1,0:T(8,128)S(1)} %fusion.61.mask_ref, s32[768,1]{1,0:T(8,128)S(1)} %broadcast_in_dim.25.place_ref, bf16[48,32,256]{2,1,0:T(8,128)(2,1)S(1)} %all-to-all-done.1.main_ref), custom_call_target="tpu_custom_call" | custom-call | tf_op jit(solution)/shard_map/assemble/pallas_call | solution.py:500
  101.1 2.3 %update.1 = f32[2,768,256]{2,1,0:T(8,128)} custom-call(f32[2]{0:T(128)S(1)} %copy-done, s32[4]{0:T(128)S(1)} %pad_add_fusion.which_ref, f32[2,768,256]{2,1,0:T(8,128)S(1)} %assemble.1.base_ref, bf16[768,768]{1,0:T(8,128)(2,1)S(1)} %panel_rows.1.panel_ref, bf16[768,256]{1,0:T(8,128)(2,1)S(1)} %select_select_fusion.w_ref, ...), custom_call_target="tpu_custom_call" | custom-call | tf_op jit(solution)/shard_map/update/pallas_call | solution.py:521
  (56 shorter events, 9.4 us)
Async XLA Ops:
  0.0 18.8 %copy-start.1 = (s32[96]{0:T(128)S(1)}, s32[96]{0:T(128)}, u32[]{:S(2)}) copy-start(s32[96]{0:T(128)} %param.9) | copy-start | bytes 1156
  1.6 32.1 %all-to-all-start = ((bf16[12,16,768]{2,1,0:T(8,128)(2,1)}), bf16[12,16,768]{2,1,0:T(8,128)(2,1)S(1)}, u32[]{:S(2)}, u32[]{:S(2)}) async-start(bf16[12,16,768]{2,1,0:T(8,128)(2,1)} %spread.1), calls=%async_computation | async-start | bytes 589824 | tf_op jit(solution)/shard_map/all_to_all | solution.py:375
  16.8 4.2 %copy-start.2 = (s32[768]{0:T(1024)S(1)}, s32[768]{0:T(1024)}, u32[]{:S(2)}) copy-start(s32[768]{0:T(1024)} %param.8) | copy-start | bytes 9220
  33.7 12.5 %collective-permute-start.1 = (bf16[192,768]{1,0:T(8,128)(2,1)S(1)}, bf16[192,768]{1,0:T(8,128)(2,1)S(1)}, u32[]{:S(2)}, u32[]{:S(2)}) collective-permute-start(bf16[192,768]{1,0:T(8,128)(2,1)S(1)} %bitcast.78), channel_id=1, source_target_pairs={{0,1},{1,2},{2,3},{3,0},{4,5},{5,6},{6,7},{7,4},{8,9},{9,10},{10,1... | collective-permute-start | bytes 884744 | tf_op jit(solution)/shard_map/ppermute | solution.py:388
  37.1 12.7 %collective-permute-start = (bf16[192,768]{1,0:T(8,128)(2,1)S(1)}, bf16[192,768]{1,0:T(8,128)(2,1)S(1)}, u32[]{:S(2)}, u32[]{:S(2)}) collective-permute-start(bf16[192,768]{1,0:T(8,128)(2,1)S(1)} %bitcast.79), channel_id=1, source_target_pairs={{0,3},{1,0},{2,1},{3,2},{4,7},{5,4},{6,5},{7,6},{8,11},{9,8},{10,9... | collective-permute-start | bytes 884744 | tf_op jit(solution)/shard_map/ppermute | solution.py:388
  41.0 58.5 %all-to-all-start.1 = ((bf16[48,32,256]{2,1,0:T(8,128)(2,1)}), bf16[48,32,256]{2,1,0:T(8,128)(2,1)S(1)}, u32[]{:S(2)}, u32[]{:S(2)}) async-start(bf16[48,32,256]{2,1,0:T(8,128)(2,1)} %pack.1), calls=%async_computation.1 | async-start | bytes 1572864 | tf_op jit(solution)/shard_map/all_to_all | solution.py:396
  46.2 22.1 %copy-start = (f32[2]{0:T(128)S(1)}, f32[2]{0:T(128)}, u32[]{:S(2)}) copy-start(f32[2]{0:T(128)} %shift_ref.7) | copy-start | bytes 28
  46.2 8.9 %collective-permute-start.2 = (bf16[96,768]{1,0:T(8,128)(2,1)S(1)}, bf16[96,768]{1,0:T(8,128)(2,1)S(1)}, u32[]{:S(2)}, u32[]{:S(2)}) collective-permute-start(bf16[96,768]{1,0:T(8,128)(2,1)S(1)} %slice.12), channel_id=1, source_target_pairs={{0,1},{1,2},{2,3},{3,0},{4,5},{5,6},{6,7},{7,4},{8,9},{9,10},{10,1... | collective-permute-start | bytes 442376 | tf_op jit(solution)/shard_map/ppermute | solution.py:388
  49.8 7.6 %collective-permute-start.3 = (bf16[96,768]{1,0:T(8,128)(2,1)S(1)}, bf16[96,768]{1,0:T(8,128)(2,1)S(1)}, u32[]{:S(2)}, u32[]{:S(2)}) collective-permute-start(bf16[96,768]{1,0:T(8,128)(2,1)S(1)} %slice.13), channel_id=1, source_target_pairs={{0,3},{1,0},{2,1},{3,2},{4,7},{5,4},{6,5},{7,6},{8,11},{9,8},{10,9... | collective-permute-start | bytes 442376 | tf_op jit(solution)/shard_map/ppermute | solution.py:388
  59.3 17.5 %collective-permute-start.6 = (bf16[256,768]{1,0:T(8,128)(2,1)}, bf16[256,768]{1,0:T(8,128)(2,1)}, u32[]{:S(2)}, u32[]{:S(2)}) collective-permute-start(bf16[256,768]{1,0:T(8,128)(2,1)} %get-tuple-element.30), channel_id=1, source_target_pairs={{0,0},{49,1},{98,2},{147,3},{196,4},{245,5},{294,6},{343,7},{392,8... | collective-permute-start | bytes 1179656 | tf_op jit(solution)/shard_map/ppermute | solution.py:442
  60.7 12.2 %collective-permute-start.4 = (bf16[128,512]{1,0:T(8,128)(2,1)}, bf16[128,512]{1,0:T(8,128)(2,1)}, u32[]{:S(2)}, u32[]{:S(2)}) collective-permute-start(bf16[128,512]{1,0:T(8,128)(2,1)} %get-tuple-element.26), channel_id=1, source_target_pairs={{48,0},{49,1},{50,2},{51,3},{52,4},{53,5},{54,6},{55,7},{56,8},{57... | collective-permute-start | bytes 393224 | tf_op jit(solution)/shard_map/ppermute | solution.py:439
  62.0 10.8 %collective-permute-start.5 = (bf16[128,256]{1,0:T(8,128)(2,1)}, bf16[128,256]{1,0:T(8,128)(2,1)S(1)}, u32[]{:S(2)}, u32[]{:S(2)}) collective-permute-start(bf16[128,256]{1,0:T(8,128)(2,1)} %get-tuple-element.27), channel_id=1, source_target_pairs={{96,0},{97,1},{98,2},{99,3},{100,4},{101,5},{102,6},{103,7},{104,8... | collective-permute-start | bytes 196616 | tf_op jit(solution)/shard_map/ppermute | solution.py:439
  78.5 2.1 %collective-permute-start.7 = (bf16[768,256]{1,0:T(8,128)(2,1)S(1)}, bf16[768,256]{1,0:T(8,128)(2,1)S(1)}, u32[]{:S(2)}, u32[]{:S(2)}) collective-permute-start(bf16[768,256]{1,0:T(8,128)(2,1)S(1)} %get-tuple-element.36), channel_id=1, source_target_pairs={{0,288},{1,289},{2,290},{3,291},{4,292},{5,293},{6,294},{7,295},{8... | collective-permute-start | bytes 1179656 | tf_op jit(solution)/shard_map/ppermute | solution.py:491
  79.2 1.4 %collective-permute-start.8 = (bf16[768,256]{1,0:T(8,128)(2,1)S(1)}, bf16[768,256]{1,0:T(8,128)(2,1)}, u32[]{:S(2)}, u32[]{:S(2)}) collective-permute-start(bf16[768,256]{1,0:T(8,128)(2,1)S(1)} %get-tuple-element.36), channel_id=1, source_target_pairs={{0,576},{1,577},{2,578},{3,579},{4,580},{5,581},{6,582},{7,583},{8... | collective-permute-start | bytes 1179656 | tf_op jit(solution)/shard_map/ppermute | solution.py:491
  80.7 16.0 %collective-permute-start.10 = (bf16[768,256]{1,0:T(8,128)(2,1)S(1)}, bf16[768,256]{1,0:T(8,128)(2,1)}, u32[]{:S(2)}, u32[]{:S(2)}) collective-permute-start(bf16[768,256]{1,0:T(8,128)(2,1)S(1)} %select_select_fusion.1), channel_id=1, source_target_pairs={{0,672},{288,192},{576,480},{1,673},{289,193},{577,481},{2,674},{2... | collective-permute-start | bytes 1179656 | tf_op jit(solution)/shard_map/ppermute | solution.py:491
  82.1 14.6 %collective-permute-start.9 = (bf16[768,256]{1,0:T(8,128)(2,1)S(1)}, bf16[768,256]{1,0:T(8,128)(2,1)}, u32[]{:S(2)}, u32[]{:S(2)}) collective-permute-start(bf16[768,256]{1,0:T(8,128)(2,1)S(1)} %select_select_fusion.1), channel_id=1, source_target_pairs={{0,96},{288,384},{1,97},{289,385},{2,98},{290,386},{3,99},{291,387... | collective-permute-start | bytes 1179656 | tf_op jit(solution)/shard_map/ppermute | solution.py:491
  83.4 2.0 %collective-permute-start.11 = (bf16[256,256]{1,0:T(8,128)(2,1)S(1)}, bf16[256,256]{1,0:T(8,128)(2,1)S(1)}, u32[]{:S(2)}, u32[]{:S(2)}) collective-permute-start(bf16[256,256]{1,0:T(8,128)(2,1)S(1)} %get-tuple-element.37), channel_id=1, source_target_pairs={{0,48},{1,49},{2,50},{3,51},{4,52},{5,53},{6,54},{7,55},{8,56},{9,... | collective-permute-start | bytes 393224 | tf_op jit(solution)/shard_map/ppermute | solution.py:509
  84.1 12.6 %collective-permute-start.12 = (bf16[256,256]{1,0:T(8,128)(2,1)S(1)}, bf16[256,256]{1,0:T(8,128)(2,1)S(1)}, u32[]{:S(2)}, u32[]{:S(2)}) collective-permute-start(bf16[256,256]{1,0:T(8,128)(2,1)S(1)} %get-tuple-element.38), channel_id=1, source_target_pairs={{0,96},{1,97},{2,98},{3,99},{4,100},{5,101},{6,102},{7,103},{8,104... | collective-permute-start | bytes 393224 | tf_op jit(solution)/shard_map/ppermute | solution.py:509
  97.8 3.2 %collective-permute-start.13 = (bf16[768,256]{1,0:T(8,128)(2,1)S(1)}, bf16[768,256]{1,0:T(8,128)(2,1)S(1)}, u32[]{:S(2)}, u32[]{:S(2)}) collective-permute-start(bf16[768,256]{1,0:T(8,128)(2,1)S(1)} %select_select_fusion.w_ref), channel_id=1, source_target_pairs={{0,48},{96,144},{192,240},{288,336},{384,432},{480,528},{576,624},... | collective-permute-start | bytes 1179656 | tf_op jit(solution)/shard_map/ppermute | solution.py:516

commit v5 on v4

--- a/solution.py
+++ b/solution.py
@@ -470,6 +470,7 @@
         in_specs=[smem, smem] + [vmem] * 3,
         out_specs=(vmem,) * 2,
         compiler_params=params,
+        cost_estimate=pl.CostEstimate(flops=3000000000, bytes_accessed=10**6, transcendentals=0),
         name="pivots",
     )(pole_shift, which, first, *tails)
     w, *u = pl.pallas_call(

time: 104 us -> 103 us (level)
  the two profiles are of different devices: /device:TPU:8 before, /device:TPU:76 now
where the time goes in v5:
time: 103 us; the launch traced here: 102 us
  starting transfers between devices  45.1 us (44%)
  waiting for transfers between devices  33.3 us (32%)
  Pallas kernels  19.1 us (19%)
  matrix products  1.67 us (2%)
  other arithmetic  1.5 us (1%)
    ppermute x2, waiting for transfers between devices, body(): lax.ppermute(u[i - 1], both, [(device(0, c), device(i, c)) for c in colum...  16.6 us
    all_to_all x1, starting transfers between devices, body(): lax.all_to_all(copies, 'pcol', 0, 0, axis_index_groups=along_z)  14.8 us
    all_to_all x1, waiting for transfers between devices, body(): lax.all_to_all(copies, 'pcol', 0, 0, axis_index_groups=along_z)  12.4 us
    ppermute x4, starting transfers between devices, shift_x(): lax.ppermute(array, 'pcol', [(c, c - c % N_X + (c % N_X + by) % N_X) for...  11.7 us
    all_to_all x1, starting transfers between devices, body(): main = lax.all_to_all(packed, 'pcol', 0, 0)  6.26 us
    ppermute x4, starting transfers between devices, along_y(): lax.ppermute(array, both, [(device(2 * start, c), device(2 * end, c)) for...  4.79 us
    ppermute x4, waiting for transfers between devices, shift_x(): lax.ppermute(array, 'pcol', [(c, c - c % N_X + (c % N_X + by) % N_X) for...  4.23 us
    pallas_call x1, Pallas kernels, body(): pl.pallas_call(pivot_kernel, out_shape=(jax.ShapeDtypeStruct((solve_heigh...  3.92 us
  transfers between devices with their start and end apart: 16, of which 4 were waited for; matrix products, arithmetic and copies ran while one was open for 4% of the time, Pallas kernels for 15%

profile of v5, /device:TPU:76, one launch (start us, length us, event | category | flops | bytes accessed | tf_op | source)
XLA Modules:
  0.0 102.2 jit_solution(5507705640373256709)
XLA Ops:
  0.0 1.6 %spread.1 = bf16[12,16,768]{2,1,0:T(8,128)(2,1)} custom-call(bf16[16,12288]{1,0:T(8,128)(2,1)} %ham_ref.3, bf16[16,12288]{1,0:T(8,128)(2,1)} %over_ref.3), custom_call_target="tpu_custom_call" | custom-call | tf_op jit(solution)/shard_map/spread/pallas_call | solution.py:361
  1.6 14.8 %all-to-all-start = ((bf16[12,16,768]{2,1,0:T(8,128)(2,1)}), bf16[12,16,768]{2,1,0:T(8,128)(2,1)S(1)}, u32[]{:S(2)}, u32[]{:S(2)}) async-start(bf16[12,16,768]{2,1,0:T(8,128)(2,1)} %spread.1), calls=%async_computation | async-start | bytes 589824 | tf_op jit(solution)/shard_map/all_to_all | solution.py:375
  16.4 2.1 %pack.1 = bf16[48,32,256]{2,1,0:T(8,128)(2,1)} custom-call(bf16[16,12288]{1,0:T(8,128)(2,1)} %ham_ref.3, bf16[16,12288]{1,0:T(8,128)(2,1)} %over_ref.3), custom_call_target="tpu_custom_call" | custom-call | tf_op jit(solution)/shard_map/pack/pallas_call | solution.py:377
  20.6 12.4 %all-to-all-done = bf16[12,16,768]{2,1,0:T(8,128)(2,1)S(1)} async-done(((bf16[12,16,768]{2,1,0:T(8,128)(2,1)}), bf16[12,16,768]{2,1,0:T(8,128)(2,1)S(1)}, u32[]{:S(2)}, u32[]{:S(2)}) %all-to-all-start) | async-done | bytes 294944 | tf_op jit(solution)/shard_map/all_to_all | solution.py:375
  33.0 3.1 %collective-permute-start.1 = (bf16[192,768]{1,0:T(8,128)(2,1)S(1)}, bf16[192,768]{1,0:T(8,128)(2,1)S(1)}, u32[]{:S(2)}, u32[]{:S(2)}) collective-permute-start(bf16[192,768]{1,0:T(8,128)(2,1)S(1)} %bitcast.78), channel_id=1, source_target_pairs={{0,1},{1,2},{2,3},{3,0},{4,5},{5,6},{6,7},{7,4},{8,9},{9,10},{10,1... | collective-permute-start | bytes 884744 | tf_op jit(solution)/shard_map/ppermute | solution.py:388
  36.2 2.7 %collective-permute-start = (bf16[192,768]{1,0:T(8,128)(2,1)S(1)}, bf16[192,768]{1,0:T(8,128)(2,1)S(1)}, u32[]{:S(2)}, u32[]{:S(2)}) collective-permute-start(bf16[192,768]{1,0:T(8,128)(2,1)S(1)} %bitcast.79), channel_id=1, source_target_pairs={{0,3},{1,0},{2,1},{3,2},{4,7},{5,4},{6,5},{7,6},{8,11},{9,8},{10,9... | collective-permute-start | bytes 884744 | tf_op jit(solution)/shard_map/ppermute | solution.py:388
  39.1 6.3 %all-to-all-start.1 = ((bf16[48,32,256]{2,1,0:T(8,128)(2,1)}), bf16[48,32,256]{2,1,0:T(8,128)(2,1)S(1)}, u32[]{:S(2)}, u32[]{:S(2)}) async-start(bf16[48,32,256]{2,1,0:T(8,128)(2,1)} %pack.1), calls=%async_computation.1 | async-start | bytes 1572864 | tf_op jit(solution)/shard_map/all_to_all | solution.py:396
  45.4 3.1 %collective-permute-start.2 = (bf16[96,768]{1,0:T(8,128)(2,1)S(1)}, bf16[96,768]{1,0:T(8,128)(2,1)S(1)}, u32[]{:S(2)}, u32[]{:S(2)}) collective-permute-start(bf16[96,768]{1,0:T(8,128)(2,1)S(1)} %slice.12), channel_id=1, source_target_pairs={{0,1},{1,2},{2,3},{3,0},{4,5},{5,6},{6,7},{7,4},{8,9},{9,10},{10,1... | collective-permute-start | bytes 442376 | tf_op jit(solution)/shard_map/ppermute | solution.py:388
  48.6 2.8 %collective-permute-start.3 = (bf16[96,768]{1,0:T(8,128)(2,1)S(1)}, bf16[96,768]{1,0:T(8,128)(2,1)S(1)}, u32[]{:S(2)}, u32[]{:S(2)}) collective-permute-start(bf16[96,768]{1,0:T(8,128)(2,1)S(1)} %slice.13), channel_id=1, source_target_pairs={{0,3},{1,0},{2,1},{3,2},{4,7},{5,4},{6,5},{7,6},{8,11},{9,8},{10,9... | collective-permute-start | bytes 442376 | tf_op jit(solution)/shard_map/ppermute | solution.py:388
  51.7 1.8 %collective-permute-done.2.refs_2_ = bf16[96,768]{1,0:T(8,128)(2,1)S(1)} collective-permute-done((bf16[96,768]{1,0:T(8,128)(2,1)S(1)}, bf16[96,768]{1,0:T(8,128)(2,1)S(1)}, u32[]{:S(2)}, u32[]{:S(2)}) %collective-permute-start.2) | collective-permute-done | bytes 147488 | tf_op jit(solution)/shard_map/ppermute | solution.py:388
  53.5 2.4 %collective-permute-done.3.refs_3_ = bf16[96,768]{1,0:T(8,128)(2,1)S(1)} collective-permute-done((bf16[96,768]{1,0:T(8,128)(2,1)S(1)}, bf16[96,768]{1,0:T(8,128)(2,1)S(1)}, u32[]{:S(2)}, u32[]{:S(2)}) %collective-permute-start.3) | collective-permute-done | bytes 147488 | tf_op jit(solution)/shard_map/ppermute | solution.py:388
  55.9 1.9 %early_rows.1 = (bf16[128,768]{1,0:T(8,128)(2,1)S(1)}, bf16[128,512]{1,0:T(8,128)(2,1)}, bf16[128,256]{1,0:T(8,128)(2,1)}, bf16[256,768]{1,0:T(8,128)(2,1)}) custom-call(s32[3]{0:T(128)S(1)} %pad_add_fusion.1.slot_ref, f32[6,3]{1,0:T(8,128)S(1)} %bitcast.82, s32[768,1]{1,0:T(8,128)S(1)} %broadcast_in_dim.26.place_ref, bf16[192,768]{1,0:T(8,128)(2,1)S(1)} %bitcast.80, ...), custom_call_target="tpu_custom_call" | custom-call | tf_op jit(solution)/shard_map/early_rows/pallas_call | solution.py:427
  57.8 1.3 %collective-permute-start.4 = (bf16[128,512]{1,0:T(8,128)(2,1)}, bf16[128,512]{1,0:T(8,128)(2,1)}, u32[]{:S(2)}, u32[]{:S(2)}) collective-permute-start(bf16[128,512]{1,0:T(8,128)(2,1)} %get-tuple-element.26), channel_id=1, source_target_pairs={{48,0},{49,1},{50,2},{51,3},{52,4},{53,5},{54,6},{55,7},{56,8},{57... | collective-permute-start | bytes 393224 | tf_op jit(solution)/shard_map/ppermute | solution.py:439
  59.1 2.3 %collective-permute-start.5 = (bf16[128,256]{1,0:T(8,128)(2,1)}, bf16[128,256]{1,0:T(8,128)(2,1)S(1)}, u32[]{:S(2)}, u32[]{:S(2)}) collective-permute-start(bf16[128,256]{1,0:T(8,128)(2,1)} %get-tuple-element.27), channel_id=1, source_target_pairs={{96,0},{97,1},{98,2},{99,3},{100,4},{101,5},{102,6},{103,7},{104,8... | collective-permute-start | bytes 196616 | tf_op jit(solution)/shard_map/ppermute | solution.py:439
  62.3 2.2 %first_pivot.1.first_ref = f32[6,128,256]{2,1,0:T(8,128)S(1)} custom-call(f32[2]{0:T(128)S(1)} %copy-done, bf16[128,768]{1,0:T(8,128)(2,1)S(1)} %get-tuple-element.28.own_ref), custom_call_target="tpu_custom_call" | custom-call | tf_op jit(solution)/shard_map/first_pivot/pallas_call | solution.py:445
  64.5 2.4 %panel_rows.1.panel_ref = bf16[768,768]{1,0:T(8,128)(2,1)S(1)} custom-call(f32[6,3]{1,0:T(8,128)S(1)} %bitcast.83, s32[768,1]{1,0:T(8,128)S(1)} %broadcast_in_dim.26.place_ref, bf16[192,768]{1,0:T(8,128)(2,1)S(1)} %bitcast.81, bf16[192,768]{1,0:T(8,128)(2,1)S(1)} %collective-permute-done.refs_1_, bf16[96,768]{1,0:T(8,128)(2,1)S(1)} %collective-permute-done.2.refs_2_, ...), custom_call_target="tpu_custom_call" | custom-call | tf_op jit(solution)/shard_map/panel_rows/pallas_call | solution.py:453
  66.8 3.9 %pivots.1 = (bf16[1280,768]{1,0:T(8,128)(2,1)S(1)}, bf16[1280,128]{1,0:T(8,128)(2,1)S(1)}) custom-call(f32[2]{0:T(128)S(1)} %copy-done, s32[4]{0:T(128)S(1)} %pad_add_fusion.which_ref, f32[6,128,256]{2,1,0:T(8,128)S(1)} %first_pivot.1.first_ref, bf16[128,512]{1,0:T(8,128)(2,1)} %collective-permute-done.4.a1_ref, ...), custom_call_target="tpu_custom_call" | custom-call | flops 3000000000 | bytes 1000000 | tf_op jit(solution)/shard_map/pivots/pallas_call | solution.py:464
  72.7 1.4 %collective-permute-start.8 = (bf16[768,256]{1,0:T(8,128)(2,1)S(1)}, bf16[768,256]{1,0:T(8,128)(2,1)}, u32[]{:S(2)}, u32[]{:S(2)}) collective-permute-start(bf16[768,256]{1,0:T(8,128)(2,1)S(1)} %get-tuple-element.36), channel_id=1, source_target_pairs={{0,576},{1,577},{2,578},{3,579},{4,580},{5,581},{6,582},{7,583},{8... | collective-permute-start | bytes 1179656 | tf_op jit(solution)/shard_map/ppermute | solution.py:492
  74.2 1.4 %collective-permute-start.10 = (bf16[768,256]{1,0:T(8,128)(2,1)S(1)}, bf16[768,256]{1,0:T(8,128)(2,1)}, u32[]{:S(2)}, u32[]{:S(2)}) collective-permute-start(bf16[768,256]{1,0:T(8,128)(2,1)S(1)} %select_select_fusion.1), channel_id=1, source_target_pairs={{0,672},{288,192},{576,480},{1,673},{289,193},{577,481},{2,674},{2... | collective-permute-start | bytes 1179656 | tf_op jit(solution)/shard_map/ppermute | solution.py:492
  77.6 1.3 %collective-permute-start.12 = (bf16[256,256]{1,0:T(8,128)(2,1)S(1)}, bf16[256,256]{1,0:T(8,128)(2,1)S(1)}, u32[]{:S(2)}, u32[]{:S(2)}) collective-permute-start(bf16[256,256]{1,0:T(8,128)(2,1)S(1)} %get-tuple-element.38), channel_id=1, source_target_pairs={{0,96},{1,97},{2,98},{3,99},{4,100},{5,101},{6,102},{7,103},{8,104... | collective-permute-start | bytes 393224 | tf_op jit(solution)/shard_map/ppermute | solution.py:510
  78.9 16.6 %collective-permute-done.12.u2_ref = bf16[256,256]{1,0:T(8,128)(2,1)S(1)} collective-permute-done((bf16[256,256]{1,0:T(8,128)(2,1)S(1)}, bf16[256,256]{1,0:T(8,128)(2,1)S(1)}, u32[]{:S(2)}, u32[]{:S(2)}) %collective-permute-start.12) | collective-permute-done | bytes 131104 | tf_op jit(solution)/shard_map/ppermute | solution.py:510
  96.6 1.3 %collective-permute-start.13 = (bf16[768,256]{1,0:T(8,128)(2,1)S(1)}, bf16[768,256]{1,0:T(8,128)(2,1)S(1)}, u32[]{:S(2)}, u32[]{:S(2)}) collective-permute-start(bf16[768,256]{1,0:T(8,128)(2,1)S(1)} %select_select_fusion.w_ref), channel_id=1, source_target_pairs={{0,48},{96,144},{192,240},{288,336},{384,432},{480,528},{576,624},... | collective-permute-start | bytes 1179656 | tf_op jit(solution)/shard_map/ppermute | solution.py:517
  98.3 1.5 %assemble.1.base_ref = f32[2,768,256]{2,1,0:T(8,128)S(1)} custom-call(f32[2]{0:T(128)S(1)} %copy-done, s32[4]{0:T(128)S(1)} %pad_add_fusion.which_ref, f32[6,2]{1,0:T(8,128)S(1)} %fusion.61.mask_ref, s32[768,1]{1,0:T(8,128)S(1)} %broadcast_in_dim.25.place_ref, bf16[48,32,256]{2,1,0:T(8,128)(2,1)S(1)} %all-to-all-done.1.main_ref), custom_call_target="tpu_custom_call" | custom-call | tf_op jit(solution)/shard_map/assemble/pallas_call | solution.py:501
  99.9 2.3 %update.1 = f32[2,768,256]{2,1,0:T(8,128)} custom-call(f32[2]{0:T(128)S(1)} %copy-done, s32[4]{0:T(128)S(1)} %pad_add_fusion.which_ref, f32[2,768,256]{2,1,0:T(8,128)S(1)} %assemble.1.base_ref, bf16[768,768]{1,0:T(8,128)(2,1)S(1)} %panel_rows.1.panel_ref, bf16[768,256]{1,0:T(8,128)(2,1)S(1)} %select_select_fusion.w_ref, ...), custom_call_target="tpu_custom_call" | custom-call | tf_op jit(solution)/shard_map/update/pallas_call | solution.py:522
  (56 shorter events, 8.8 us)
Async XLA Ops:
  0.0 18.4 %copy-start.1 = (s32[96]{0:T(128)S(1)}, s32[96]{0:T(128)}, u32[]{:S(2)}) copy-start(s32[96]{0:T(128)} %param.9) | copy-start | bytes 1156
  1.6 31.5 %all-to-all-start = ((bf16[12,16,768]{2,1,0:T(8,128)(2,1)}), bf16[12,16,768]{2,1,0:T(8,128)(2,1)S(1)}, u32[]{:S(2)}, u32[]{:S(2)}) async-start(bf16[12,16,768]{2,1,0:T(8,128)(2,1)} %spread.1), calls=%async_computation | async-start | bytes 589824 | tf_op jit(solution)/shard_map/all_to_all | solution.py:375
  16.4 4.2 %copy-start.2 = (s32[768]{0:T(1024)S(1)}, s32[768]{0:T(1024)}, u32[]{:S(2)}) copy-start(s32[768]{0:T(1024)} %param.8) | copy-start | bytes 9220
  33.0 12.4 %collective-permute-start.1 = (bf16[192,768]{1,0:T(8,128)(2,1)S(1)}, bf16[192,768]{1,0:T(8,128)(2,1)S(1)}, u32[]{:S(2)}, u32[]{:S(2)}) collective-permute-start(bf16[192,768]{1,0:T(8,128)(2,1)S(1)} %bitcast.78), channel_id=1, source_target_pairs={{0,1},{1,2},{2,3},{3,0},{4,5},{5,6},{6,7},{7,4},{8,9},{9,10},{10,1... | collective-permute-start | bytes 884744 | tf_op jit(solution)/shard_map/ppermute | solution.py:388
  36.2 12.4 %collective-permute-start = (bf16[192,768]{1,0:T(8,128)(2,1)S(1)}, bf16[192,768]{1,0:T(8,128)(2,1)S(1)}, u32[]{:S(2)}, u32[]{:S(2)}) collective-permute-start(bf16[192,768]{1,0:T(8,128)(2,1)S(1)} %bitcast.79), channel_id=1, source_target_pairs={{0,3},{1,0},{2,1},{3,2},{4,7},{5,4},{6,5},{7,6},{8,11},{9,8},{10,9... | collective-permute-start | bytes 884744 | tf_op jit(solution)/shard_map/ppermute | solution.py:388
  39.1 59.2 %all-to-all-start.1 = ((bf16[48,32,256]{2,1,0:T(8,128)(2,1)}), bf16[48,32,256]{2,1,0:T(8,128)(2,1)S(1)}, u32[]{:S(2)}, u32[]{:S(2)}) async-start(bf16[48,32,256]{2,1,0:T(8,128)(2,1)} %pack.1), calls=%async_computation.1 | async-start | bytes 1572864 | tf_op jit(solution)/shard_map/all_to_all | solution.py:396
  45.4 16.9 %copy-start = (f32[2]{0:T(128)S(1)}, f32[2]{0:T(128)}, u32[]{:S(2)}) copy-start(f32[2]{0:T(128)} %shift_ref.7) | copy-start | bytes 28
  45.4 8.0 %collective-permute-start.2 = (bf16[96,768]{1,0:T(8,128)(2,1)S(1)}, bf16[96,768]{1,0:T(8,128)(2,1)S(1)}, u32[]{:S(2)}, u32[]{:S(2)}) collective-permute-start(bf16[96,768]{1,0:T(8,128)(2,1)S(1)} %slice.12), channel_id=1, source_target_pairs={{0,1},{1,2},{2,3},{3,0},{4,5},{5,6},{6,7},{7,4},{8,9},{9,10},{10,1... | collective-permute-start | bytes 442376 | tf_op jit(solution)/shard_map/ppermute | solution.py:388
  48.6 7.3 %collective-permute-start.3 = (bf16[96,768]{1,0:T(8,128)(2,1)S(1)}, bf16[96,768]{1,0:T(8,128)(2,1)S(1)}, u32[]{:S(2)}, u32[]{:S(2)}) collective-permute-start(bf16[96,768]{1,0:T(8,128)(2,1)S(1)} %slice.13), channel_id=1, source_target_pairs={{0,3},{1,0},{2,1},{3,2},{4,7},{5,4},{6,5},{7,6},{8,11},{9,8},{10,9... | collective-permute-start | bytes 442376 | tf_op jit(solution)/shard_map/ppermute | solution.py:388
  57.8 9.0 %collective-permute-start.4 = (bf16[128,512]{1,0:T(8,128)(2,1)}, bf16[128,512]{1,0:T(8,128)(2,1)}, u32[]{:S(2)}, u32[]{:S(2)}) collective-permute-start(bf16[128,512]{1,0:T(8,128)(2,1)} %get-tuple-element.26), channel_id=1, source_target_pairs={{48,0},{49,1},{50,2},{51,3},{52,4},{53,5},{54,6},{55,7},{56,8},{57... | collective-permute-start | bytes 393224 | tf_op jit(solution)/shard_map/ppermute | solution.py:439
  59.1 7.7 %collective-permute-start.5 = (bf16[128,256]{1,0:T(8,128)(2,1)}, bf16[128,256]{1,0:T(8,128)(2,1)S(1)}, u32[]{:S(2)}, u32[]{:S(2)}) collective-permute-start(bf16[128,256]{1,0:T(8,128)(2,1)} %get-tuple-element.27), channel_id=1, source_target_pairs={{96,0},{97,1},{98,2},{99,3},{100,4},{101,5},{102,6},{103,7},{104,8... | collective-permute-start | bytes 196616 | tf_op jit(solution)/shard_map/ppermute | solution.py:439
  61.5 9.3 %collective-permute-start.6 = (bf16[256,768]{1,0:T(8,128)(2,1)}, bf16[256,768]{1,0:T(8,128)(2,1)S(1)}, u32[]{:S(2)}, u32[]{:S(2)}) collective-permute-start(bf16[256,768]{1,0:T(8,128)(2,1)} %get-tuple-element.30), channel_id=1, source_target_pairs={{0,0},{49,1},{98,2},{147,3},{196,4},{245,5},{294,6},{343,7},{392,8... | collective-permute-start | bytes 1179656 | tf_op jit(solution)/shard_map/ppermute | solution.py:442
  72.0 2.1 %collective-permute-start.7 = (bf16[768,256]{1,0:T(8,128)(2,1)S(1)}, bf16[768,256]{1,0:T(8,128)(2,1)S(1)}, u32[]{:S(2)}, u32[]{:S(2)}) collective-permute-start(bf16[768,256]{1,0:T(8,128)(2,1)S(1)} %get-tuple-element.36), channel_id=1, source_target_pairs={{0,288},{1,289},{2,290},{3,291},{4,292},{5,293},{6,294},{7,295},{8... | collective-permute-start | bytes 1179656 | tf_op jit(solution)/shard_map/ppermute | solution.py:492
  72.7 1.4 %collective-permute-start.8 = (bf16[768,256]{1,0:T(8,128)(2,1)S(1)}, bf16[768,256]{1,0:T(8,128)(2,1)}, u32[]{:S(2)}, u32[]{:S(2)}) collective-permute-start(bf16[768,256]{1,0:T(8,128)(2,1)S(1)} %get-tuple-element.36), channel_id=1, source_target_pairs={{0,576},{1,577},{2,578},{3,579},{4,580},{5,581},{6,582},{7,583},{8... | collective-permute-start | bytes 1179656 | tf_op jit(solution)/shard_map/ppermute | solution.py:492
  74.2 21.3 %collective-permute-start.10 = (bf16[768,256]{1,0:T(8,128)(2,1)S(1)}, bf16[768,256]{1,0:T(8,128)(2,1)}, u32[]{:S(2)}, u32[]{:S(2)}) collective-permute-start(bf16[768,256]{1,0:T(8,128)(2,1)S(1)} %select_select_fusion.1), channel_id=1, source_target_pairs={{0,672},{288,192},{576,480},{1,673},{289,193},{577,481},{2,674},{2... | collective-permute-start | bytes 1179656 | tf_op jit(solution)/shard_map/ppermute | solution.py:492
  75.6 19.9 %collective-permute-start.9 = (bf16[768,256]{1,0:T(8,128)(2,1)S(1)}, bf16[768,256]{1,0:T(8,128)(2,1)}, u32[]{:S(2)}, u32[]{:S(2)}) collective-permute-start(bf16[768,256]{1,0:T(8,128)(2,1)S(1)} %select_select_fusion.1), channel_id=1, source_target_pairs={{0,96},{288,384},{1,97},{289,385},{2,98},{290,386},{3,99},{291,387... | collective-permute-start | bytes 1179656 | tf_op jit(solution)/shard_map/ppermute | solution.py:492
  76.9 2.0 %collective-permute-start.11 = (bf16[256,256]{1,0:T(8,128)(2,1)S(1)}, bf16[256,256]{1,0:T(8,128)(2,1)S(1)}, u32[]{:S(2)}, u32[]{:S(2)}) collective-permute-start(bf16[256,256]{1,0:T(8,128)(2,1)S(1)} %get-tuple-element.37), channel_id=1, source_target_pairs={{0,48},{1,49},{2,50},{3,51},{4,52},{5,53},{6,54},{7,55},{8,56},{9,... | collective-permute-start | bytes 393224 | tf_op jit(solution)/shard_map/ppermute | solution.py:510
  77.6 17.9 %collective-permute-start.12 = (bf16[256,256]{1,0:T(8,128)(2,1)S(1)}, bf16[256,256]{1,0:T(8,128)(2,1)S(1)}, u32[]{:S(2)}, u32[]{:S(2)}) collective-permute-start(bf16[256,256]{1,0:T(8,128)(2,1)S(1)} %get-tuple-element.38), channel_id=1, source_target_pairs={{0,96},{1,97},{2,98},{3,99},{4,100},{5,101},{6,102},{7,103},{8,104... | collective-permute-start | bytes 393224 | tf_op jit(solution)/shard_map/ppermute | solution.py:510
  96.6 3.2 %collective-permute-start.13 = (bf16[768,256]{1,0:T(8,128)(2,1)S(1)}, bf16[768,256]{1,0:T(8,128)(2,1)S(1)}, u32[]{:S(2)}, u32[]{:S(2)}) collective-permute-start(bf16[768,256]{1,0:T(8,128)(2,1)S(1)} %select_select_fusion.w_ref), channel_id=1, source_target_pairs={{0,48},{96,144},{192,240},{288,336},{384,432},{480,528},{576,624},... | collective-permute-start | bytes 1179656 | tf_op jit(solution)/shard_map/ppermute | solution.py:517

commit v6 on v5

--- a/solution.py
+++ b/solution.py
@@ -271,6 +271,16 @@
             out_ref[1, rows, cols] = imag[:, cols] * keep
 
 
+def pick_kernel(which_ref, first_ref, second_ref, third_ref, out_ref, sem):
+    for index, ref in enumerate((first_ref, second_ref, third_ref)):
+
+        @pl.when(which_ref[0] == index)
+        def _():
+            copy = pltpu.make_async_copy(ref, out_ref, sem)
+            copy.start()
+            copy.wait()
+
+
 def update_kernel(
     shift_ref,
     which_ref,
@@ -488,6 +498,19 @@
 
     offset = my_row // 2
 
+    anywhere = pl.BlockSpec(memory_space=pl.ANY)
+
+    def pick(index, *arrays):
+        return pl.pallas_call(
+            pick_kernel,
+            out_shape=jax.ShapeDtypeStruct(arrays[0].shape, arrays[0].dtype),
+            in_specs=[smem] + [anywhere] * 3,
+            out_specs=vmem,
+            scratch_shapes=[pltpu.SemaphoreType.DMA],
+            compiler_params=params,
+            name="pick",
+        )(index.astype(jnp.int32)[None], *arrays)
+
     def along_y(array, hops):
         return lax.ppermute(
             array,
@@ -496,7 +519,7 @@
         )
 
     up, down = along_y(w, [(0, 3)]), along_y(w, [(0, 6)])
-    w = jnp.where((offset == 3) & same_core, up, jnp.where((offset == 6) & same_core, down, w))
+    w = pick(jnp.where(same_core, jnp.where(offset == 3, 1, jnp.where(offset == 6, 2, 0)), 0), w, up, down)
     up, down = along_y(w, [(0, 1), (3, 4)]), along_y(w, [(0, 7), (3, 2), (6, 5)])
     base = pl.pallas_call(
         assemble_kernel,

time: 103 us -> 103 us (level)
  starting transfers between devices: 45.1 us -> 43.7 us
    ppermute x4, starting transfers between devices: 4.79 us -> 3.34 us  [along_y(): lax.ppermute(array, both, [(device(2 * start, c), device(2 * end, c)) for...]
  transfers between devices with their start and end apart: 16 -> 16, of which waited for: 4 -> 4; matrix products, arithmetic and copies ran while one was open for 4% -> 4% of each run, Pallas kernels for 15% -> 16%
where the time goes in v6:
time: 103 us; the launch traced here: 102 us
  starting transfers between devices  43.7 us (42%)
  waiting for transfers between devices  34 us (33%)
  Pallas kernels  20 us (19%)
  matrix products  1.67 us (2%)
  other arithmetic  1.45 us (1%)
    ppermute x2, waiting for transfers between devices, body(): lax.ppermute(u[i - 1], both, [(device(0, c), device(i, c)) for c in colum...  17.3 us
    all_to_all x1, starting transfers between devices, body(): lax.all_to_all(copies, 'pcol', 0, 0, axis_index_groups=along_z)  14.8 us
    all_to_all x1, waiting for transfers between devices, body(): lax.all_to_all(copies, 'pcol', 0, 0, axis_index_groups=along_z)  12.5 us
    ppermute x4, starting transfers between devices, shift_x(): lax.ppermute(array, 'pcol', [(c, c - c % N_X + (c % N_X + by) % N_X) for...  11.7 us
    all_to_all x1, starting transfers between devices, body(): main = lax.all_to_all(packed, 'pcol', 0, 0)  6.26 us
    ppermute x4, waiting for transfers between devices, shift_x(): lax.ppermute(array, 'pcol', [(c, c - c % N_X + (c % N_X + by) % N_X) for...  4.22 us
    pallas_call x1, Pallas kernels, body(): pl.pallas_call(pivot_kernel, out_shape=(jax.ShapeDtypeStruct((solve_heigh...  3.92 us
    ppermute x2, starting transfers between devices, body(): lax.ppermute(tail, both, [(device(t, c), device(0, c)) for c in columns])  3.66 us
  transfers between devices with their start and end apart: 16, of which 4 were waited for; matrix products, arithmetic and copies ran while one was open for 4% of the time, Pallas kernels for 16%

profile of v6, /device:TPU:76, one launch (start us, length us, event | category | flops | bytes accessed | tf_op | source)
XLA Modules:
  0.0 102.3 jit_solution(14380330440969131365)
XLA Ops:
  0.0 1.6 %spread.1 = bf16[12,16,768]{2,1,0:T(8,128)(2,1)} custom-call(bf16[16,12288]{1,0:T(8,128)(2,1)} %ham_ref.3, bf16[16,12288]{1,0:T(8,128)(2,1)} %over_ref.3), custom_call_target="tpu_custom_call" | custom-call | tf_op jit(solution)/shard_map/spread/pallas_call | solution.py:371
  1.6 14.8 %all-to-all-start = ((bf16[12,16,768]{2,1,0:T(8,128)(2,1)}), bf16[12,16,768]{2,1,0:T(8,128)(2,1)S(1)}, u32[]{:S(2)}, u32[]{:S(2)}) async-start(bf16[12,16,768]{2,1,0:T(8,128)(2,1)} %spread.1), calls=%async_computation | async-start | bytes 589824 | tf_op jit(solution)/shard_map/all_to_all | solution.py:385
  17.9 2.0 %pack.1 = bf16[48,32,256]{2,1,0:T(8,128)(2,1)} custom-call(bf16[16,12288]{1,0:T(8,128)(2,1)} %ham_ref.3, bf16[16,12288]{1,0:T(8,128)(2,1)} %over_ref.3), custom_call_target="tpu_custom_call" | custom-call | tf_op jit(solution)/shard_map/pack/pallas_call | solution.py:387
  20.5 12.5 %all-to-all-done = bf16[12,16,768]{2,1,0:T(8,128)(2,1)S(1)} async-done(((bf16[12,16,768]{2,1,0:T(8,128)(2,1)}), bf16[12,16,768]{2,1,0:T(8,128)(2,1)S(1)}, u32[]{:S(2)}, u32[]{:S(2)}) %all-to-all-start) | async-done | bytes 294944 | tf_op jit(solution)/shard_map/all_to_all | solution.py:385
  33.0 3.1 %collective-permute-start.1 = (bf16[192,768]{1,0:T(8,128)(2,1)S(1)}, bf16[192,768]{1,0:T(8,128)(2,1)S(1)}, u32[]{:S(2)}, u32[]{:S(2)}) collective-permute-start(bf16[192,768]{1,0:T(8,128)(2,1)S(1)} %bitcast.79), channel_id=1, source_target_pairs={{0,1},{1,2},{2,3},{3,0},{4,5},{5,6},{6,7},{7,4},{8,9},{9,10},{10,1... | collective-permute-start | bytes 884744 | tf_op jit(solution)/shard_map/ppermute | solution.py:398
  36.2 2.7 %collective-permute-start = (bf16[192,768]{1,0:T(8,128)(2,1)S(1)}, bf16[192,768]{1,0:T(8,128)(2,1)S(1)}, u32[]{:S(2)}, u32[]{:S(2)}) collective-permute-start(bf16[192,768]{1,0:T(8,128)(2,1)S(1)} %bitcast.80), channel_id=1, source_target_pairs={{0,3},{1,0},{2,1},{3,2},{4,7},{5,4},{6,5},{7,6},{8,11},{9,8},{10,9... | collective-permute-start | bytes 884744 | tf_op jit(solution)/shard_map/ppermute | solution.py:398
  38.9 6.3 %all-to-all-start.1 = ((bf16[48,32,256]{2,1,0:T(8,128)(2,1)}), bf16[48,32,256]{2,1,0:T(8,128)(2,1)S(1)}, u32[]{:S(2)}, u32[]{:S(2)}) async-start(bf16[48,32,256]{2,1,0:T(8,128)(2,1)} %pack.1), calls=%async_computation.1 | async-start | bytes 1572864 | tf_op jit(solution)/shard_map/all_to_all | solution.py:406
  45.5 3.1 %collective-permute-start.2 = (bf16[96,768]{1,0:T(8,128)(2,1)S(1)}, bf16[96,768]{1,0:T(8,128)(2,1)S(1)}, u32[]{:S(2)}, u32[]{:S(2)}) collective-permute-start(bf16[96,768]{1,0:T(8,128)(2,1)S(1)} %slice.12), channel_id=1, source_target_pairs={{0,1},{1,2},{2,3},{3,0},{4,5},{5,6},{6,7},{7,4},{8,9},{9,10},{10,1... | collective-permute-start | bytes 442376 | tf_op jit(solution)/shard_map/ppermute | solution.py:398
  48.6 2.8 %collective-permute-start.3 = (bf16[96,768]{1,0:T(8,128)(2,1)S(1)}, bf16[96,768]{1,0:T(8,128)(2,1)S(1)}, u32[]{:S(2)}, u32[]{:S(2)}) collective-permute-start(bf16[96,768]{1,0:T(8,128)(2,1)S(1)} %slice.13), channel_id=1, source_target_pairs={{0,3},{1,0},{2,1},{3,2},{4,7},{5,4},{6,5},{7,6},{8,11},{9,8},{10,9... | collective-permute-start | bytes 442376 | tf_op jit(solution)/shard_map/ppermute | solution.py:398
  51.7 1.6 %collective-permute-done.2.refs_2_ = bf16[96,768]{1,0:T(8,128)(2,1)S(1)} collective-permute-done((bf16[96,768]{1,0:T(8,128)(2,1)S(1)}, bf16[96,768]{1,0:T(8,128)(2,1)S(1)}, u32[]{:S(2)}, u32[]{:S(2)}) %collective-permute-start.2) | collective-permute-done | bytes 147488 | tf_op jit(solution)/shard_map/ppermute | solution.py:398
  53.3 2.6 %collective-permute-done.3.refs_3_ = bf16[96,768]{1,0:T(8,128)(2,1)S(1)} collective-permute-done((bf16[96,768]{1,0:T(8,128)(2,1)S(1)}, bf16[96,768]{1,0:T(8,128)(2,1)S(1)}, u32[]{:S(2)}, u32[]{:S(2)}) %collective-permute-start.3) | collective-permute-done | bytes 147488 | tf_op jit(solution)/shard_map/ppermute | solution.py:398
  55.9 1.9 %early_rows.1 = (bf16[128,768]{1,0:T(8,128)(2,1)S(1)}, bf16[128,512]{1,0:T(8,128)(2,1)}, bf16[128,256]{1,0:T(8,128)(2,1)}, bf16[256,768]{1,0:T(8,128)(2,1)}) custom-call(s32[3]{0:T(128)S(1)} %pad_add_fusion.1.slot_ref, f32[6,3]{1,0:T(8,128)S(1)} %bitcast.83, s32[768,1]{1,0:T(8,128)S(1)} %broadcast_in_dim.30.place_ref, bf16[192,768]{1,0:T(8,128)(2,1)S(1)} %bitcast.81, ...), custom_call_target="tpu_custom_call" | custom-call | tf_op jit(solution)/shard_map/early_rows/pallas_call | solution.py:437
  57.8 1.3 %collective-permute-start.4 = (bf16[128,512]{1,0:T(8,128)(2,1)}, bf16[128,512]{1,0:T(8,128)(2,1)}, u32[]{:S(2)}, u32[]{:S(2)}) collective-permute-start(bf16[128,512]{1,0:T(8,128)(2,1)} %get-tuple-element.26), channel_id=1, source_target_pairs={{48,0},{49,1},{50,2},{51,3},{52,4},{53,5},{54,6},{55,7},{56,8},{57... | collective-permute-start | bytes 393224 | tf_op jit(solution)/shard_map/ppermute | solution.py:449
  59.2 2.3 %collective-permute-start.5 = (bf16[128,256]{1,0:T(8,128)(2,1)}, bf16[128,256]{1,0:T(8,128)(2,1)S(1)}, u32[]{:S(2)}, u32[]{:S(2)}) collective-permute-start(bf16[128,256]{1,0:T(8,128)(2,1)} %get-tuple-element.27), channel_id=1, source_target_pairs={{96,0},{97,1},{98,2},{99,3},{100,4},{101,5},{102,6},{103,7},{104,8... | collective-permute-start | bytes 196616 | tf_op jit(solution)/shard_map/ppermute | solution.py:449
  62.3 2.2 %first_pivot.1.first_ref = f32[6,128,256]{2,1,0:T(8,128)S(1)} custom-call(f32[2]{0:T(128)S(1)} %copy-done, bf16[128,768]{1,0:T(8,128)(2,1)S(1)} %get-tuple-element.28.own_ref), custom_call_target="tpu_custom_call" | custom-call | tf_op jit(solution)/shard_map/first_pivot/pallas_call | solution.py:455
  64.5 2.4 %panel_rows.1.panel_ref = bf16[768,768]{1,0:T(8,128)(2,1)S(1)} custom-call(f32[6,3]{1,0:T(8,128)S(1)} %bitcast.84, s32[768,1]{1,0:T(8,128)S(1)} %broadcast_in_dim.30.place_ref, bf16[192,768]{1,0:T(8,128)(2,1)S(1)} %bitcast.82, bf16[192,768]{1,0:T(8,128)(2,1)S(1)} %collective-permute-done.refs_1_, bf16[96,768]{1,0:T(8,128)(2,1)S(1)} %collective-permute-done.2.refs_2_, ...), custom_call_target="tpu_custom_call" | custom-call | tf_op jit(solution)/shard_map/panel_rows/pallas_call | solution.py:463
  66.9 3.9 %pivots.1 = (bf16[1280,768]{1,0:T(8,128)(2,1)S(1)}, bf16[1280,128]{1,0:T(8,128)(2,1)S(1)}) custom-call(f32[2]{0:T(128)S(1)} %copy-done, s32[4]{0:T(128)S(1)} %pad_add_fusion.which_ref, f32[6,128,256]{2,1,0:T(8,128)S(1)} %first_pivot.1.first_ref, bf16[128,512]{1,0:T(8,128)(2,1)} %collective-permute-done.4.a1_ref, ...), custom_call_target="tpu_custom_call" | custom-call | flops 3000000000 | bytes 1000000 | tf_op jit(solution)/shard_map/pivots/pallas_call | solution.py:474
  70.8 1.9 %solve.1 = (bf16[768,256]{1,0:T(8,128)(2,1)S(1)}, bf16[256,256]{1,0:T(8,128)(2,1)}, bf16[256,256]{1,0:T(8,128)(2,1)}) custom-call(s32[4]{0:T(128)S(1)} %pad_add_fusion.which_ref, bf16[256,768]{1,0:T(8,128)(2,1)S(1)} %collective-permute-done.6.cross_ref, bf16[1280,768]{1,0:T(8,128)(2,1)S(1)} %get-tuple-element.34.solve_ref, ...), custom_call_target="tpu_custom_call" | custom-call | tf_op jit(solution)/shard_map/solve/pallas_call | solution.py:486
  75.1 1.3 %collective-permute-start.9 = (bf16[768,256]{1,0:T(8,128)(2,1)S(1)}, bf16[768,256]{1,0:T(8,128)(2,1)}, u32[]{:S(2)}, u32[]{:S(2)}) collective-permute-start(bf16[768,256]{1,0:T(8,128)(2,1)S(1)} %pick.1), channel_id=1, source_target_pairs={{0,96},{288,384},{1,97},{289,385},{2,98},{290,386},{3,99},{291,387... | collective-permute-start | bytes 1179656 | tf_op jit(solution)/shard_map/ppermute | solution.py:515
  77.0 1.3 %collective-permute-start.12 = (bf16[256,256]{1,0:T(8,128)(2,1)}, bf16[256,256]{1,0:T(8,128)(2,1)S(1)}, u32[]{:S(2)}, u32[]{:S(2)}) collective-permute-start(bf16[256,256]{1,0:T(8,128)(2,1)} %get-tuple-element.38), channel_id=1, source_target_pairs={{0,96},{1,97},{2,98},{3,99},{4,100},{5,101},{6,102},{7,103},{8,104... | collective-permute-start | bytes 393224 | tf_op jit(solution)/shard_map/ppermute | solution.py:533
  78.4 17.3 %collective-permute-done.12.u2_ref = bf16[256,256]{1,0:T(8,128)(2,1)S(1)} collective-permute-done((bf16[256,256]{1,0:T(8,128)(2,1)}, bf16[256,256]{1,0:T(8,128)(2,1)S(1)}, u32[]{:S(2)}, u32[]{:S(2)}) %collective-permute-start.12) | collective-permute-done | bytes 131104 | tf_op jit(solution)/shard_map/ppermute | solution.py:533
  96.7 1.3 %collective-permute-start.13 = (bf16[768,256]{1,0:T(8,128)(2,1)S(1)}, bf16[768,256]{1,0:T(8,128)(2,1)S(1)}, u32[]{:S(2)}, u32[]{:S(2)}) collective-permute-start(bf16[768,256]{1,0:T(8,128)(2,1)S(1)} %select_select_fusion.w_ref), channel_id=1, source_target_pairs={{0,48},{96,144},{192,240},{288,336},{384,432},{480,528},{576,624},... | collective-permute-start | bytes 1179656 | tf_op jit(solution)/shard_map/ppermute | solution.py:540
  98.4 1.6 %assemble.1.base_ref = f32[2,768,256]{2,1,0:T(8,128)S(1)} custom-call(f32[2]{0:T(128)S(1)} %copy-done, s32[4]{0:T(128)S(1)} %pad_add_fusion.which_ref, f32[6,2]{1,0:T(8,128)S(1)} %fusion.61.mask_ref, s32[768,1]{1,0:T(8,128)S(1)} %broadcast_in_dim.29.place_ref, bf16[48,32,256]{2,1,0:T(8,128)(2,1)S(1)} %all-to-all-done.1.main_ref), custom_call_target="tpu_custom_call" | custom-call | tf_op jit(solution)/shard_map/assemble/pallas_call | solution.py:524
  100.0 2.3 %update.1 = f32[2,768,256]{2,1,0:T(8,128)} custom-call(f32[2]{0:T(128)S(1)} %copy-done, s32[4]{0:T(128)S(1)} %pad_add_fusion.which_ref, f32[2,768,256]{2,1,0:T(8,128)S(1)} %assemble.1.base_ref, bf16[768,768]{1,0:T(8,128)(2,1)S(1)} %panel_rows.1.panel_ref, bf16[768,256]{1,0:T(8,128)(2,1)S(1)} %select_select_fusion.w_ref, ...), custom_call_target="tpu_custom_call" | custom-call | tf_op jit(solution)/shard_map/update/pallas_call | solution.py:545
  (56 shorter events, 7.7 us)
Async XLA Ops:
  0.0 16.4 %copy-start.1 = (s32[96]{0:T(128)S(1)}, s32[96]{0:T(128)}, u32[]{:S(2)}) copy-start(s32[96]{0:T(128)} %param.9) | copy-start | bytes 1156
  1.6 31.5 %all-to-all-start = ((bf16[12,16,768]{2,1,0:T(8,128)(2,1)}), bf16[12,16,768]{2,1,0:T(8,128)(2,1)S(1)}, u32[]{:S(2)}, u32[]{:S(2)}) async-start(bf16[12,16,768]{2,1,0:T(8,128)(2,1)} %spread.1), calls=%async_computation | async-start | bytes 589824 | tf_op jit(solution)/shard_map/all_to_all | solution.py:385
  19.9 25.5 %copy-start.2 = (s32[768]{0:T(1024)S(1)}, s32[768]{0:T(1024)}, u32[]{:S(2)}) copy-start(s32[768]{0:T(1024)} %param.8) | copy-start | bytes 9220
  33.0 12.4 %collective-permute-start.1 = (bf16[192,768]{1,0:T(8,128)(2,1)S(1)}, bf16[192,768]{1,0:T(8,128)(2,1)S(1)}, u32[]{:S(2)}, u32[]{:S(2)}) collective-permute-start(bf16[192,768]{1,0:T(8,128)(2,1)S(1)} %bitcast.79), channel_id=1, source_target_pairs={{0,1},{1,2},{2,3},{3,0},{4,5},{5,6},{6,7},{7,4},{8,9},{9,10},{10,1... | collective-permute-start | bytes 884744 | tf_op jit(solution)/shard_map/ppermute | solution.py:398
  36.2 12.4 %collective-permute-start = (bf16[192,768]{1,0:T(8,128)(2,1)S(1)}, bf16[192,768]{1,0:T(8,128)(2,1)S(1)}, u32[]{:S(2)}, u32[]{:S(2)}) collective-permute-start(bf16[192,768]{1,0:T(8,128)(2,1)S(1)} %bitcast.80), channel_id=1, source_target_pairs={{0,3},{1,0},{2,1},{3,2},{4,7},{5,4},{6,5},{7,6},{8,11},{9,8},{10,9... | collective-permute-start | bytes 884744 | tf_op jit(solution)/shard_map/ppermute | solution.py:398
  38.9 59.5 %all-to-all-start.1 = ((bf16[48,32,256]{2,1,0:T(8,128)(2,1)}), bf16[48,32,256]{2,1,0:T(8,128)(2,1)S(1)}, u32[]{:S(2)}, u32[]{:S(2)}) async-start(bf16[48,32,256]{2,1,0:T(8,128)(2,1)} %pack.1), calls=%async_computation.1 | async-start | bytes 1572864 | tf_op jit(solution)/shard_map/all_to_all | solution.py:406
  45.2 17.1 %copy-start = (f32[2]{0:T(128)S(1)}, f32[2]{0:T(128)}, u32[]{:S(2)}) copy-start(f32[2]{0:T(128)} %shift_ref.7) | copy-start | bytes 28
  45.5 7.8 %collective-permute-start.2 = (bf16[96,768]{1,0:T(8,128)(2,1)S(1)}, bf16[96,768]{1,0:T(8,128)(2,1)S(1)}, u32[]{:S(2)}, u32[]{:S(2)}) collective-permute-start(bf16[96,768]{1,0:T(8,128)(2,1)S(1)} %slice.12), channel_id=1, source_target_pairs={{0,1},{1,2},{2,3},{3,0},{4,5},{5,6},{6,7},{7,4},{8,9},{9,10},{10,1... | collective-permute-start | bytes 442376 | tf_op jit(solution)/shard_map/ppermute | solution.py:398
  48.6 7.3 %collective-permute-start.3 = (bf16[96,768]{1,0:T(8,128)(2,1)S(1)}, bf16[96,768]{1,0:T(8,128)(2,1)S(1)}, u32[]{:S(2)}, u32[]{:S(2)}) collective-permute-start(bf16[96,768]{1,0:T(8,128)(2,1)S(1)} %slice.13), channel_id=1, source_target_pairs={{0,3},{1,0},{2,1},{3,2},{4,7},{5,4},{6,5},{7,6},{8,11},{9,8},{10,9... | collective-permute-start | bytes 442376 | tf_op jit(solution)/shard_map/ppermute | solution.py:398
  57.8 9.0 %collective-permute-start.4 = (bf16[128,512]{1,0:T(8,128)(2,1)}, bf16[128,512]{1,0:T(8,128)(2,1)}, u32[]{:S(2)}, u32[]{:S(2)}) collective-permute-start(bf16[128,512]{1,0:T(8,128)(2,1)} %get-tuple-element.26), channel_id=1, source_target_pairs={{48,0},{49,1},{50,2},{51,3},{52,4},{53,5},{54,6},{55,7},{56,8},{57... | collective-permute-start | bytes 393224 | tf_op jit(solution)/shard_map/ppermute | solution.py:449
  59.2 7.7 %collective-permute-start.5 = (bf16[128,256]{1,0:T(8,128)(2,1)}, bf16[128,256]{1,0:T(8,128)(2,1)S(1)}, u32[]{:S(2)}, u32[]{:S(2)}) collective-permute-start(bf16[128,256]{1,0:T(8,128)(2,1)} %get-tuple-element.27), channel_id=1, source_target_pairs={{96,0},{97,1},{98,2},{99,3},{100,4},{101,5},{102,6},{103,7},{104,8... | collective-permute-start | bytes 196616 | tf_op jit(solution)/shard_map/ppermute | solution.py:449
  61.5 9.3 %collective-permute-start.6 = (bf16[256,768]{1,0:T(8,128)(2,1)}, bf16[256,768]{1,0:T(8,128)(2,1)S(1)}, u32[]{:S(2)}, u32[]{:S(2)}) collective-permute-start(bf16[256,768]{1,0:T(8,128)(2,1)} %get-tuple-element.30), channel_id=1, source_target_pairs={{0,0},{49,1},{98,2},{147,3},{196,4},{245,5},{294,6},{343,7},{392,8... | collective-permute-start | bytes 1179656 | tf_op jit(solution)/shard_map/ppermute | solution.py:452
  72.7 1.4 %collective-permute-start.7 = (bf16[768,256]{1,0:T(8,128)(2,1)S(1)}, bf16[768,256]{1,0:T(8,128)(2,1)S(1)}, u32[]{:S(2)}, u32[]{:S(2)}) collective-permute-start(bf16[768,256]{1,0:T(8,128)(2,1)S(1)} %get-tuple-element.36.first_ref), channel_id=1, source_target_pairs={{0,288},{1,289},{2,290},{3,291},{4,292},{5,293},{6,294},{7,295},{8... | collective-permute-start | bytes 1179656 | tf_op jit(solution)/shard_map/ppermute | solution.py:515
  73.4 0.7 collective-permute-start.8
  74.4 21.3 %collective-permute-start.10 = (bf16[768,256]{1,0:T(8,128)(2,1)S(1)}, bf16[768,256]{1,0:T(8,128)(2,1)S(1)}, u32[]{:S(2)}, u32[]{:S(2)}) collective-permute-start(bf16[768,256]{1,0:T(8,128)(2,1)S(1)} %pick.1), channel_id=1, source_target_pairs={{0,672},{288,192},{576,480},{1,673},{289,193},{577,481},{2,674},{2... | collective-permute-start | bytes 1179656 | tf_op jit(solution)/shard_map/ppermute | solution.py:515
  75.1 20.6 %collective-permute-start.9 = (bf16[768,256]{1,0:T(8,128)(2,1)S(1)}, bf16[768,256]{1,0:T(8,128)(2,1)}, u32[]{:S(2)}, u32[]{:S(2)}) collective-permute-start(bf16[768,256]{1,0:T(8,128)(2,1)S(1)} %pick.1), channel_id=1, source_target_pairs={{0,96},{288,384},{1,97},{289,385},{2,98},{290,386},{3,99},{291,387... | collective-permute-start | bytes 1179656 | tf_op jit(solution)/shard_map/ppermute | solution.py:515
  76.4 2.0 %collective-permute-start.11 = (bf16[256,256]{1,0:T(8,128)(2,1)}, bf16[256,256]{1,0:T(8,128)(2,1)S(1)}, u32[]{:S(2)}, u32[]{:S(2)}) collective-permute-start(bf16[256,256]{1,0:T(8,128)(2,1)} %get-tuple-element.37), channel_id=1, source_target_pairs={{0,48},{1,49},{2,50},{3,51},{4,52},{5,53},{6,54},{7,55},{8,56},{9,... | collective-permute-start | bytes 393224 | tf_op jit(solution)/shard_map/ppermute | solution.py:533
  77.0 18.6 %collective-permute-start.12 = (bf16[256,256]{1,0:T(8,128)(2,1)}, bf16[256,256]{1,0:T(8,128)(2,1)S(1)}, u32[]{:S(2)}, u32[]{:S(2)}) collective-permute-start(bf16[256,256]{1,0:T(8,128)(2,1)} %get-tuple-element.38), channel_id=1, source_target_pairs={{0,96},{1,97},{2,98},{3,99},{4,100},{5,101},{6,102},{7,103},{8,104... | collective-permute-start | bytes 393224 | tf_op jit(solution)/shard_map/ppermute | solution.py:533
  96.7 3.2 %collective-permute-start.13 = (bf16[768,256]{1,0:T(8,128)(2,1)S(1)}, bf16[768,256]{1,0:T(8,128)(2,1)S(1)}, u32[]{:S(2)}, u32[]{:S(2)}) collective-permute-start(bf16[768,256]{1,0:T(8,128)(2,1)S(1)} %select_select_fusion.w_ref), channel_id=1, source_target_pairs={{0,48},{96,144},{192,240},{288,336},{384,432},{480,528},{576,624},... | collective-permute-start | bytes 1179656 | tf_op jit(solution)/shard_map/ppermute | solution.py:540

commit v7 on v5

--- a/solution.py
+++ b/solution.py
@@ -18,25 +18,13 @@
 BF16 = jnp.bfloat16
 
 
-def split(x):
-    high = x.astype(BF16)
-    return high, (x - high.astype(F32)).astype(BF16)
-
-
 def embed(block):
     real, imag = block[:, :SN], block[:, SN:]
     return jnp.concatenate([block, jnp.concatenate([-imag, real], axis=1)], axis=0)
 
 
-def times(left, right, passes=1):
-    dot = functools.partial(jnp.dot, preferred_element_type=F32)
-    if passes == 1:
-        return dot(left.astype(BF16), embed(right.astype(BF16)))
-    height = left.shape[0]
-    left_high, left_low = split(left)
-    right_high, right_low = split(right)
-    both = dot(jnp.concatenate([left_high, left_low], axis=0), embed(right_high))
-    return both[:height] + (both[height:] + dot(left_high, embed(right_low)))
+def times(left, right):
+    return jnp.dot(left.astype(BF16), embed(right.astype(BF16)), preferred_element_type=F32)
 
 
 def invert_pivot(pivot):
@@ -61,9 +49,9 @@
         axis=1,
     )
     residue = jnp.concatenate([res_real, res_imag], axis=1)
-    power = times(residue, residue, 3)
+    power = times(residue, residue)
     for sweep in range(NSI - 2):
-        both = times(jnp.concatenate([approx, power], axis=0), power, 3 if sweep == 0 else 1)
+        both = times(jnp.concatenate([approx, power], axis=0), power)
         approx, power = approx + both[:SN], both[SN:]
     return approx + times(approx, power)
 
@@ -162,18 +150,18 @@
     return jnp.concatenate([block[:, :SN].T, block[:, SN:].T], axis=1)
 
 
-def stacked(lefts, right, passes=1):
-    product = times(jnp.concatenate(lefts, axis=0), right, passes)
+def stacked(lefts, right):
+    product = times(jnp.concatenate(lefts, axis=0), right)
     return [product[i * SN : (i + 1) * SN] for i in range(len(lefts))]
 
 
 def first_pivot_kernel(shift_ref, own_ref, out_ref):
     a00, a01, a02 = [shifted(shift_ref, own_ref, s, STEPS) for s in range(STEPS)]
     x0 = invert_pivot(a00)
-    f10, f20 = stacked([flip(a01), flip(a02)], x0, 3)
+    f10, f20 = stacked([flip(a01), flip(a02)], x0)
     out_ref[0], out_ref[1], out_ref[2] = x0, f10, f20
-    out_ref[3] = times(f10, a01, 3)
-    out_ref[4], out_ref[5] = stacked([f10, f20], a02, 3)
+    out_ref[3] = times(f10, a01)
+    out_ref[4], out_ref[5] = stacked([f10, f20], a02)
 
 
 def pivot_kernel(shift_ref, which_ref, first_ref, a1_ref, a2_ref, solve_ref, special_ref):
@@ -184,8 +172,8 @@
     a12 = shifted(shift_ref, a1_ref, 1, 2) - first_ref[4]
     a22 = shifted(shift_ref, a2_ref, 0, 1) - first_ref[5]
     x1 = invert_pivot(a11)
-    f21 = times(flip(a12), x1, 3)
-    x2 = invert_pivot(a22 - times(f21, a12, 3))
+    f21 = times(flip(a12), x1)
+    x2 = invert_pivot(a22 - times(f21, a12))
     k01, k12 = -flip(f10), -flip(f21)
     k02 = times(k01, k12) - flip(f20)
     h01 = times(k01, x1)

time: 103 us -> 102 us (level)
  Pallas kernels: 19.1 us -> 18 us
  transfers between devices with their start and end apart: 16 -> 16, of which waited for: 4 -> 4; matrix products, arithmetic and copies ran while one was open for 4% -> 4% of each run, Pallas kernels for 15% -> 14%
where the time goes in v7:
time: 102 us; the launch traced here: 101 us
  starting transfers between devices  45.1 us (44%)
  waiting for transfers between devices  33.3 us (33%)
  Pallas kernels  18 us (18%)
  matrix products  1.67 us (2%)
  other arithmetic  1.5 us (1%)
    ppermute x2, waiting for transfers between devices, body(): lax.ppermute(u[i - 1], both, [(device(0, c), device(i, c)) for c in colum...  16.6 us
    all_to_all x1, starting transfers between devices, body(): lax.all_to_all(copies, 'pcol', 0, 0, axis_index_groups=along_z)  14.8 us
    all_to_all x1, waiting for transfers between devices, body(): lax.all_to_all(copies, 'pcol', 0, 0, axis_index_groups=along_z)  12.4 us
    ppermute x4, starting transfers between devices, shift_x(): lax.ppermute(array, 'pcol', [(c, c - c % N_X + (c % N_X + by) % N_X) for...  11.7 us
    all_to_all x1, starting transfers between devices, body(): main = lax.all_to_all(packed, 'pcol', 0, 0)  6.26 us
    ppermute x4, starting transfers between devices, along_y(): lax.ppermute(array, both, [(device(2 * start, c), device(2 * end, c)) for...  4.79 us
    ppermute x4, waiting for transfers between devices, shift_x(): lax.ppermute(array, 'pcol', [(c, c - c % N_X + (c % N_X + by) % N_X) for...  4.23 us
    ppermute x2, starting transfers between devices, body(): lax.ppermute(tail, both, [(device(t, c), device(0, c)) for c in columns])  3.66 us
  transfers between devices with their start and end apart: 16, of which 4 were waited for; matrix products, arithmetic and copies ran while one was open for 4% of the time, Pallas kernels for 14%

profile of v7, /device:TPU:76, one launch (start us, length us, event | category | flops | bytes accessed | tf_op | source)
XLA Modules:
  0.0 101.1 jit_solution(8563227660427837691)
XLA Ops:
  0.0 1.6 %spread.1 = bf16[12,16,768]{2,1,0:T(8,128)(2,1)} custom-call(bf16[16,12288]{1,0:T(8,128)(2,1)} %ham_ref.3, bf16[16,12288]{1,0:T(8,128)(2,1)} %over_ref.3), custom_call_target="tpu_custom_call" | custom-call | tf_op jit(solution)/shard_map/spread/pallas_call | solution.py:349
  1.6 14.8 %all-to-all-start = ((bf16[12,16,768]{2,1,0:T(8,128)(2,1)}), bf16[12,16,768]{2,1,0:T(8,128)(2,1)S(1)}, u32[]{:S(2)}, u32[]{:S(2)}) async-start(bf16[12,16,768]{2,1,0:T(8,128)(2,1)} %spread.1), calls=%async_computation | async-start | bytes 589824 | tf_op jit(solution)/shard_map/all_to_all | solution.py:363
  16.4 2.1 %pack.1 = bf16[48,32,256]{2,1,0:T(8,128)(2,1)} custom-call(bf16[16,12288]{1,0:T(8,128)(2,1)} %ham_ref.3, bf16[16,12288]{1,0:T(8,128)(2,1)} %over_ref.3), custom_call_target="tpu_custom_call" | custom-call | tf_op jit(solution)/shard_map/pack/pallas_call | solution.py:365
  20.6 12.4 %all-to-all-done = bf16[12,16,768]{2,1,0:T(8,128)(2,1)S(1)} async-done(((bf16[12,16,768]{2,1,0:T(8,128)(2,1)}), bf16[12,16,768]{2,1,0:T(8,128)(2,1)S(1)}, u32[]{:S(2)}, u32[]{:S(2)}) %all-to-all-start) | async-done | bytes 294944 | tf_op jit(solution)/shard_map/all_to_all | solution.py:363
  33.0 3.1 %collective-permute-start.1 = (bf16[192,768]{1,0:T(8,128)(2,1)S(1)}, bf16[192,768]{1,0:T(8,128)(2,1)S(1)}, u32[]{:S(2)}, u32[]{:S(2)}) collective-permute-start(bf16[192,768]{1,0:T(8,128)(2,1)S(1)} %bitcast.78), channel_id=1, source_target_pairs={{0,1},{1,2},{2,3},{3,0},{4,5},{5,6},{6,7},{7,4},{8,9},{9,10},{10,1... | collective-permute-start | bytes 884744 | tf_op jit(solution)/shard_map/ppermute | solution.py:376
  36.2 2.7 %collective-permute-start = (bf16[192,768]{1,0:T(8,128)(2,1)S(1)}, bf16[192,768]{1,0:T(8,128)(2,1)S(1)}, u32[]{:S(2)}, u32[]{:S(2)}) collective-permute-start(bf16[192,768]{1,0:T(8,128)(2,1)S(1)} %bitcast.79), channel_id=1, source_target_pairs={{0,3},{1,0},{2,1},{3,2},{4,7},{5,4},{6,5},{7,6},{8,11},{9,8},{10,9... | collective-permute-start | bytes 884744 | tf_op jit(solution)/shard_map/ppermute | solution.py:376
  39.1 6.3 %all-to-all-start.1 = ((bf16[48,32,256]{2,1,0:T(8,128)(2,1)}), bf16[48,32,256]{2,1,0:T(8,128)(2,1)S(1)}, u32[]{:S(2)}, u32[]{:S(2)}) async-start(bf16[48,32,256]{2,1,0:T(8,128)(2,1)} %pack.1), calls=%async_computation.1 | async-start | bytes 1572864 | tf_op jit(solution)/shard_map/all_to_all | solution.py:384
  45.4 3.1 %collective-permute-start.2 = (bf16[96,768]{1,0:T(8,128)(2,1)S(1)}, bf16[96,768]{1,0:T(8,128)(2,1)S(1)}, u32[]{:S(2)}, u32[]{:S(2)}) collective-permute-start(bf16[96,768]{1,0:T(8,128)(2,1)S(1)} %slice.12), channel_id=1, source_target_pairs={{0,1},{1,2},{2,3},{3,0},{4,5},{5,6},{6,7},{7,4},{8,9},{9,10},{10,1... | collective-permute-start | bytes 442376 | tf_op jit(solution)/shard_map/ppermute | solution.py:376
  48.6 2.8 %collective-permute-start.3 = (bf16[96,768]{1,0:T(8,128)(2,1)S(1)}, bf16[96,768]{1,0:T(8,128)(2,1)S(1)}, u32[]{:S(2)}, u32[]{:S(2)}) collective-permute-start(bf16[96,768]{1,0:T(8,128)(2,1)S(1)} %slice.13), channel_id=1, source_target_pairs={{0,3},{1,0},{2,1},{3,2},{4,7},{5,4},{6,5},{7,6},{8,11},{9,8},{10,9... | collective-permute-start | bytes 442376 | tf_op jit(solution)/shard_map/ppermute | solution.py:376
  51.7 1.8 %collective-permute-done.2.refs_2_ = bf16[96,768]{1,0:T(8,128)(2,1)S(1)} collective-permute-done((bf16[96,768]{1,0:T(8,128)(2,1)S(1)}, bf16[96,768]{1,0:T(8,128)(2,1)S(1)}, u32[]{:S(2)}, u32[]{:S(2)}) %collective-permute-start.2) | collective-permute-done | bytes 147488 | tf_op jit(solution)/shard_map/ppermute | solution.py:376
  53.5 2.4 %collective-permute-done.3.refs_3_ = bf16[96,768]{1,0:T(8,128)(2,1)S(1)} collective-permute-done((bf16[96,768]{1,0:T(8,128)(2,1)S(1)}, bf16[96,768]{1,0:T(8,128)(2,1)S(1)}, u32[]{:S(2)}, u32[]{:S(2)}) %collective-permute-start.3) | collective-permute-done | bytes 147488 | tf_op jit(solution)/shard_map/ppermute | solution.py:376
  55.9 1.9 %early_rows.1 = (bf16[128,768]{1,0:T(8,128)(2,1)S(1)}, bf16[128,512]{1,0:T(8,128)(2,1)}, bf16[128,256]{1,0:T(8,128)(2,1)}, bf16[256,768]{1,0:T(8,128)(2,1)}) custom-call(s32[3]{0:T(128)S(1)} %pad_add_fusion.1.slot_ref, f32[6,3]{1,0:T(8,128)S(1)} %bitcast.82, s32[768,1]{1,0:T(8,128)S(1)} %broadcast_in_dim.26.place_ref, bf16[192,768]{1,0:T(8,128)(2,1)S(1)} %bitcast.80, ...), custom_call_target="tpu_custom_call" | custom-call | tf_op jit(solution)/shard_map/early_rows/pallas_call | solution.py:415
  57.8 1.3 %collective-permute-start.4 = (bf16[128,512]{1,0:T(8,128)(2,1)}, bf16[128,512]{1,0:T(8,128)(2,1)}, u32[]{:S(2)}, u32[]{:S(2)}) collective-permute-start(bf16[128,512]{1,0:T(8,128)(2,1)} %get-tuple-element.26), channel_id=1, source_target_pairs={{48,0},{49,1},{50,2},{51,3},{52,4},{53,5},{54,6},{55,7},{56,8},{57... | collective-permute-start | bytes 393224 | tf_op jit(solution)/shard_map/ppermute | solution.py:427
  59.1 2.3 %collective-permute-start.5 = (bf16[128,256]{1,0:T(8,128)(2,1)}, bf16[128,256]{1,0:T(8,128)(2,1)S(1)}, u32[]{:S(2)}, u32[]{:S(2)}) collective-permute-start(bf16[128,256]{1,0:T(8,128)(2,1)} %get-tuple-element.27), channel_id=1, source_target_pairs={{96,0},{97,1},{98,2},{99,3},{100,4},{101,5},{102,6},{103,7},{104,8... | collective-permute-start | bytes 196616 | tf_op jit(solution)/shard_map/ppermute | solution.py:427
  62.3 1.7 %first_pivot.1.first_ref = f32[6,128,256]{2,1,0:T(8,128)S(1)} custom-call(f32[2]{0:T(128)S(1)} %copy-done, bf16[128,768]{1,0:T(8,128)(2,1)S(1)} %get-tuple-element.28.own_ref), custom_call_target="tpu_custom_call" | custom-call | tf_op jit(solution)/shard_map/first_pivot/pallas_call | solution.py:433
  63.9 2.4 %panel_rows.1.panel_ref = bf16[768,768]{1,0:T(8,128)(2,1)S(1)} custom-call(f32[6,3]{1,0:T(8,128)S(1)} %bitcast.83, s32[768,1]{1,0:T(8,128)S(1)} %broadcast_in_dim.26.place_ref, bf16[192,768]{1,0:T(8,128)(2,1)S(1)} %bitcast.81, bf16[192,768]{1,0:T(8,128)(2,1)S(1)} %collective-permute-done.refs_1_, bf16[96,768]{1,0:T(8,128)(2,1)S(1)} %collective-permute-done.2.refs_2_, ...), custom_call_target="tpu_custom_call" | custom-call | tf_op jit(solution)/shard_map/panel_rows/pallas_call | solution.py:441
  66.3 3.4 %pivots.1 = (bf16[1280,768]{1,0:T(8,128)(2,1)S(1)}, bf16[1280,128]{1,0:T(8,128)(2,1)S(1)}) custom-call(f32[2]{0:T(128)S(1)} %copy-done, s32[4]{0:T(128)S(1)} %pad_add_fusion.which_ref, f32[6,128,256]{2,1,0:T(8,128)S(1)} %first_pivot.1.first_ref, bf16[128,512]{1,0:T(8,128)(2,1)} %collective-permute-done.4.a1_ref, ...), custom_call_target="tpu_custom_call" | custom-call | flops 3000000000 | bytes 1000000 | tf_op jit(solution)/shard_map/pivots/pallas_call | solution.py:452
  71.6 1.4 %collective-permute-start.8 = (bf16[768,256]{1,0:T(8,128)(2,1)S(1)}, bf16[768,256]{1,0:T(8,128)(2,1)}, u32[]{:S(2)}, u32[]{:S(2)}) collective-permute-start(bf16[768,256]{1,0:T(8,128)(2,1)S(1)} %get-tuple-element.36), channel_id=1, source_target_pairs={{0,576},{1,577},{2,578},{3,579},{4,580},{5,581},{6,582},{7,583},{8... | collective-permute-start | bytes 1179656 | tf_op jit(solution)/shard_map/ppermute | solution.py:480
  73.1 1.4 %collective-permute-start.10 = (bf16[768,256]{1,0:T(8,128)(2,1)S(1)}, bf16[768,256]{1,0:T(8,128)(2,1)}, u32[]{:S(2)}, u32[]{:S(2)}) collective-permute-start(bf16[768,256]{1,0:T(8,128)(2,1)S(1)} %select_select_fusion.1), channel_id=1, source_target_pairs={{0,672},{288,192},{576,480},{1,673},{289,193},{577,481},{2,674},{2... | collective-permute-start | bytes 1179656 | tf_op jit(solution)/shard_map/ppermute | solution.py:480
  76.5 1.3 %collective-permute-start.12 = (bf16[256,256]{1,0:T(8,128)(2,1)S(1)}, bf16[256,256]{1,0:T(8,128)(2,1)S(1)}, u32[]{:S(2)}, u32[]{:S(2)}) collective-permute-start(bf16[256,256]{1,0:T(8,128)(2,1)S(1)} %get-tuple-element.38), channel_id=1, source_target_pairs={{0,96},{1,97},{2,98},{3,99},{4,100},{5,101},{6,102},{7,103},{8,104... | collective-permute-start | bytes 393224 | tf_op jit(solution)/shard_map/ppermute | solution.py:498
  77.8 16.6 %collective-permute-done.12.u2_ref = bf16[256,256]{1,0:T(8,128)(2,1)S(1)} collective-permute-done((bf16[256,256]{1,0:T(8,128)(2,1)S(1)}, bf16[256,256]{1,0:T(8,128)(2,1)S(1)}, u32[]{:S(2)}, u32[]{:S(2)}) %collective-permute-start.12) | collective-permute-done | bytes 131104 | tf_op jit(solution)/shard_map/ppermute | solution.py:498
  95.5 1.3 %collective-permute-start.13 = (bf16[768,256]{1,0:T(8,128)(2,1)S(1)}, bf16[768,256]{1,0:T(8,128)(2,1)S(1)}, u32[]{:S(2)}, u32[]{:S(2)}) collective-permute-start(bf16[768,256]{1,0:T(8,128)(2,1)S(1)} %select_select_fusion.w_ref), channel_id=1, source_target_pairs={{0,48},{96,144},{192,240},{288,336},{384,432},{480,528},{576,624},... | collective-permute-start | bytes 1179656 | tf_op jit(solution)/shard_map/ppermute | solution.py:505
  97.2 1.6 %assemble.1.base_ref = f32[2,768,256]{2,1,0:T(8,128)S(1)} custom-call(f32[2]{0:T(128)S(1)} %copy-done, s32[4]{0:T(128)S(1)} %pad_add_fusion.which_ref, f32[6,2]{1,0:T(8,128)S(1)} %fusion.61.mask_ref, s32[768,1]{1,0:T(8,128)S(1)} %broadcast_in_dim.25.place_ref, bf16[48,32,256]{2,1,0:T(8,128)(2,1)S(1)} %all-to-all-done.1.main_ref), custom_call_target="tpu_custom_call" | custom-call | tf_op jit(solution)/shard_map/assemble/pallas_call | solution.py:489
  98.8 2.3 %update.1 = f32[2,768,256]{2,1,0:T(8,128)} custom-call(f32[2]{0:T(128)S(1)} %copy-done, s32[4]{0:T(128)S(1)} %pad_add_fusion.which_ref, f32[2,768,256]{2,1,0:T(8,128)S(1)} %assemble.1.base_ref, bf16[768,768]{1,0:T(8,128)(2,1)S(1)} %panel_rows.1.panel_ref, bf16[768,256]{1,0:T(8,128)(2,1)S(1)} %select_select_fusion.w_ref, ...), custom_call_target="tpu_custom_call" | custom-call | tf_op jit(solution)/shard_map/update/pallas_call | solution.py:510
  (56 shorter events, 8.8 us)
Async XLA Ops:
  0.0 18.4 %copy-start.1 = (s32[96]{0:T(128)S(1)}, s32[96]{0:T(128)}, u32[]{:S(2)}) copy-start(s32[96]{0:T(128)} %param.9) | copy-start | bytes 1156
  1.6 31.5 %all-to-all-start = ((bf16[12,16,768]{2,1,0:T(8,128)(2,1)}), bf16[12,16,768]{2,1,0:T(8,128)(2,1)S(1)}, u32[]{:S(2)}, u32[]{:S(2)}) async-start(bf16[12,16,768]{2,1,0:T(8,128)(2,1)} %spread.1), calls=%async_computation | async-start | bytes 589824 | tf_op jit(solution)/shard_map/all_to_all | solution.py:363
  16.4 4.2 %copy-start.2 = (s32[768]{0:T(1024)S(1)}, s32[768]{0:T(1024)}, u32[]{:S(2)}) copy-start(s32[768]{0:T(1024)} %param.8) | copy-start | bytes 9220
  33.0 12.4 %collective-permute-start.1 = (bf16[192,768]{1,0:T(8,128)(2,1)S(1)}, bf16[192,768]{1,0:T(8,128)(2,1)S(1)}, u32[]{:S(2)}, u32[]{:S(2)}) collective-permute-start(bf16[192,768]{1,0:T(8,128)(2,1)S(1)} %bitcast.78), channel_id=1, source_target_pairs={{0,1},{1,2},{2,3},{3,0},{4,5},{5,6},{6,7},{7,4},{8,9},{9,10},{10,1... | collective-permute-start | bytes 884744 | tf_op jit(solution)/shard_map/ppermute | solution.py:376
  36.2 12.4 %collective-permute-start = (bf16[192,768]{1,0:T(8,128)(2,1)S(1)}, bf16[192,768]{1,0:T(8,128)(2,1)S(1)}, u32[]{:S(2)}, u32[]{:S(2)}) collective-permute-start(bf16[192,768]{1,0:T(8,128)(2,1)S(1)} %bitcast.79), channel_id=1, source_target_pairs={{0,3},{1,0},{2,1},{3,2},{4,7},{5,4},{6,5},{7,6},{8,11},{9,8},{10,9... | collective-permute-start | bytes 884744 | tf_op jit(solution)/shard_map/ppermute | solution.py:376
  39.1 58.1 %all-to-all-start.1 = ((bf16[48,32,256]{2,1,0:T(8,128)(2,1)}), bf16[48,32,256]{2,1,0:T(8,128)(2,1)S(1)}, u32[]{:S(2)}, u32[]{:S(2)}) async-start(bf16[48,32,256]{2,1,0:T(8,128)(2,1)} %pack.1), calls=%async_computation.1 | async-start | bytes 1572864 | tf_op jit(solution)/shard_map/all_to_all | solution.py:384
  45.4 16.9 %copy-start = (f32[2]{0:T(128)S(1)}, f32[2]{0:T(128)}, u32[]{:S(2)}) copy-start(f32[2]{0:T(128)} %shift_ref.7) | copy-start | bytes 28
  45.4 8.0 %collective-permute-start.2 = (bf16[96,768]{1,0:T(8,128)(2,1)S(1)}, bf16[96,768]{1,0:T(8,128)(2,1)S(1)}, u32[]{:S(2)}, u32[]{:S(2)}) collective-permute-start(bf16[96,768]{1,0:T(8,128)(2,1)S(1)} %slice.12), channel_id=1, source_target_pairs={{0,1},{1,2},{2,3},{3,0},{4,5},{5,6},{6,7},{7,4},{8,9},{9,10},{10,1... | collective-permute-start | bytes 442376 | tf_op jit(solution)/shard_map/ppermute | solution.py:376
  48.6 7.3 %collective-permute-start.3 = (bf16[96,768]{1,0:T(8,128)(2,1)S(1)}, bf16[96,768]{1,0:T(8,128)(2,1)S(1)}, u32[]{:S(2)}, u32[]{:S(2)}) collective-permute-start(bf16[96,768]{1,0:T(8,128)(2,1)S(1)} %slice.13), channel_id=1, source_target_pairs={{0,3},{1,0},{2,1},{3,2},{4,7},{5,4},{6,5},{7,6},{8,11},{9,8},{10,9... | collective-permute-start | bytes 442376 | tf_op jit(solution)/shard_map/ppermute | solution.py:376
  57.8 8.5 %collective-permute-start.4 = (bf16[128,512]{1,0:T(8,128)(2,1)}, bf16[128,512]{1,0:T(8,128)(2,1)}, u32[]{:S(2)}, u32[]{:S(2)}) collective-permute-start(bf16[128,512]{1,0:T(8,128)(2,1)} %get-tuple-element.26), channel_id=1, source_target_pairs={{48,0},{49,1},{50,2},{51,3},{52,4},{53,5},{54,6},{55,7},{56,8},{57... | collective-permute-start | bytes 393224 | tf_op jit(solution)/shard_map/ppermute | solution.py:427
  59.1 7.2 %collective-permute-start.5 = (bf16[128,256]{1,0:T(8,128)(2,1)}, bf16[128,256]{1,0:T(8,128)(2,1)S(1)}, u32[]{:S(2)}, u32[]{:S(2)}) collective-permute-start(bf16[128,256]{1,0:T(8,128)(2,1)} %get-tuple-element.27), channel_id=1, source_target_pairs={{96,0},{97,1},{98,2},{99,3},{100,4},{101,5},{102,6},{103,7},{104,8... | collective-permute-start | bytes 196616 | tf_op jit(solution)/shard_map/ppermute | solution.py:427
  61.5 8.2 %collective-permute-start.6 = (bf16[256,768]{1,0:T(8,128)(2,1)}, bf16[256,768]{1,0:T(8,128)(2,1)S(1)}, u32[]{:S(2)}, u32[]{:S(2)}) collective-permute-start(bf16[256,768]{1,0:T(8,128)(2,1)} %get-tuple-element.30), channel_id=1, source_target_pairs={{0,0},{49,1},{98,2},{147,3},{196,4},{245,5},{294,6},{343,7},{392,8... | collective-permute-start | bytes 1179656 | tf_op jit(solution)/shard_map/ppermute | solution.py:430
  71.0 2.1 %collective-permute-start.7 = (bf16[768,256]{1,0:T(8,128)(2,1)S(1)}, bf16[768,256]{1,0:T(8,128)(2,1)S(1)}, u32[]{:S(2)}, u32[]{:S(2)}) collective-permute-start(bf16[768,256]{1,0:T(8,128)(2,1)S(1)} %get-tuple-element.36), channel_id=1, source_target_pairs={{0,288},{1,289},{2,290},{3,291},{4,292},{5,293},{6,294},{7,295},{8... | collective-permute-start | bytes 1179656 | tf_op jit(solution)/shard_map/ppermute | solution.py:480
  71.6 1.4 %collective-permute-start.8 = (bf16[768,256]{1,0:T(8,128)(2,1)S(1)}, bf16[768,256]{1,0:T(8,128)(2,1)}, u32[]{:S(2)}, u32[]{:S(2)}) collective-permute-start(bf16[768,256]{1,0:T(8,128)(2,1)S(1)} %get-tuple-element.36), channel_id=1, source_target_pairs={{0,576},{1,577},{2,578},{3,579},{4,580},{5,581},{6,582},{7,583},{8... | collective-permute-start | bytes 1179656 | tf_op jit(solution)/shard_map/ppermute | solution.py:480
  73.1 21.3 %collective-permute-start.10 = (bf16[768,256]{1,0:T(8,128)(2,1)S(1)}, bf16[768,256]{1,0:T(8,128)(2,1)}, u32[]{:S(2)}, u32[]{:S(2)}) collective-permute-start(bf16[768,256]{1,0:T(8,128)(2,1)S(1)} %select_select_fusion.1), channel_id=1, source_target_pairs={{0,672},{288,192},{576,480},{1,673},{289,193},{577,481},{2,674},{2... | collective-permute-start | bytes 1179656 | tf_op jit(solution)/shard_map/ppermute | solution.py:480
  74.5 19.9 %collective-permute-start.9 = (bf16[768,256]{1,0:T(8,128)(2,1)S(1)}, bf16[768,256]{1,0:T(8,128)(2,1)}, u32[]{:S(2)}, u32[]{:S(2)}) collective-permute-start(bf16[768,256]{1,0:T(8,128)(2,1)S(1)} %select_select_fusion.1), channel_id=1, source_target_pairs={{0,96},{288,384},{1,97},{289,385},{2,98},{290,386},{3,99},{291,387... | collective-permute-start | bytes 1179656 | tf_op jit(solution)/shard_map/ppermute | solution.py:480
  75.8 2.0 %collective-permute-start.11 = (bf16[256,256]{1,0:T(8,128)(2,1)S(1)}, bf16[256,256]{1,0:T(8,128)(2,1)S(1)}, u32[]{:S(2)}, u32[]{:S(2)}) collective-permute-start(bf16[256,256]{1,0:T(8,128)(2,1)S(1)} %get-tuple-element.37), channel_id=1, source_target_pairs={{0,48},{1,49},{2,50},{3,51},{4,52},{5,53},{6,54},{7,55},{8,56},{9,... | collective-permute-start | bytes 393224 | tf_op jit(solution)/shard_map/ppermute | solution.py:498
  76.5 17.9 %collective-permute-start.12 = (bf16[256,256]{1,0:T(8,128)(2,1)S(1)}, bf16[256,256]{1,0:T(8,128)(2,1)S(1)}, u32[]{:S(2)}, u32[]{:S(2)}) collective-permute-start(bf16[256,256]{1,0:T(8,128)(2,1)S(1)} %get-tuple-element.38), channel_id=1, source_target_pairs={{0,96},{1,97},{2,98},{3,99},{4,100},{5,101},{6,102},{7,103},{8,104... | collective-permute-start | bytes 393224 | tf_op jit(solution)/shard_map/ppermute | solution.py:498
  95.5 3.3 %collective-permute-start.13 = (bf16[768,256]{1,0:T(8,128)(2,1)S(1)}, bf16[768,256]{1,0:T(8,128)(2,1)S(1)}, u32[]{:S(2)}, u32[]{:S(2)}) collective-permute-start(bf16[768,256]{1,0:T(8,128)(2,1)S(1)} %select_select_fusion.w_ref), channel_id=1, source_target_pairs={{0,48},{96,144},{192,240},{288,336},{384,432},{480,528},{576,624},... | collective-permute-start | bytes 1179656 | tf_op jit(solution)/shard_map/ppermute | solution.py:505
